TPU v7x, 768 devices: a whole 4x8x12 slice. The times are simulated.
768 devices in a mesh: seq: 48 (over z, x), tp: 16 (over y, core).
Axes of the slice: x: 4, y: 8, z: 12, core: 2. Of those that a mesh axis runs over, the one named last changes fastest.
Arguments:
- teacher_hidden: bfloat16 [6144, 4096], P('seq', 'tp'), may hold values from -6 to 6
- proj_weight: bfloat16 [4096, 3584], P('tp'), may hold values from -0.09375 to 0.09375
- student_in: bfloat16 [7680, 3584], P('seq'), may hold values from -6 to 6
- norm_gain: float32 [3584], replicated, may hold values from 0.25 to 1.75
- w_query: bfloat16 [3584, 4096], P(None, 'tp')
- w_keyval: bfloat16 [3584, 4096], P(None, 'tp')
- w_out: bfloat16 [4096, 3584], P('tp'), may hold values from -0.09375 to 0.09375
- row_offsets: int32 [48], P('seq'), may hold values from 0 to 5984, as said below
- row_counts: int32 [48], P('seq'), may hold values from 96 to 160, as said below
- doc_start: int32 [7680], P('seq'), may hold values from 0 to 159, as said below
Outputs:
- student_out: bfloat16 [7680, 3584], P('seq')
- grad_in: bfloat16 [7680, 3584], P(('seq', 'tp'))
Inputs may be any that keep to these rules, and one draw needn't show every extreme that they name: Block s holds the tokens row_offsets[s] to row_offsets[s] + row_counts[s] - 1 in its first slots; row_offsets[0] = 0, for s >= 1 row_offsets[s] lies between s * 128 - 128 // 4 and s * 128 - 1, and row_offsets[s] + row_counts[s] = row_offsets[s + 1], the last block ending at 6144. `row_counts`: see row_offsets; some block holds 160 tokens and some 128 - 128 // 4. Within a block doc_start never falls, doc_start[p] <= p, documents lie whole in one block, and the slots from row_counts onward start a new document at row_counts.
All inputs are finite; a program needn't handle non-finite values.
Results may differ from a plain program's by a relative error of at most 0.028.
The roundings to bfloat16 on the way count: a program that leaves them out, or rounds other values in their place, can miss the bound.
Values may be sent and summed in bfloat16 or wider, within the bound.
No kernel may reach another device: no remote copies, remote signals or barrier semaphores. Data moves between devices by JAX's collectives and lax.ppermute only.
A program may use at most 64 MiB of HBM per device.

v0:
```python
import math

import jax
import jax.numpy as jnp
from jax import lax
from jax.sharding import PartitionSpec as P

HD = 128
QPK = 2


epsilon = 1e-06


def from_behind(block, axis, distance):
    devices = range(lax.axis_size(axis))
    route = [(i - distance, i) for i in devices if i - distance in devices]
    return lax.ppermute(block, axis, route)


def body(
    teacher_hidden,
    proj_weight,
    student_in,
    norm_gain,
    w_query,
    w_keyval,
    w_out,
    row_offsets,
    row_counts,
    doc_start,
):
    scale = 1.0 / math.sqrt(HD)
    tokens_here = teacher_hidden.shape[0]
    quarter = tokens_here // 4
    slots_here = student_in.shape[0]
    width = student_in.shape[1]
    start = row_offsets[0] - lax.axis_index("seq") * tokens_here + quarter
    count = row_counts[0]
    xf = student_in.astype(jnp.float32)
    inv = lax.rsqrt(jnp.mean(xf * xf, axis=1, keepdims=True) + epsilon)
    normed = (xf * inv * norm_gain).astype(jnp.bfloat16)
    query = (
        jnp.dot(normed, w_query, preferred_element_type=jnp.float32)
        .astype(jnp.bfloat16)
        .reshape(slots_here, QPK, HD)
    )
    keyval = (
        jnp.dot(normed, w_keyval, preferred_element_type=jnp.float32)
        .astype(jnp.bfloat16)
        .reshape(slots_here, 2, HD)
    )
    keys = keyval[:, 0, :]
    values = keyval[:, 1, :]
    slots = jnp.arange(slots_here, dtype=jnp.int32)
    allowed = (slots[None, :] >= doc_start[:, None]) & (slots[None, :] <= slots[:, None])
    scores = jnp.einsum("peh,kh->epk", query, keys, preferred_element_type=jnp.float32) * scale
    scores = jnp.where(allowed[None], scores, -jnp.inf)
    top = jnp.max(scores, axis=-1, keepdims=True)
    expo = jnp.exp(scores - top)
    probs = expo / jnp.sum(expo, axis=-1, keepdims=True)
    probs_b = probs.astype(jnp.bfloat16)
    attn = jnp.einsum("epk,kh->peh", probs_b, values, preferred_element_type=jnp.float32).astype(
        jnp.bfloat16
    )
    attn = attn.reshape(slots_here, QPK * HD)
    branch_part = jnp.dot(attn, w_out, preferred_element_type=jnp.float32).astype(jnp.bfloat16)
    blank = jnp.zeros((quarter, width), jnp.bfloat16)
    projected = jnp.dot(teacher_hidden, proj_weight, preferred_element_type=jnp.float32).astype(
        jnp.bfloat16
    )
    target_rows = lax.psum(projected, "tp").astype(jnp.float32).astype(jnp.bfloat16)
    earlier = from_behind(target_rows[tokens_here - quarter :], "seq", 1)
    window = jnp.concatenate([earlier, target_rows, blank], axis=0)
    goal = lax.dynamic_slice_in_dim(window, start, slots_here, 0)
    branch = lax.psum(branch_part, "tp").astype(jnp.float32)
    student_out = (xf + branch).astype(jnp.bfloat16)
    yf = student_out.astype(jnp.float32)
    tf = goal.astype(jnp.float32)
    live = (slots < count).astype(jnp.float32)[:, None]
    asum = jnp.sum(yf * yf, axis=1, keepdims=True) + epsilon
    bsum = jnp.sum(tf * tf, axis=1, keepdims=True) + epsilon
    both = lax.rsqrt(asum * bsum)
    cosv = jnp.sum(yf * tf, axis=1, keepdims=True) * both
    dy = -math.sqrt(width) * live * (tf * both - cosv * yf / asum)
    dy_b = dy.astype(jnp.bfloat16)
    d_attn = lax.dot_general(
        dy_b, w_out, (((1,), (1,)), ((), ())), preferred_element_type=jnp.float32
    ).astype(jnp.bfloat16)
    d_out = d_attn.reshape(slots_here, QPK, HD)
    d_values = jnp.einsum("epk,peh->kh", probs_b, d_out, preferred_element_type=jnp.float32).astype(
        jnp.bfloat16
    )
    dprob = jnp.einsum("peh,kh->epk", d_out, values, preferred_element_type=jnp.float32)
    dscore = probs * (dprob - jnp.sum(dprob * probs, axis=-1, keepdims=True)) * scale
    dscore_b = dscore.astype(jnp.bfloat16)
    d_query = jnp.einsum("epk,kh->peh", dscore_b, keys, preferred_element_type=jnp.float32).astype(
        jnp.bfloat16
    )
    d_query = d_query.reshape(slots_here, QPK * HD)
    d_keys = jnp.einsum("epk,peh->kh", dscore_b, query, preferred_element_type=jnp.float32).astype(
        jnp.bfloat16
    )
    d_keyval = jnp.stack([d_keys, d_values], axis=1).reshape(slots_here, 2 * HD)
    own_rows = slots_here // lax.axis_size("tp")
    total = lax.dot_general(
        d_query, w_query, (((1,), (1,)), ((), ())), preferred_element_type=jnp.float32
    )
    d_normed = lax.psum_scatter(
        (
            total
            + lax.dot_general(
                d_keyval, w_keyval, (((1,), (1,)), ((), ())), preferred_element_type=jnp.float32
            )
        ).astype(jnp.bfloat16),
        "tp",
        scatter_dimension=0,
        tiled=True,
    ).astype(jnp.float32)
    first_row = lax.axis_index("tp") * own_rows
    x_own = lax.dynamic_slice_in_dim(xf, first_row, own_rows, 0)
    inv_own = lax.dynamic_slice_in_dim(inv, first_row, own_rows, 0)
    dy_own = lax.dynamic_slice_in_dim(dy, first_row, own_rows, 0)
    upper = d_normed * norm_gain
    dx = inv_own * upper - x_own * inv_own * inv_own * inv_own * jnp.mean(
        upper * x_own, axis=1, keepdims=True
    )
    grad_in = (dy_own + dx).astype(jnp.bfloat16)
    return (student_out, grad_in)


def solution(mesh):
    in_specs = (
        P("seq", "tp"),
        P("tp", None),
        P("seq", None),
        P(),
        P(None, "tp"),
        P(None, "tp"),
        P("tp", None),
        P("seq"),
        P("seq"),
        P("seq"),
    )
    out_specs = (P("seq", None), P(("seq", "tp"), None))
    return jax.shard_map(body, mesh=mesh, in_specs=in_specs, out_specs=out_specs, check_vma=False)
```

profile of v0, /device:TPU:1, one launch (start us, length us, event | category | flops | bytes accessed | tf_op | source)
XLA Modules:
  0.0 311.0 jit_solution(12493140656098159648)
XLA Ops:
  7.2 1.7 multiply_reduce_fusion
  8.9 0.7 fusion.40
  9.7 2.5 fusion.26
  12.2 0.2 copy-done.4
  12.4 0.5 convolution_convert_fusion.3
  13.0 0.1 fusion.71
  13.1 0.2 copy-done.8
  13.3 2.9 convolution_convert_fusion.1
  16.2 1.0 fusion.72
  17.2 1.2 fusion.24
  18.4 1.5 convolution_convert_fusion
  20.0 133.7 %all-reduce.7.cloned.1.call-done = (bf16[160,3584]{1,0:T(8,128)(2,1)}, bf16[128,3584]{1,0:T(8,128)(2,1)}) async-done(((bf16[160,3584]{1,0:T(8,128)(2,1)}, bf16[128,3584]{1,0:T(8,128)(2,1)}), (bf16[160,3584]{1,0:T(8,128)(2,1)}, bf16[128,3584]{1,0:T(8,128)(2,1)})) %all-reduce.7.cloned.1.call-update) | async-done | bytes 2064400 | tf_op jit(solution)/shard_map/psum | solution.py:76
  153.7 1.0 slice.14
  154.6 3.1 collective-permute-start
  159.1 0.1 pad_dynamic-slice_fusion.2
  159.2 3.1 %collective-permute-done = bf16[32,3584]{1,0:T(8,128)(2,1)S(1)} collective-permute-done((bf16[32,3584]{1,0:T(8,128)(2,1)S(1)}, bf16[32,3584]{1,0:T(8,128)(2,1)S(1)}, u32[]{:S(2)}, u32[]{:S(2)}) %collective-permute-start) | collective-permute-done | bytes 229408 | tf_op jit(solution)/shard_map/ppermute | solution.py:18
  162.3 2.9 fusion.3
  165.2 0.8 fusion.5
  166.0 0.2 copy-done.3
  166.2 0.8 fusion.27
  166.9 0.6 copy-done.2
  167.6 0.8 fusion.32
  168.4 0.2 convolution_bitcast_fusion
  168.6 2.0 fusion.33
  170.6 1.4 fusion.25
  172.0 2.4 fusion.43
  174.4 1.8 fusion.2
  176.3 1.6 convert_element_type.73
  177.9 1.3 dynamic-slice.4
  179.8 121.2 %all-reduce.5.cloned.1.call-done = bf16[160,3584]{1,0:T(8,128)(2,1)} async-done(((bf16[160,3584]{1,0:T(8,128)(2,1)}), bf16[160,3584]{1,0:T(8,128)(2,1)}) %all-reduce.5.cloned.1.call-update) | async-done | bytes 1146896
  301.1 1.2 multiply_reduce_fusion.2
  302.3 1.9 add_convert_fusion.1
  (35 shorter events, 0.3 us)
Async XLA Ops:
  7.2 11.3 %copy-start = (bf16[256,3584]{1,0:T(8,128)(2,1)S(1)}, bf16[256,3584]{1,0:T(8,128)(2,1)}, u32[]{:S(2)}) copy-start(bf16[256,3584]{1,0:T(8,128)(2,1)} %param.16) | copy-start | bytes 5505028
  7.2 146.5 %all-reduce.7.cloned.1.call-start = ((), (), s32[]{:S(2)}) async-start(), calls=%async_computation.1 | async-start | bytes 4128768 | tf_op jit(solution)/shard_map/psum | solution.py:76
  9.7 2.6 copy-start.1
  9.7 2.8 copy-start.4
  9.7 2.7 copy-start.9
  12.4 3.8 %copy-start.13 = (bf16[20,2,8,128]{3,2,1,0:T(8,128)(2,1)}, bf16[20,2,8,128]{3,2,1,0:T(8,128)(2,1)S(1)}, u32[]{:S(2)}) copy-start(bf16[20,2,8,128]{3,2,1,0:T(8,128)(2,1)S(1)} %fusion.26) | copy-start | bytes 245764
  12.4 0.9 copy-start.8
  13.3 5.1 %copy-start.6 = (bf16[160,1,128]{2,1,0:T(2,128)(2,1)}, bf16[160,1,128]{2,1,0:T(2,128)(2,1)S(1)}, u32[]{:S(2)}) copy-start(bf16[160,1,128]{2,1,0:T(2,128)(2,1)S(1)} %get-tuple-element.11) | copy-start | bytes 122884
  19.9 281.1 %all-reduce.5.cloned.1.call-start = ((), (), s32[]{:S(2)}) async-start(), calls=%async_computation | async-start | bytes 2293760
  154.6 7.6 %collective-permute-start = (bf16[32,3584]{1,0:T(8,128)(2,1)S(1)}, bf16[32,3584]{1,0:T(8,128)(2,1)S(1)}, u32[]{:S(2)}, u32[]{:S(2)}) collective-permute-start(bf16[32,3584]{1,0:T(8,128)(2,1)S(1)} %slice.14), channel_id=1, source_target_pairs={{0,16},{16,32},{32,48},{48,64},{64,80},{80,96},{96,112},{112,128},... | collective-permute-start | bytes 688136 | tf_op jit(solution)/shard_map/ppermute | solution.py:18
  165.2 1.0 copy-start.3
  166.2 1.4 copy-start.2
  166.2 1.4 copy-start.12
  167.6 3.0 copy-start.7
  172.0 2.4 copy-start.5
  172.0 2.4 copy-start.10
  172.0 2.4 copy-start.11
Sparse Core Ops, SparseCore 0:
  20.1 133.5 all-reduce.6
  176.4 124.6 all-reduce.4
where the time goes:
time: 312 us; the launch traced here: 311 us
  waiting for transfers between devices  258 us (83%)
  matrix products  19 us (6%)
  between operations  16.2 us (5%)
  other arithmetic  10.8 us (3%)
  local copies, waits for them, and re-layouts  3.78 us (1%)
  starting transfers between devices  3.19 us (1%)
    psum x1, waiting for transfers between devices, body(): branch = lax.psum(branch_part, 'tp').astype(jnp.float32)  134 us
    unnamed x3, waiting for transfers between devices  121 us
  transfers between devices with their start and end apart: 3, of which 3 were waited for; matrix products, arithmetic and copies ran while one was open for 1% of the time, Pallas kernels for 0%

commit v1 on v0

--- a/solution.py
+++ b/solution.py
@@ -3,10 +3,12 @@
 import jax
 import jax.numpy as jnp
 from jax import lax
+from jax.sharding import Mesh
 from jax.sharding import PartitionSpec as P
 
 HD = 128
 QPK = 2
+PAIR = [(0, 1), (1, 0)]
 
 
 epsilon = 1e-06
@@ -16,6 +18,34 @@
     devices = range(lax.axis_size(axis))
     route = [(i - distance, i) for i in devices if i - distance in devices]
     return lax.ppermute(block, axis, route)
+
+
+def rows_of(array, first, count):
+    return lax.dynamic_slice_in_dim(array, first, count, 0)
+
+
+def sum_blocks(part, core, cols):
+    half = part.shape[0] // 2
+    width = part.shape[1]
+    mine = rows_of(part, core * half, half).astype(jnp.float32)
+    other = lax.ppermute(rows_of(part, (1 - core) * half, half), "core", PAIR)
+    chip = (mine + other.astype(jnp.float32)).astype(jnp.bfloat16)
+    bands = 8 // cols
+    blocks = chip.reshape(bands, half // bands, cols, width // cols).transpose(0, 2, 1, 3)
+    blocks = blocks.reshape(8, half // bands, width // cols)
+    got = lax.all_to_all(blocks, "y", 0, 0)
+    return jnp.sum(got.astype(jnp.float32), axis=0)
+
+
+def gather_blocks(block, core, cols):
+    bands = 8 // cols
+    high, wide = block.shape
+    got = lax.all_to_all(jnp.broadcast_to(block[None], (8, high, wide)), "y", 0, 0)
+    half = got.reshape(bands, cols, high, wide).transpose(0, 2, 1, 3).reshape(bands * high, cols * wide)
+    other = lax.ppermute(half, "core", PAIR)
+    first = jnp.where(core == 0, half, other)
+    second = jnp.where(core == 0, other, half)
+    return jnp.concatenate([first, second], axis=0)
 
 
 def body(
@@ -35,8 +65,20 @@
     quarter = tokens_here // 4
     slots_here = student_in.shape[0]
     width = student_in.shape[1]
+    cols = 4
+    core = lax.axis_index("core")
+    ypos = lax.axis_index("y")
     start = row_offsets[0] - lax.axis_index("seq") * tokens_here + quarter
     count = row_counts[0]
+    earlier = from_behind(teacher_hidden[tokens_here - quarter :], "seq", 1)
+    blank = jnp.zeros((quarter, teacher_hidden.shape[1]), jnp.bfloat16)
+    window = jnp.concatenate([earlier, teacher_hidden, blank], axis=0)
+    window = lax.dynamic_slice_in_dim(window, start, slots_here, 0)
+    goal_part = jnp.dot(window, proj_weight, preferred_element_type=jnp.float32).astype(
+        jnp.bfloat16
+    )
+    goal_own = sum_blocks(goal_part, core, cols).astype(jnp.bfloat16)
+    goal = gather_blocks(goal_own, core, cols)
     xf = student_in.astype(jnp.float32)
     inv = lax.rsqrt(jnp.mean(xf * xf, axis=1, keepdims=True) + epsilon)
     normed = (xf * inv * norm_gain).astype(jnp.bfloat16)
@@ -65,16 +107,14 @@
     )
     attn = attn.reshape(slots_here, QPK * HD)
     branch_part = jnp.dot(attn, w_out, preferred_element_type=jnp.float32).astype(jnp.bfloat16)
-    blank = jnp.zeros((quarter, width), jnp.bfloat16)
-    projected = jnp.dot(teacher_hidden, proj_weight, preferred_element_type=jnp.float32).astype(
-        jnp.bfloat16
+    high = slots_here // (2 * (8 // cols))
+    x_block = lax.dynamic_slice(
+        student_in,
+        (core * (slots_here // 2) + (ypos // cols) * high, (ypos % cols) * (width // cols)),
+        (high, width // cols),
     )
-    target_rows = lax.psum(projected, "tp").astype(jnp.float32).astype(jnp.bfloat16)
-    earlier = from_behind(target_rows[tokens_here - quarter :], "seq", 1)
-    window = jnp.concatenate([earlier, target_rows, blank], axis=0)
-    goal = lax.dynamic_slice_in_dim(window, start, slots_here, 0)
-    branch = lax.psum(branch_part, "tp").astype(jnp.float32)
-    student_out = (xf + branch).astype(jnp.bfloat16)
+    y_own = (x_block.astype(jnp.float32) + sum_blocks(branch_part, core, cols)).astype(jnp.bfloat16)
+    student_out = gather_blocks(y_own, core, cols)
     yf = student_out.astype(jnp.float32)
     tf = goal.astype(jnp.float32)
     live = (slots < count).astype(jnp.float32)[:, None]
@@ -102,22 +142,27 @@
         jnp.bfloat16
     )
     d_keyval = jnp.stack([d_keys, d_values], axis=1).reshape(slots_here, 2 * HD)
-    own_rows = slots_here // lax.axis_size("tp")
     total = lax.dot_general(
         d_query, w_query, (((1,), (1,)), ((), ())), preferred_element_type=jnp.float32
     )
-    d_normed = lax.psum_scatter(
+    own_rows = slots_here // 16
+    part = (
         (
             total
             + lax.dot_general(
                 d_keyval, w_keyval, (((1,), (1,)), ((), ())), preferred_element_type=jnp.float32
             )
-        ).astype(jnp.bfloat16),
-        "tp",
-        scatter_dimension=0,
-        tiled=True,
+        )
+        .astype(jnp.bfloat16)
+        .reshape(8, 2, own_rows * width // HD, HD)
+    )
+    mine = lax.dynamic_index_in_dim(part, core, 1, keepdims=False).astype(jnp.float32)
+    other = lax.ppermute(
+        lax.dynamic_index_in_dim(part, 1 - core, 1, keepdims=False), "core", PAIR
     ).astype(jnp.float32)
-    first_row = lax.axis_index("tp") * own_rows
+    got = lax.all_to_all((mine + other).astype(jnp.bfloat16), "y", 0, 0)
+    d_normed = jnp.sum(got.astype(jnp.float32), axis=0).reshape(own_rows, width)
+    first_row = (ypos * 2 + core) * own_rows
     x_own = lax.dynamic_slice_in_dim(xf, first_row, own_rows, 0)
     inv_own = lax.dynamic_slice_in_dim(inv, first_row, own_rows, 0)
     dy_own = lax.dynamic_slice_in_dim(dy, first_row, own_rows, 0)
@@ -130,17 +175,20 @@
 
 
 def solution(mesh):
+    seqs, tps = mesh.devices.shape
+    split = Mesh(mesh.devices.reshape(seqs, tps // 2, 2), ("seq", "y", "core"))
+    tp = ("y", "core")
     in_specs = (
-        P("seq", "tp"),
-        P("tp", None),
+        P("seq", tp),
+        P(tp, None),
         P("seq", None),
         P(),
-        P(None, "tp"),
-        P(None, "tp"),
-        P("tp", None),
+        P(None, tp),
+        P(None, tp),
+        P(tp, None),
         P("seq"),
         P("seq"),
         P("seq"),
     )
-    out_specs = (P("seq", None), P(("seq", "tp"), None))
-    return jax.shard_map(body, mesh=mesh, in_specs=in_specs, out_specs=out_specs, check_vma=False)
+    out_specs = (P("seq", None), P(("seq", "y", "core"), None))
+    return jax.shard_map(body, mesh=split, in_specs=in_specs, out_specs=out_specs, check_vma=False)

time: 312 us -> 193 us (0.62)
  waiting for transfers between devices: 258 us -> 86.1 us
  starting transfers between devices: 3.19 us -> 42.9 us
  local copies, waits for them, and re-layouts: 3.78 us -> 26.2 us
  between operations: 16.2 us -> 2.45 us
  other arithmetic: 10.8 us -> 17.6 us
    psum x1 -> x0, waiting for transfers between devices: 134 us -> none  [body(): branch = lax.psum(branch_part, 'tp').astype(jnp.float32)]
    unnamed x3 -> x0, waiting for transfers between devices: 121 us -> none
    all_to_all x0 -> x5, waiting for transfers between devices: none -> 82.4 us  [the longest x2 33.4 us: sum_blocks(): got = lax.all_to_all(blocks, 'y', 0, 0)]
    all_to_all x0 -> x5, starting transfers between devices: none -> 19.7 us  [the longest x2 8.39 us: gather_blocks(): lax.all_to_all(jnp.broadcast_to(block[None], (8, high, wide)), 'y', 0, 0)]
    ppermute x0 -> x5, starting transfers between devices: none -> 18.7 us  [the longest x2 11.7 us: sum_blocks(): other = lax.ppermute(rows_of(part, (1 - core) * half, half), 'core', PAIR)]
    reshape x0 -> x6, local copies, waits for them, and re-layouts: none -> 10.2 us  [the longest x4 6.83 us: sum_blocks(): chip.reshape(bands, half // bands, cols, width // cols)]
    convert_element_type x0 -> x3, other arithmetic: none -> 5.33 us  [the longest x1 2.64 us: sum_blocks(): chip = (mine + other.astype(jnp.float32)).astype(jnp.bfloat16)]
    ppermute x0 -> x5, waiting for transfers between devices: none -> 3.67 us  [the longest x1 1.8 us: body(): lax.ppermute(lax.dynamic_index_in_dim(part, 1 - core, 1, keepdims=False),...]
  transfers between devices with their start and end apart: 3 -> 11, of which waited for: 3 -> 8; matrix products, arithmetic and copies ran while one was open for 1% -> 13% of each run, Pallas kernels for 0% -> 0%
where the time goes in v1:
time: 193 us; the launch traced here: 191 us
  waiting for transfers between devices  86.1 us (45%)
  starting transfers between devices  42.9 us (22%)
  local copies, waits for them, and re-layouts  26.2 us (14%)
  other arithmetic  17.6 us (9%)
  matrix products  15.9 us (8%)
  between operations  2.45 us (1%)
    all_to_all x2, waiting for transfers between devices, sum_blocks(): got = lax.all_to_all(blocks, 'y', 0, 0)  33.4 us
    all_to_all x2, waiting for transfers between devices, gather_blocks(): lax.all_to_all(jnp.broadcast_to(block[None], (8, high, wide)), 'y', 0, 0)  32.4 us
    all_to_all x1, waiting for transfers between devices, body(): got = lax.all_to_all((mine + other).astype(jnp.bfloat16), 'y', 0, 0)  16.6 us
    ppermute x2, starting transfers between devices, sum_blocks(): other = lax.ppermute(rows_of(part, (1 - core) * half, half), 'core', PAIR)  11.7 us
    all_to_all x2, starting transfers between devices, gather_blocks(): lax.all_to_all(jnp.broadcast_to(block[None], (8, high, wide)), 'y', 0, 0)  8.39 us
    all_to_all x2, starting transfers between devices, sum_blocks(): got = lax.all_to_all(blocks, 'y', 0, 0)  7.73 us
    reshape x4, local copies, waits for them, and re-layouts, sum_blocks(): chip.reshape(bands, half // bands, cols, width // cols)  6.83 us
    ppermute x2, starting transfers between devices, gather_blocks(): other = lax.ppermute(half, 'core', PAIR)  4.79 us
  transfers between devices with their start and end apart: 11, of which 8 were waited for; matrix products, arithmetic and copies ran while one was open for 13% of the time, Pallas kernels for 0%

profile of v1, /device:TPU:1, one launch (start us, length us, event | category | flops | bytes accessed | tf_op | source)
XLA Modules:
  0.0 191.2 jit_solution(6193104667231504694)
XLA Ops:
  2.1 4.5 %collective-permute-start.2 = (bf16[32,256]{1,0:T(8,128)(2,1)}, bf16[32,256]{1,0:T(8,128)(2,1)}, u32[]{:S(2)}, u32[]{:S(2)}) collective-permute-start(bf16[32,256]{1,0:T(8,128)(2,1)} %slice.11), channel_id=1, source_target_pairs={{0,16},{16,32},{32,48},{48,64},{64,80},{80,96},{96,112},{112,128},... | collective-permute-start | bytes 49160 | tf_op jit(solution)/shard_map/ppermute | solution.py:20
  9.0 2.5 %fusion.25 = bf16[20,2,8,128]{3,2,1,0:T(8,128)(2,1)S(1)} fusion(bf16[3584,256]{1,0:T(8,128)(2,1)} %param.14, f32[3584]{0:T(1024)} %param.13, f32[160]{0:T(256)S(1)} %add_rsqrt_fusion, bf16[160,3584]{1,0:T(8,128)(2,1)} %param.12), kind=kOutput, calls=%fused_computation.46 | convolution fusion | flops 295936000 | bytes 3078784 | tf_op jit(solution)/shard_map/dot_general | solution.py:86
  17.1 9.7 %collective-permute-start = (bf16[80,3584]{1,0:T(8,128)(2,1)}, bf16[80,3584]{1,0:T(8,128)(2,1)S(1)}, u32[]{:S(2)}, u32[]{:S(2)}) collective-permute-start(bf16[80,3584]{1,0:T(8,128)(2,1)} %constant_dynamic-slice_fusion.1), channel_id=1, source_target_pairs={{0,1},{1,0},{2,3},{3,2},{4,5},{5,4},{6,7},{7,6},{8,9},{9,8},{10,11... | collective-permute-start | bytes 1720328 | tf_op jit(solution)/shard_map/ppermute | solution.py:31
  27.6 2.0 %convolution_convert_fusion = bf16[160,3584]{1,0:T(8,128)(2,1)S(1)} fusion(bf16[256,3584]{1,0:T(8,128)(2,1)} %param.11, s32[]{:T(128)S(6)} %select_n.74, bf16[32,256]{1,0:T(8,128)(2,1)} %collective-permute-done.2, bf16[128,256]{1,0:T(8,128)(2,1)} %param.10, bf16[160]{0:T(256)(128)(2,1)S(1)} %pad_dynamic-slice_fusion.3), kind=kOutput, calls=%fused_computation.4 | convolution fusion | flops 294420480 | bytes 3064132 | tf_op jit(solution)/shard_map/dot_general | solution.py:77
  31.5 1.9 collective-permute-start.3
  35.7 2.6 %add_convert_fusion = (bf16[80,3584]{1,0:T(8,128)(2,1)S(1)}, bf16[80,3584]{1,0:T(8,128)(2,1)}) fusion(bf16[80,3584]{1,0:T(8,128)(2,1)} %collective-permute-done.3, bf16[160,3584]{1,0:T(8,128)(2,1)} %copy-done.5, s32[]{:T(128)S(6)} %select_n.70, bf16[80,3584]{1,0:T(8,128)(2,1)} %copy-done.8, bf16[160,3584]{1,0:T(8,128)(2,1)} %copy-done.3), kind=kLoop, calls=%fused_computation.36 | loop fusion | flops 2293760 | bytes 3440644 | tf_op jit(solution)/shard_map/convert_element_type | solution.py:32
  38.3 2.0 %reshape.149 = bf16[2,40,4,896]{3,2,1,0:T(4,128)(2,1)} reshape(bf16[80,3584]{1,0:T(8,128)(2,1)} %get-tuple-element.18) | data formatting | bytes 1146880 | tf_op jit(solution)/shard_map/reshape | solution.py:34
  40.3 2.0 %copy.38 = bf16[2,40,4,896]{3,1,2,0:T(8,128)(2,1)} copy(bf16[2,40,4,896]{3,2,1,0:T(4,128)(2,1)} %reshape.149) | data formatting | bytes 1146880 | tf_op jit(solution)/shard_map/reshape | solution.py:34
  42.3 4.2 %all-to-all-start = ((bf16[8,40,896]{2,1,0:T(8,128)(2,1)}), bf16[8,40,896]{2,1,0:T(8,128)(2,1)}, u32[]{:S(2)}, u32[]{:S(2)}) async-start(bf16[8,40,896]{2,1,0:T(8,128)(2,1)} %bitcast.120), calls=%async_computation | async-start | bytes 1146880 | tf_op jit(solution)/shard_map/all_to_all | solution.py:36
  47.4 1.9 %copy.40 = bf16[2,40,4,896]{3,1,2,0:T(8,128)(2,1)} copy(bf16[2,40,4,896]{3,2,1,0:T(4,128)(2,1)} %reshape.153) | data formatting | bytes 1146880 | tf_op jit(solution)/shard_map/reshape | solution.py:34
  49.3 16.2 %all-to-all-done = bf16[8,40,896]{2,1,0:T(8,128)(2,1)} async-done(((bf16[8,40,896]{2,1,0:T(8,128)(2,1)}), bf16[8,40,896]{2,1,0:T(8,128)(2,1)}, u32[]{:S(2)}, u32[]{:S(2)}) %all-to-all-start) | async-done | bytes 573472 | tf_op jit(solution)/shard_map/all_to_all | solution.py:36
  65.5 3.5 %all-to-all-start.2 = ((bf16[8,40,896]{2,1,0:T(8,128)(2,1)}), bf16[8,40,896]{2,1,0:T(8,128)(2,1)S(1)}, u32[]{:S(2)}, u32[]{:S(2)}) async-start(bf16[8,40,896]{2,1,0:T(8,128)(2,1)} %bitcast.119), calls=%async_computation.2 | async-start | bytes 1146880 | tf_op jit(solution)/shard_map/all_to_all | solution.py:36
  70.9 17.1 %all-to-all-done.2 = bf16[8,40,896]{2,1,0:T(8,128)(2,1)S(1)} async-done(((bf16[8,40,896]{2,1,0:T(8,128)(2,1)}), bf16[8,40,896]{2,1,0:T(8,128)(2,1)S(1)}, u32[]{:S(2)}, u32[]{:S(2)}) %all-to-all-start.2) | async-done | bytes 573472 | tf_op jit(solution)/shard_map/all_to_all | solution.py:36
  88.1 1.7 broadcast_in_dim.20
  89.8 4.2 %all-to-all-start.1 = ((bf16[8,40,896]{2,1,0:T(8,128)(2,1)}), bf16[8,40,896]{2,1,0:T(8,128)(2,1)}, u32[]{:S(2)}, u32[]{:S(2)}) async-start(bf16[8,40,896]{2,1,0:T(8,128)(2,1)} %broadcast_in_dim.20), calls=%async_computation.1 | async-start | bytes 1146880 | tf_op jit(solution)/shard_map/all_to_all | solution.py:43
  94.7 18.3 %all-to-all-done.1 = bf16[8,40,896]{2,1,0:T(8,128)(2,1)} async-done(((bf16[8,40,896]{2,1,0:T(8,128)(2,1)}), bf16[8,40,896]{2,1,0:T(8,128)(2,1)}, u32[]{:S(2)}, u32[]{:S(2)}) %all-to-all-start.1) | async-done | bytes 573472 | tf_op jit(solution)/shard_map/all_to_all | solution.py:43
  113.1 1.7 broadcast_in_dim.22
  114.8 4.2 %all-to-all-start.3 = ((bf16[8,40,896]{2,1,0:T(8,128)(2,1)}), bf16[8,40,896]{2,1,0:T(8,128)(2,1)}, u32[]{:S(2)}, u32[]{:S(2)}) async-start(bf16[8,40,896]{2,1,0:T(8,128)(2,1)} %broadcast_in_dim.22), calls=%async_computation.3 | async-start | bytes 1146880 | tf_op jit(solution)/shard_map/all_to_all | solution.py:43
  120.4 2.4 %collective-permute-start.1 = (bf16[80,3584]{1,0:T(8,128)(2,1)S(1)}, bf16[80,3584]{1,0:T(8,128)(2,1)}, u32[]{:S(2)}, u32[]{:S(2)}) collective-permute-start(bf16[80,3584]{1,0:T(8,128)(2,1)S(1)} %bitcast.115), channel_id=1, source_target_pairs={{0,1},{1,0},{2,3},{3,2},{4,5},{5,4},{6,7},{7,6},{8,9},{9,8},{10,11... | collective-permute-start | bytes 1720328 | tf_op jit(solution)/shard_map/ppermute | solution.py:45
  124.0 14.0 %all-to-all-done.3 = bf16[8,40,896]{2,1,0:T(8,128)(2,1)} async-done(((bf16[8,40,896]{2,1,0:T(8,128)(2,1)}), bf16[8,40,896]{2,1,0:T(8,128)(2,1)}, u32[]{:S(2)}, u32[]{:S(2)}) %all-to-all-start.3) | async-done | bytes 573472 | tf_op jit(solution)/shard_map/all_to_all | solution.py:43
  139.4 2.4 %collective-permute-start.4 = (bf16[80,3584]{1,0:T(8,128)(2,1)S(1)}, bf16[80,3584]{1,0:T(8,128)(2,1)S(1)}, u32[]{:S(2)}, u32[]{:S(2)}) collective-permute-start(bf16[80,3584]{1,0:T(8,128)(2,1)S(1)} %bitcast.117), channel_id=1, source_target_pairs={{0,1},{1,0},{2,3},{3,2},{4,5},{5,4},{6,7},{7,6},{8,9},{9,8},{10,11... | collective-permute-start | bytes 1720328 | tf_op jit(solution)/shard_map/ppermute | solution.py:45
  150.0 2.4 %fusion.45 = f32[160,3584]{1,0:T(8,128)S(1)} fusion(bf16[3584,256]{1,0:T(8,128)(2,1)} %param.14, bf16[2,20,8,128]{3,2,1,0:T(8,128)(2,1)S(1)} %fusion.24), kind=kOutput, calls=%fused_computation.77 | convolution fusion | flops 293601280 | bytes 4210688 | tf_op jit(solution)/shard_map/dot_general | solution.py:145
  152.4 1.8 fusion.2
  154.2 3.3 %reshape.160 = bf16[8,2,280,128]{3,2,1,0:T(8,128)(2,1)} reshape(bf16[160,3584]{1,0:T(8,128)(2,1)} %fusion.2) | data formatting | bytes 2293760 | tf_op jit(solution)/shard_map/reshape | solution.py:157
  157.5 1.9 %dynamic-slice_bitcast_fusion = bf16[8,280,128]{2,1,0:T(8,128)(2,1)} fusion(bf16[8,2,280,128]{3,2,1,0:T(8,128)(2,1)} %reshape.160, s32[]{:T(128)S(6)} %select_n.79), kind=kLoop, calls=%fused_computation.57 | loop fusion | bytes 1146884 | tf_op jit(solution)/shard_map/jit(dynamic_index_in_dim)/squeeze | solution.py:161
  159.4 2.3 %collective-permute-start.5 = (bf16[8,280,128]{2,1,0:T(8,128)(2,1)}, bf16[8,280,128]{2,1,0:T(8,128)(2,1)S(1)}, u32[]{:S(2)}, u32[]{:S(2)}) collective-permute-start(bf16[8,280,128]{2,1,0:T(8,128)(2,1)} %dynamic-slice_bitcast_fusion), channel_id=1, source_target_pairs={{0,1},{1,0},{2,3},{3,2},{4,5},{5,4},{6,7},{7,6},{8,9},{9,8},{10,11... | collective-permute-start | bytes 1720328 | tf_op jit(solution)/shard_map/ppermute | solution.py:160
  161.7 1.8 collective-permute-done.5
  163.5 2.0 %fusion.17 = bf16[8,280,128]{2,1,0:T(8,128)(2,1)} fusion(bf16[8,280,128]{2,1,0:T(8,128)(2,1)S(1)} %collective-permute-done.5, bf16[8,2,280,128]{3,2,1,0:T(8,128)(2,1)} %reshape.160, s32[]{:T(128)S(6)} %select_n.78), kind=kLoop, calls=%fused_computation.32 | loop fusion | flops 1146880 | bytes 1720324 | tf_op jit(solution)/shard_map/convert_element_type | solution.py:163
  165.5 3.5 %all-to-all-start.4 = ((bf16[8,280,128]{2,1,0:T(8,128)(2,1)}), bf16[8,280,128]{2,1,0:T(8,128)(2,1)S(1)}, u32[]{:S(2)}, u32[]{:S(2)}) async-start(bf16[8,280,128]{2,1,0:T(8,128)(2,1)} %fusion.17), calls=%async_computation.4 | async-start | bytes 1146880 | tf_op jit(solution)/shard_map/all_to_all | solution.py:163
  169.1 1.6 convert_element_type.107
  171.4 16.6 %all-to-all-done.4 = bf16[8,280,128]{2,1,0:T(8,128)(2,1)S(1)} async-done(((bf16[8,280,128]{2,1,0:T(8,128)(2,1)}), bf16[8,280,128]{2,1,0:T(8,128)(2,1)S(1)}, u32[]{:S(2)}, u32[]{:S(2)}) %all-to-all-start.4) | async-done | bytes 573472 | tf_op jit(solution)/shard_map/all_to_all | solution.py:163
  189.3 1.9 add_convert_fusion.2
  (85 shorter events, 30.2 us)
Async XLA Ops:
  0.6 14.0 %copy-start = (bf16[256,3584]{1,0:T(8,128)(2,1)S(1)}, bf16[256,3584]{1,0:T(8,128)(2,1)}, u32[]{:S(2)}) copy-start(bf16[256,3584]{1,0:T(8,128)(2,1)} %param.16) | copy-start | bytes 5505028
  2.1 25.5 %collective-permute-start.2 = (bf16[32,256]{1,0:T(8,128)(2,1)}, bf16[32,256]{1,0:T(8,128)(2,1)}, u32[]{:S(2)}, u32[]{:S(2)}) collective-permute-start(bf16[32,256]{1,0:T(8,128)(2,1)} %slice.11), channel_id=1, source_target_pairs={{0,16},{16,32},{32,48},{48,64},{64,80},{80,96},{96,112},{112,128},... | collective-permute-start | bytes 49160 | tf_op jit(solution)/shard_map/ppermute | solution.py:20
  8.2 3.3 %copy-start.14 = (f32[160]{0:T(256)}, f32[160]{0:T(256)S(1)}, u32[]{:S(2)}) copy-start(f32[160]{0:T(256)S(1)} %add_rsqrt_fusion) | copy-start | bytes 1924
  8.9 2.6 %copy-start.2 = (bf16[160,3584]{1,0:T(8,128)(2,1)S(1)}, bf16[160,3584]{1,0:T(8,128)(2,1)}, u32[]{:S(2)}) copy-start(bf16[160,3584]{1,0:T(8,128)(2,1)} %param.12) | copy-start | bytes 3440644
  8.9 2.8 %copy-start.6 = (bf16[3584,256]{1,0:T(8,128)(2,1)S(1)}, bf16[3584,256]{1,0:T(8,128)(2,1)}, u32[]{:S(2)}) copy-start(bf16[3584,256]{1,0:T(8,128)(2,1)} %param.15) | copy-start | bytes 5505028
  9.0 2.7 %copy-start.13 = (f32[3584]{0:T(1024)S(1)}, f32[3584]{0:T(1024)}, u32[]{:S(2)}) copy-start(f32[3584]{0:T(1024)} %param.13) | copy-start | bytes 43012
  11.7 0.7 copy-start.17
  12.4 2.8 %copy-start.9 = (bf16[160,1,128]{2,1,0:T(2,128)(2,1)}, bf16[160,1,128]{2,1,0:T(2,128)(2,1)S(1)}, u32[]{:S(2)}) copy-start(bf16[160,1,128]{2,1,0:T(2,128)(2,1)S(1)} %get-tuple-element.13) | copy-start | bytes 122884
  12.4 2.8 %copy-start.11 = (bf16[160,1,128]{2,1,0:T(2,128)(2,1)}, bf16[160,1,128]{2,1,0:T(2,128)(2,1)S(1)}, u32[]{:S(2)}) copy-start(bf16[160,1,128]{2,1,0:T(2,128)(2,1)S(1)} %get-tuple-element.12) | copy-start | bytes 122884
  13.4 1.7 copy-start.19
  15.2 1.0 copy-start.3
  17.1 16.3 %collective-permute-start = (bf16[80,3584]{1,0:T(8,128)(2,1)}, bf16[80,3584]{1,0:T(8,128)(2,1)S(1)}, u32[]{:S(2)}, u32[]{:S(2)}) collective-permute-start(bf16[80,3584]{1,0:T(8,128)(2,1)} %constant_dynamic-slice_fusion.1), channel_id=1, source_target_pairs={{0,1},{1,0},{2,3},{3,2},{4,5},{5,4},{6,7},{7,6},{8,9},{9,8},{10,11... | collective-permute-start | bytes 1720328 | tf_op jit(solution)/shard_map/ppermute | solution.py:31
  29.6 1.0 copy-start.5
  31.5 4.2 %collective-permute-start.3 = (bf16[80,3584]{1,0:T(8,128)(2,1)}, bf16[80,3584]{1,0:T(8,128)(2,1)}, u32[]{:S(2)}, u32[]{:S(2)}) collective-permute-start(bf16[80,3584]{1,0:T(8,128)(2,1)} %constant_dynamic-slice_fusion), channel_id=1, source_target_pairs={{0,1},{1,0},{2,3},{3,2},{4,5},{5,4},{6,7},{7,6},{8,9},{9,8},{10,11... | collective-permute-start | bytes 1720328 | tf_op jit(solution)/shard_map/ppermute | solution.py:31
  33.4 0.8 copy-start.8
  42.3 23.3 %all-to-all-start = ((bf16[8,40,896]{2,1,0:T(8,128)(2,1)}), bf16[8,40,896]{2,1,0:T(8,128)(2,1)}, u32[]{:S(2)}, u32[]{:S(2)}) async-start(bf16[8,40,896]{2,1,0:T(8,128)(2,1)} %bitcast.120), calls=%async_computation | async-start | bytes 1146880 | tf_op jit(solution)/shard_map/all_to_all | solution.py:36
  65.5 22.5 %all-to-all-start.2 = ((bf16[8,40,896]{2,1,0:T(8,128)(2,1)}), bf16[8,40,896]{2,1,0:T(8,128)(2,1)S(1)}, u32[]{:S(2)}, u32[]{:S(2)}) async-start(bf16[8,40,896]{2,1,0:T(8,128)(2,1)} %bitcast.119), calls=%async_computation.2 | async-start | bytes 1146880 | tf_op jit(solution)/shard_map/all_to_all | solution.py:36
  89.8 23.3 %all-to-all-start.1 = ((bf16[8,40,896]{2,1,0:T(8,128)(2,1)}), bf16[8,40,896]{2,1,0:T(8,128)(2,1)}, u32[]{:S(2)}, u32[]{:S(2)}) async-start(bf16[8,40,896]{2,1,0:T(8,128)(2,1)} %broadcast_in_dim.20), calls=%async_computation.1 | async-start | bytes 1146880 | tf_op jit(solution)/shard_map/all_to_all | solution.py:43
  114.8 23.3 %all-to-all-start.3 = ((bf16[8,40,896]{2,1,0:T(8,128)(2,1)}), bf16[8,40,896]{2,1,0:T(8,128)(2,1)}, u32[]{:S(2)}, u32[]{:S(2)}) async-start(bf16[8,40,896]{2,1,0:T(8,128)(2,1)} %broadcast_in_dim.22), calls=%async_computation.3 | async-start | bytes 1146880 | tf_op jit(solution)/shard_map/all_to_all | solution.py:43
  120.4 21.5 %collective-permute-start.1 = (bf16[80,3584]{1,0:T(8,128)(2,1)S(1)}, bf16[80,3584]{1,0:T(8,128)(2,1)}, u32[]{:S(2)}, u32[]{:S(2)}) collective-permute-start(bf16[80,3584]{1,0:T(8,128)(2,1)S(1)} %bitcast.115), channel_id=1, source_target_pairs={{0,1},{1,0},{2,3},{3,2},{4,5},{5,4},{6,7},{7,6},{8,9},{9,8},{10,11... | collective-permute-start | bytes 1720328 | tf_op jit(solution)/shard_map/ppermute | solution.py:45
  139.4 4.0 %collective-permute-start.4 = (bf16[80,3584]{1,0:T(8,128)(2,1)S(1)}, bf16[80,3584]{1,0:T(8,128)(2,1)S(1)}, u32[]{:S(2)}, u32[]{:S(2)}) collective-permute-start(bf16[80,3584]{1,0:T(8,128)(2,1)S(1)} %bitcast.117), channel_id=1, source_target_pairs={{0,1},{1,0},{2,3},{3,2},{4,5},{5,4},{6,7},{7,6},{8,9},{9,8},{10,11... | collective-permute-start | bytes 1720328 | tf_op jit(solution)/shard_map/ppermute | solution.py:45
  143.5 0.8 copy-start.15
  144.3 1.0 copy-start.4
  145.3 1.4 copy-start.1
  145.3 1.4 copy-start.16
  145.3 1.4 copy-start.20
  145.3 1.6 copy-start.10
  145.3 1.9 copy-start.18
  146.7 1.8 copy-start.12
  150.0 2.4 %copy-start.7 = (bf16[3584,256]{1,0:T(8,128)(2,1)S(1)}, bf16[3584,256]{1,0:T(8,128)(2,1)}, u32[]{:S(2)}) copy-start(bf16[3584,256]{1,0:T(8,128)(2,1)} %param.15) | copy-start | bytes 5505028
  159.4 4.1 %collective-permute-start.5 = (bf16[8,280,128]{2,1,0:T(8,128)(2,1)}, bf16[8,280,128]{2,1,0:T(8,128)(2,1)S(1)}, u32[]{:S(2)}, u32[]{:S(2)}) collective-permute-start(bf16[8,280,128]{2,1,0:T(8,128)(2,1)} %dynamic-slice_bitcast_fusion), channel_id=1, source_target_pairs={{0,1},{1,0},{2,3},{3,2},{4,5},{5,4},{6,7},{7,6},{8,9},{9,8},{10,11... | collective-permute-start | bytes 1720328 | tf_op jit(solution)/shard_map/ppermute | solution.py:160
  165.5 22.5 %all-to-all-start.4 = ((bf16[8,280,128]{2,1,0:T(8,128)(2,1)}), bf16[8,280,128]{2,1,0:T(8,128)(2,1)S(1)}, u32[]{:S(2)}, u32[]{:S(2)}) async-start(bf16[8,280,128]{2,1,0:T(8,128)(2,1)} %fusion.17), calls=%async_computation.4 | async-start | bytes 1146880 | tf_op jit(solution)/shard_map/all_to_all | solution.py:163

commit v2 on v0

v2 whole, which is shorter than its diff:
```python
import math

import jax
import jax.numpy as jnp
from jax import lax
from jax.experimental import pallas as pl
from jax.experimental.pallas import tpu as pltpu
from jax.sharding import Mesh
from jax.sharding import PartitionSpec as P

HD = 128
QPK = 2
PAIR = [(0, 1), (1, 0)]
COLS = 4
TP = ("y", "core")
CUT = 24

epsilon = 1e-06

VMEM = pl.BlockSpec(memory_space=pltpu.VMEM)
SMEM = pl.BlockSpec(memory_space=pltpu.SMEM)
ANY = pl.BlockSpec(memory_space=pl.ANY)
F32 = jnp.float32
BF16 = jnp.bfloat16


def shape(dims, dtype):
    return jax.ShapeDtypeStruct(dims, dtype)


def nt(a, b):
    return lax.dot_general(a, b, (((1,), (1,)), ((), ())), preferred_element_type=F32)


def tn(a, b):
    return lax.dot_general(a, b, (((0,), (0,)), ((), ())), preferred_element_type=F32)


def nn(a, b):
    return jnp.dot(a, b, preferred_element_type=F32)


def emit_blocks(core, lhs_ref, weight_ref, mine_ref, send_ref):
    half = lhs_ref.shape[0] // 2
    high, wide = mine_ref.shape[1:]
    first = lhs_ref[pl.ds(pl.multiple_of(core * half, 16), half), :]
    second = lhs_ref[pl.ds(pl.multiple_of((1 - core) * half, 16), half), :]
    lhs = jnp.concatenate([first, second], axis=0)
    for j in range(COLS):
        out = nn(lhs, weight_ref[:, j * wide : (j + 1) * wide])
        for i in range(2):
            mine_ref[i * COLS + j] = out[i * high : (i + 1) * high].astype(BF16)
            send_ref[i * COLS + j] = out[half + i * high : half + (i + 1) * high].astype(BF16)


def goal_kernel(core_ref, rows_ref, weight_ref, mine_ref, send_ref):
    emit_blocks(core_ref[0], rows_ref, weight_ref, mine_ref, send_ref)


def forward_kernel(
    core_ref,
    x_ref,
    gain_ref,
    starts_ref,
    w_query_hbm,
    w_keyval_hbm,
    w_out_hbm,
    query_ref,
    keyval_ref,
    probs_ref,
    mine_ref,
    send_ref,
    w_query,
    w_keyval,
    w_out,
    attn_ref,
    sems,
):
    loads = [
        pltpu.make_async_copy(source, target, sems.at[n])
        for n, (source, target) in enumerate(
            ((w_query_hbm, w_query), (w_keyval_hbm, w_keyval), (w_out_hbm, w_out))
        )
    ]
    for load in loads:
        load.start()
    slots = x_ref.shape[0]
    xf = x_ref[...].astype(F32)
    inv = lax.rsqrt(jnp.mean(xf * xf, axis=1, keepdims=True) + epsilon)
    normed = (xf * inv * gain_ref[...]).astype(BF16)
    loads[0].wait()
    query = nn(normed, w_query[...]).astype(BF16)
    query_ref[...] = query
    loads[1].wait()
    keyval = nn(normed, w_keyval[...]).astype(BF16)
    keyval_ref[...] = keyval
    keys = keyval[:, :HD]
    values = keyval[:, HD:]
    row = lax.broadcasted_iota(jnp.int32, (slots, slots), 0)
    col = lax.broadcasted_iota(jnp.int32, (slots, slots), 1)
    allowed = (col >= starts_ref[...]) & (col <= row)
    for e in range(QPK):
        scores = nt(query[:, e * HD : (e + 1) * HD], keys) * (1.0 / math.sqrt(HD))
        scores = jnp.where(allowed, scores, -jnp.inf)
        expo = jnp.exp(scores - jnp.max(scores, axis=1, keepdims=True))
        probs = expo / jnp.sum(expo, axis=1, keepdims=True)
        probs_ref[e] = probs
        attn_ref[:, e * HD : (e + 1) * HD] = nn(probs.astype(BF16), values).astype(BF16)
    loads[2].wait()
    emit_blocks(core_ref[0], attn_ref, w_out, mine_ref, send_ref)


def total_kernel(got_ref, x_ref, out_ref):
    total = x_ref[...].astype(F32)
    branch = got_ref[0].astype(F32)
    for n in range(1, got_ref.shape[0]):
        branch = branch + got_ref[n].astype(F32)
    total = (total + branch).astype(BF16)
    for n in range(out_ref.shape[0]):
        out_ref[n] = total


def backward_kernel(
    core_ref,
    count_ref,
    own_ref,
    other_ref,
    top_ref,
    bottom_ref,
    probs_ref,
    query_ref,
    keyval_ref,
    w_out_hbm,
    w_query_hbm,
    w_keyval_hbm,
    student_ref,
    dy_hbm,
    mine_ref,
    send_ref,
    w_out,
    w_query,
    w_keyval,
    dy_ref,
    dyb_ref,
    grads_ref,
    sems,
):
    loads = [
        pltpu.make_async_copy(source, target, sems.at[n])
        for n, (source, target) in enumerate(
            ((w_out_hbm, w_out), (w_query_hbm, w_query), (w_keyval_hbm, w_keyval))
        )
    ]
    for load in loads:
        load.start()
    core = core_ref[0]
    count = count_ref[0]
    slots, width = student_ref.shape
    high, wide = own_ref.shape[1:]
    for c in range(2):
        for i in range(2):
            y, t = [], []
            for j in range(COLS):
                n = i * COLS + j
                block = jnp.where(core == c, own_ref[n].astype(F32), other_ref[n].astype(F32))
                y.append(block)
                t.append(
                    jnp.concatenate(
                        [top_ref[2 * n + c].astype(F32), bottom_ref[2 * n + c].astype(F32)], axis=0
                    )
                )
            asum = sum(jnp.sum(a * a, axis=1, keepdims=True) for a in y) + epsilon
            bsum = sum(jnp.sum(a * a, axis=1, keepdims=True) for a in t) + epsilon
            dots = sum(jnp.sum(a * b, axis=1, keepdims=True) for a, b in zip(y, t))
            both = lax.rsqrt(asum * bsum)
            first = (2 * c + i) * high
            live = (
                lax.broadcasted_iota(jnp.int32, (high, 1), 0) + first < count
            ).astype(F32)
            factor = -math.sqrt(width) * live
            t_scale = factor * both
            y_scale = factor * (dots * both) / asum
            for j in range(COLS):
                dy = t[j] * t_scale - y[j] * y_scale
                where = (slice(first, first + high), slice(j * wide, (j + 1) * wide))
                student_ref[where] = y[j].astype(BF16)
                dy_ref[where] = dy
                dyb_ref[where] = dy.astype(BF16)
    store = pltpu.make_async_copy(dy_ref, dy_hbm, sems.at[3])
    store.start()
    loads[0].wait()
    d_attn = nt(dyb_ref[...], w_out[...]).astype(BF16)
    keys = keyval_ref[:, :HD]
    values = keyval_ref[:, HD:]
    d_keys = d_values = None
    for e in range(QPK):
        head = slice(e * HD, (e + 1) * HD)
        d_out = d_attn[:, head]
        probs = probs_ref[e]
        d_value = tn(probs.astype(BF16), d_out)
        dprob = nt(d_out, values)
        dscore = probs * (dprob - jnp.sum(dprob * probs, axis=1, keepdims=True))
        dscore = (dscore * (1.0 / math.sqrt(HD))).astype(BF16)
        grads_ref[:, head] = nn(dscore, keys).astype(BF16)
        d_key = tn(dscore, query_ref[:, head])
        d_keys = d_key if d_keys is None else d_keys + d_key
        d_values = d_value if d_values is None else d_values + d_value
    grads_ref[:, QPK * HD : (QPK + 1) * HD] = d_keys.astype(BF16)
    grads_ref[:, (QPK + 1) * HD :] = d_values.astype(BF16)
    half = slots // 2
    row = lax.broadcasted_iota(jnp.int32, (slots, slots), 0)
    col = lax.broadcasted_iota(jnp.int32, (slots, slots), 1)
    sent = (row >= half).astype(jnp.int32)
    place = row - half * sent
    parity = core + sent - 2 * core * sent
    late = (place >= 64).astype(jnp.int32)
    early_row = 20 * (place >> 3) + (place & 7)
    late_row = 20 * ((place - 64) >> 1) + 8 + (place & 1)
    source = early_row + late * (late_row - early_row) + 10 * parity
    pick = (col == source).astype(BF16)
    rows = nn(pick, grads_ref[...]).astype(BF16)
    loads[1].wait()
    loads[2].wait()
    sub = lax.broadcasted_iota(jnp.int32, (8, HD), 0) >> 1
    for j in range(width // (4 * HD)):
        span = slice(j * 4 * HD, (j + 1) * 4 * HD)
        part = nt(rows[:, : QPK * HD], w_query[span, :]) + nt(rows[:, QPK * HD :], w_keyval[span, :])
        for h, ref in ((0, mine_ref), (1, send_ref)):
            base = h * half
            for k in range(4):
                lane = slice(k * HD, (k + 1) * HD)
                at = 8 * (4 * j + k)
                for n in range(8):
                    ref[n, at : at + 8, :] = part[base + 8 * n : base + 8 * n + 8, lane].astype(BF16)
            for g in range(2):
                low = base + 64 + 8 * g
                tiles = [part[low : low + 8, k * HD : (k + 1) * HD] for k in range(4)]
                for i in range(4):
                    tile = None
                    for k in range(4):
                        turned = pltpu.roll(tiles[k], (2 * k - 2 * i) % 8, 0) if k != i else tiles[k]
                        tile = turned if tile is None else jnp.where(sub == k, turned, tile)
                    at = 224 + 8 * j
                    ref[4 * g + i, at : at + 8, :] = tile.astype(BF16)
    store.wait()


def final_kernel(got_ref, x_ref, dy_ref, gain_ref, out_ref, rows_ref):
    total = got_ref[0].astype(F32)
    for n in range(1, got_ref.shape[0]):
        total = total + got_ref[n].astype(F32)
    for t in range(28):
        lane = slice(t * HD, (t + 1) * HD)
        rows_ref[0:8, lane] = total[8 * t : 8 * t + 8]
        at = 224 + 2 * t
        rows_ref[8:10, lane] = total[at : at + 2]
    x = x_ref[...].astype(F32)
    inv = lax.rsqrt(jnp.mean(x * x, axis=1, keepdims=True) + epsilon)
    upper = rows_ref[0:10, :] * gain_ref[...]
    dx = inv * upper - x * (inv * inv * inv) * jnp.mean(upper * x, axis=1, keepdims=True)
    out_ref[...] = (dy_ref[...] + dx).astype(BF16)


def from_behind(block, axis, distance):
    devices = range(lax.axis_size(axis))
    route = [(i - distance, i) for i in devices if i - distance in devices]
    return lax.ppermute(block, axis, route)


def swap(block):
    return lax.ppermute(block, "core", PAIR)


def spread(mine, send):
    other = swap(send)
    chip = (mine.astype(F32) + other.astype(F32)).astype(BF16)
    return lax.all_to_all(chip, "y", 0, 0)


def body(
    teacher_hidden,
    proj_weight,
    student_in,
    norm_gain,
    w_query,
    w_keyval,
    w_out,
    row_offsets,
    row_counts,
    doc_start,
):
    tokens_here = teacher_hidden.shape[0]
    quarter = tokens_here // 4
    slots, width = student_in.shape
    high, wide = slots // 4, width // COLS
    core = lax.axis_index("core")
    ypos = lax.axis_index("y")
    core_s = core.astype(jnp.int32).reshape(1)
    start = row_offsets[0] - lax.axis_index("seq") * tokens_here + quarter
    blocks = shape((8, high, wide), BF16)
    with jax.named_scope("shift"):
        earlier = from_behind(teacher_hidden[tokens_here - quarter :], "seq", 1)
    blank = jnp.zeros((quarter, teacher_hidden.shape[1]), BF16)
    window = jnp.concatenate([earlier, teacher_hidden, blank], axis=0)
    window = lax.dynamic_slice_in_dim(window, start, slots, 0)
    goal_mine, goal_send = pl.pallas_call(
        goal_kernel,
        out_shape=(blocks, blocks),
        in_specs=[SMEM, VMEM, VMEM],
        out_specs=(VMEM, VMEM),
        name="goal",
    )(core_s, window, proj_weight)
    with jax.named_scope("rsa"):
        goal_got = spread(goal_mine, goal_send)
    gain = norm_gain.reshape(1, width)
    query, keyval, probs, mine, send = pl.pallas_call(
        forward_kernel,
        out_shape=(
            shape((slots, QPK * HD), BF16),
            shape((slots, 2 * HD), BF16),
            shape((QPK, slots, slots), F32),
            blocks,
            blocks,
        ),
        in_specs=[SMEM, VMEM, VMEM, VMEM, ANY, ANY, ANY],
        out_specs=(VMEM,) * 5,
        scratch_shapes=[
            pltpu.VMEM(w_query.shape, BF16),
            pltpu.VMEM(w_keyval.shape, BF16),
            pltpu.VMEM(w_out.shape, BF16),
            pltpu.VMEM((slots, QPK * HD), BF16),
            pltpu.SemaphoreType.DMA((3,)),
        ],
        name="forward",
    )(core_s, student_in, gain, doc_start.reshape(slots, 1), w_query, w_keyval, w_out)
    with jax.named_scope("rsb"):
        branch_got = spread(mine, send)
    goal_own = jnp.sum(goal_got.astype(F32), axis=0).astype(BF16)
    with jax.named_scope("agt1"):
        goal_top = lax.all_gather(goal_own[:CUT], TP)
    with jax.named_scope("agt2"):
        goal_bottom = lax.all_gather(goal_own[CUT:], TP)
    x_block = lax.dynamic_slice(
        student_in,
        (core * (slots // 2) + (ypos // COLS) * high, (ypos % COLS) * wide),
        (high, wide),
    )
    y_own = pl.pallas_call(
        total_kernel, out_shape=blocks, in_specs=[VMEM, VMEM], out_specs=VMEM, name="total"
    )(branch_got, x_block)
    with jax.named_scope("agy"):
        y_half = lax.all_to_all(y_own, "y", 0, 0)
    y_other = swap(y_half)
    pieces = shape((8, slots // 16 * (width // HD), HD), BF16)
    student_out, dy, mine, send = pl.pallas_call(
        backward_kernel,
        out_shape=(shape((slots, width), BF16), shape((slots, width), F32), pieces, pieces),
        in_specs=[SMEM, SMEM] + [VMEM] * 7 + [ANY] * 3,
        out_specs=(VMEM, ANY, VMEM, VMEM),
        scratch_shapes=[
            pltpu.VMEM(w_out.shape, BF16),
            pltpu.VMEM(w_query.shape, BF16),
            pltpu.VMEM(w_keyval.shape, BF16),
            pltpu.VMEM((slots, width), F32),
            pltpu.VMEM((slots, width), BF16),
            pltpu.VMEM((slots, (QPK + 2) * HD), BF16),
            pltpu.SemaphoreType.DMA((4,)),
        ],
        name="backward",
    )(
        core_s,
        row_counts,
        y_half,
        y_other,
        goal_top,
        goal_bottom,
        probs,
        query,
        keyval,
        w_out,
        w_query,
        w_keyval,
    )
    with jax.named_scope("rsd"):
        got = spread(mine, send)
    own_rows = slots // 16
    first_row = (ypos * 2 + core) * own_rows
    x_own = lax.dynamic_slice_in_dim(student_in, first_row, own_rows, 0)
    dy_own = lax.dynamic_slice_in_dim(dy, first_row, own_rows, 0)
    grad_in = pl.pallas_call(
        final_kernel,
        out_shape=shape((own_rows, width), BF16),
        in_specs=[VMEM] * 4,
        out_specs=VMEM,
        scratch_shapes=[pltpu.VMEM((16, width), F32)],
        name="final",
    )(got, x_own, dy_own, gain)
    return (student_out, grad_in)


def solution(mesh):
    seqs, tps = mesh.devices.shape
    split = Mesh(mesh.devices.reshape(seqs, tps // 2, 2), ("seq",) + TP)
    in_specs = (
        P("seq", TP),
        P(TP, None),
        P("seq", None),
        P(),
        P(None, TP),
        P(None, TP),
        P(TP, None),
        P("seq"),
        P("seq"),
        P("seq"),
    )
    out_specs = (P("seq", None), P(("seq",) + TP, None))
    return jax.shard_map(body, mesh=split, in_specs=in_specs, out_specs=out_specs, check_vma=False)
```

time: 312 us -> 175 us (0.56)
  waiting for transfers between devices: 258 us -> 61.6 us
  blocking collectives: 0 us -> 36.5 us
  starting transfers between devices: 3.19 us -> 34.7 us
  Pallas kernels: 0 us -> 22.2 us
  matrix products: 19 us -> 0 us
  between operations: 16.2 us -> 2.11 us
  local copies, waits for them, and re-layouts: 3.78 us -> 10.1 us
  other arithmetic: 10.8 us -> 6.88 us
    psum x1 -> x0, waiting for transfers between devices: 134 us -> none  [body(): branch = lax.psum(branch_part, 'tp').astype(jnp.float32)]
    unnamed x3 -> x0, waiting for transfers between devices: 121 us -> none
    all_to_all x0 -> x4, waiting for transfers between devices: none -> 56 us  [the longest x3 47 us: spread(): return lax.all_to_all(chip, 'y', 0, 0)]
    all_gather x0 -> x2, blocking collectives: none -> 36.5 us  [the longest x1 18.9 us: body(): goal_top = lax.all_gather(goal_own[:CUT], TP)]
    pallas_call x0 -> x5, Pallas kernels: none -> 22.2 us  [the longest x1 8.74 us: body(): pl.pallas_call(backward_kernel, out_shape=(shape((slots, width), BF16), s...]
    ppermute x0 -> x4, starting transfers between devices: none -> 19.2 us  [swap(): return lax.ppermute(block, 'core', PAIR)]
    dot_general x12 -> x0, matrix products: 18 us -> none  [the longest x1 2.88 us: body(): jnp.dot(teacher_hidden, proj_weight, preferred_element_type=jnp.float32)]
    all_to_all x0 -> x4, starting transfers between devices: none -> 14.2 us  [the longest x3 10.6 us: spread(): return lax.all_to_all(chip, 'y', 0, 0)]
  transfers between devices with their start and end apart: 3 -> 9, of which waited for: 3 -> 7; matrix products, arithmetic and copies ran while one was open for 1% -> 4% of each run, Pallas kernels for 0% -> 3%
where the time goes in v2:
time: 175 us; the launch traced here: 174 us
  waiting for transfers between devices  61.6 us (35%)
  blocking collectives  36.5 us (21%)
  starting transfers between devices  34.7 us (20%)
  Pallas kernels  22.2 us (13%)
  local copies, waits for them, and re-layouts  10.1 us (6%)
  other arithmetic  6.88 us (4%)
  between operations  2.11 us (1%)
    all_to_all x3, waiting for transfers between devices, spread(): return lax.all_to_all(chip, 'y', 0, 0)  47 us
    ppermute x4, starting transfers between devices, swap(): return lax.ppermute(block, 'core', PAIR)  19.2 us
    all_gather x1, blocking collectives, body(): goal_top = lax.all_gather(goal_own[:CUT], TP)  18.9 us
    all_gather x1, blocking collectives, body(): goal_bottom = lax.all_gather(goal_own[CUT:], TP)  17.6 us
    all_to_all x3, starting transfers between devices, spread(): return lax.all_to_all(chip, 'y', 0, 0)  10.6 us
    all_to_all x1, waiting for transfers between devices, body(): y_half = lax.all_to_all(y_own, 'y', 0, 0)  9 us
    pallas_call x1, Pallas kernels, body(): pl.pallas_call(backward_kernel, out_shape=(shape((slots, width), BF16), s...  8.74 us
    pallas_call x1, Pallas kernels, body(): pl.pallas_call(forward_kernel, out_shape=(shape((slots, QPK * HD), BF16),...  6.34 us
  transfers between devices with their start and end apart: 9, of which 7 were waited for; matrix products, arithmetic and copies ran while one was open for 4% of the time, Pallas kernels for 3%

profile of v2, /device:TPU:1, one launch (start us, length us, event | category | flops | bytes accessed | tf_op | source)
XLA Modules:
  0.0 174.0 jit_solution(14441096959971406160)
XLA Ops:
  0.6 1.3 reshape.14.gain_ref
  2.0 1.4 copy.12.starts_ref
  3.4 6.3 %forward.1 = (bf16[160,256]{1,0:T(8,128)(2,1)}, bf16[160,256]{1,0:T(8,128)(2,1)}, f32[2,160,160]{2,1,0:T(8,128)}, bf16[8,40,896]{2,1,0:T(8,128)(2,1)}, bf16[8,40,896]{2,1,0:T(8,128)(2,1)}) custom-call(s32[1]{0:T(128)} %bitcast.core_ref, bf16[160,3584]{1,0:T(8,128)(2,1)} %x_ref.1, f32[1,3584]{1,0:T(1,128)} %reshape.14.gain_ref, s32[160,1]{1,0:T(8,128)} %copy.12.starts_ref, ...), custom_call_target="tpu_custom_call" | custom-call | tf_op jit(solution)/shard_map/forward/pallas_call | solution.py:316
  9.7 12.4 %collective-permute-start = (bf16[8,40,896]{2,1,0:T(8,128)(2,1)}, bf16[8,40,896]{2,1,0:T(8,128)(2,1)S(1)}, u32[]{:S(2)}, u32[]{:S(2)}) collective-permute-start(bf16[8,40,896]{2,1,0:T(8,128)(2,1)} %get-tuple-element.14), channel_id=1, source_target_pairs={{0,1},{1,0},{2,3},{3,2},{4,5},{5,4},{6,7},{7,6},{8,9},{9,8},{10,11... | collective-permute-start | bytes 1720328 | tf_op jit(solution)/shard_map/rsb/ppermute | solution.py:271
  22.1 1.8 %collective-permute-done = bf16[8,40,896]{2,1,0:T(8,128)(2,1)S(1)} collective-permute-done((bf16[8,40,896]{2,1,0:T(8,128)(2,1)}, bf16[8,40,896]{2,1,0:T(8,128)(2,1)S(1)}, u32[]{:S(2)}, u32[]{:S(2)}) %collective-permute-start) | collective-permute-done | bytes 573472 | tf_op jit(solution)/shard_map/rsb/ppermute | solution.py:271
  23.9 2.0 %add_convert_fusion.2 = bf16[8,40,896]{2,1,0:T(8,128)(2,1)} fusion(bf16[8,40,896]{2,1,0:T(8,128)(2,1)S(1)} %collective-permute-done, bf16[8,40,896]{2,1,0:T(8,128)(2,1)} %get-tuple-element.13), kind=kLoop, calls=%fused_computation.2 | loop fusion | flops 1146880 | bytes 1720320 | tf_op jit(solution)/shard_map/rsb/convert_element_type | solution.py:276
  26.0 3.5 %all-to-all-start = ((bf16[8,40,896]{2,1,0:T(8,128)(2,1)}), bf16[8,40,896]{2,1,0:T(8,128)(2,1)S(1)}, u32[]{:S(2)}, u32[]{:S(2)}) async-start(bf16[8,40,896]{2,1,0:T(8,128)(2,1)} %add_convert_fusion.2), calls=%async_computation | async-start | bytes 1146880 | tf_op jit(solution)/shard_map/rsb/all_to_all | solution.py:277
  29.5 1.3 collective-permute-start.2
  31.6 1.5 dynamic_slice.12.x_ref
  33.1 15.4 %all-to-all-done.got_ref = bf16[8,40,896]{2,1,0:T(8,128)(2,1)S(1)} async-done(((bf16[8,40,896]{2,1,0:T(8,128)(2,1)}), bf16[8,40,896]{2,1,0:T(8,128)(2,1)S(1)}, u32[]{:S(2)}, u32[]{:S(2)}) %all-to-all-start) | async-done | bytes 573472 | tf_op jit(solution)/shard_map/rsb/all_to_all | solution.py:277
  49.3 2.0 %total.1 = bf16[8,40,896]{2,1,0:T(8,128)(2,1)} custom-call(bf16[8,40,896]{2,1,0:T(8,128)(2,1)} %copy-done.1, bf16[40,896]{1,0:T(8,128)(2,1)} %dynamic_slice.12.x_ref), custom_call_target="tpu_custom_call" | custom-call | tf_op jit(solution)/shard_map/total/pallas_call | solution.py:348
  51.3 3.5 %all-to-all-start.1 = ((bf16[8,40,896]{2,1,0:T(8,128)(2,1)}), bf16[8,40,896]{2,1,0:T(8,128)(2,1)S(1)}, u32[]{:S(2)}, u32[]{:S(2)}) async-start(bf16[8,40,896]{2,1,0:T(8,128)(2,1)} %total.1), calls=%async_computation.1 | async-start | bytes 1146880 | tf_op jit(solution)/shard_map/agy/all_to_all | solution.py:352
  55.6 3.1 %goal.1 = (bf16[8,40,896]{2,1,0:T(8,128)(2,1)}, bf16[8,40,896]{2,1,0:T(8,128)(2,1)}) custom-call(s32[1]{0:T(128)} %bitcast.core_ref, bf16[160,256]{1,0:T(8,128)(2,1)} %fusion.1.rows_ref, bf16[256,3584]{1,0:T(8,128)(2,1)} %weight_ref.1), custom_call_target="tpu_custom_call" | custom-call | tf_op jit(solution)/shard_map/goal/pallas_call | solution.py:306
  58.6 2.4 %collective-permute-start.3 = (bf16[8,40,896]{2,1,0:T(8,128)(2,1)}, bf16[8,40,896]{2,1,0:T(8,128)(2,1)S(1)}, u32[]{:S(2)}, u32[]{:S(2)}) collective-permute-start(bf16[8,40,896]{2,1,0:T(8,128)(2,1)} %get-tuple-element.16), channel_id=1, source_target_pairs={{0,1},{1,0},{2,3},{3,2},{4,5},{5,4},{6,7},{7,6},{8,9},{9,8},{10,11... | collective-permute-start | bytes 1720328 | tf_op jit(solution)/shard_map/rsa/ppermute | solution.py:271
  61.0 1.8 %collective-permute-done.3 = bf16[8,40,896]{2,1,0:T(8,128)(2,1)S(1)} collective-permute-done((bf16[8,40,896]{2,1,0:T(8,128)(2,1)}, bf16[8,40,896]{2,1,0:T(8,128)(2,1)S(1)}, u32[]{:S(2)}, u32[]{:S(2)}) %collective-permute-start.3) | collective-permute-done | bytes 573472 | tf_op jit(solution)/shard_map/rsa/ppermute | solution.py:271
  62.8 2.0 %add_convert_fusion.1 = bf16[8,40,896]{2,1,0:T(8,128)(2,1)} fusion(bf16[8,40,896]{2,1,0:T(8,128)(2,1)S(1)} %collective-permute-done.3, bf16[8,40,896]{2,1,0:T(8,128)(2,1)} %get-tuple-element.15), kind=kLoop, calls=%fused_computation.1 | loop fusion | flops 1146880 | bytes 1720320 | tf_op jit(solution)/shard_map/rsa/convert_element_type | solution.py:276
  64.8 9.0 %all-to-all-done.1.own_ref = bf16[8,40,896]{2,1,0:T(8,128)(2,1)S(1)} async-done(((bf16[8,40,896]{2,1,0:T(8,128)(2,1)}), bf16[8,40,896]{2,1,0:T(8,128)(2,1)S(1)}, u32[]{:S(2)}, u32[]{:S(2)}) %all-to-all-start.1) | async-done | bytes 573472 | tf_op jit(solution)/shard_map/agy/all_to_all | solution.py:352
  73.8 3.5 %all-to-all-start.2 = ((bf16[8,40,896]{2,1,0:T(8,128)(2,1)}), bf16[8,40,896]{2,1,0:T(8,128)(2,1)S(1)}, u32[]{:S(2)}, u32[]{:S(2)}) async-start(bf16[8,40,896]{2,1,0:T(8,128)(2,1)} %add_convert_fusion.1), calls=%async_computation.2 | async-start | bytes 1146880 | tf_op jit(solution)/shard_map/rsa/all_to_all | solution.py:277
  77.3 2.4 %collective-permute-start.1 = (bf16[8,40,896]{2,1,0:T(8,128)(2,1)S(1)}, bf16[8,40,896]{2,1,0:T(8,128)(2,1)S(1)}, u32[]{:S(2)}, u32[]{:S(2)}) collective-permute-start(bf16[8,40,896]{2,1,0:T(8,128)(2,1)S(1)} %all-to-all-done.1.own_ref), channel_id=1, source_target_pairs={{0,1},{1,0},{2,3},{3,2},{4,5},{5,4},{6,7},{7,6},{8,9},{9,8},{10,11... | collective-permute-start | bytes 1720328 | tf_op jit(solution)/shard_map/ppermute | solution.py:271
  80.4 15.9 %all-to-all-done.2 = bf16[8,40,896]{2,1,0:T(8,128)(2,1)S(1)} async-done(((bf16[8,40,896]{2,1,0:T(8,128)(2,1)}), bf16[8,40,896]{2,1,0:T(8,128)(2,1)S(1)}, u32[]{:S(2)}, u32[]{:S(2)}) %all-to-all-start.2) | async-done | bytes 573472 | tf_op jit(solution)/shard_map/rsa/all_to_all | solution.py:277
  96.4 17.6 %all-gather.1 = bf16[256,896]{1,0:T(8,128)(2,1)} all-gather(bf16[16,896]{1,0:T(8,128)(2,1)S(1)} %slice.13), channel_id=3, replica_groups=mesh['seq'=48,'y'=8,'core'=2] {'y','core'}, dimensions={0}, use_global_device_ids=true | all-gather | bytes 487424 | tf_op jit(solution)/shard_map/agt2/all_gather | solution.py:342
  114.1 18.9 %all-gather = bf16[384,896]{1,0:T(8,128)(2,1)} all-gather(bf16[24,896]{1,0:T(8,128)(2,1)S(1)} %slice.12), channel_id=2, replica_groups=mesh['seq'=48,'y'=8,'core'=2] {'y','core'}, dimensions={0}, use_global_device_ids=true | all-gather | bytes 731136 | tf_op jit(solution)/shard_map/agt1/all_gather | solution.py:340
  133.8 8.7 %backward.1 = (bf16[160,3584]{1,0:T(8,128)(2,1)}, f32[160,3584]{1,0:T(8,128)}, bf16[8,280,128]{2,1,0:T(8,128)(2,1)}, bf16[8,280,128]{2,1,0:T(8,128)(2,1)}) custom-call(s32[1]{0:T(128)} %bitcast.core_ref, s32[1]{0:T(128)S(6)} %copy.14.count_ref, bf16[8,40,896]{2,1,0:T(8,128)(2,1)} %copy-done, bf16[8,40,896]{2,1,0:T(8,128)(2,1)} %copy-done.3, ...), custom_call_target="tpu_custom_call" | custom-call | tf_op jit(solution)/shard_map/backward/pallas_call | solution.py:355
  142.5 2.1 %collective-permute-start.4 = (bf16[8,280,128]{2,1,0:T(8,128)(2,1)}, bf16[8,280,128]{2,1,0:T(8,128)(2,1)S(1)}, u32[]{:S(2)}, u32[]{:S(2)}) collective-permute-start(bf16[8,280,128]{2,1,0:T(8,128)(2,1)} %get-tuple-element.22), channel_id=1, source_target_pairs={{0,1},{1,0},{2,3},{3,2},{4,5},{5,4},{6,7},{7,6},{8,9},{9,8},{10,11... | collective-permute-start | bytes 1720328 | tf_op jit(solution)/shard_map/rsd/ppermute | solution.py:271
  144.6 2.0 %collective-permute-done.4 = bf16[8,280,128]{2,1,0:T(8,128)(2,1)S(1)} collective-permute-done((bf16[8,280,128]{2,1,0:T(8,128)(2,1)}, bf16[8,280,128]{2,1,0:T(8,128)(2,1)S(1)}, u32[]{:S(2)}, u32[]{:S(2)}) %collective-permute-start.4) | collective-permute-done | bytes 573472 | tf_op jit(solution)/shard_map/rsd/ppermute | solution.py:271
  146.6 2.0 %add_convert_fusion = bf16[8,280,128]{2,1,0:T(8,128)(2,1)} fusion(bf16[8,280,128]{2,1,0:T(8,128)(2,1)S(1)} %collective-permute-done.4, bf16[8,280,128]{2,1,0:T(8,128)(2,1)} %get-tuple-element.21), kind=kLoop, calls=%fused_computation | loop fusion | flops 1146880 | bytes 1720320 | tf_op jit(solution)/shard_map/rsd/convert_element_type | solution.py:276
  148.6 3.5 %all-to-all-start.3 = ((bf16[8,280,128]{2,1,0:T(8,128)(2,1)}), bf16[8,280,128]{2,1,0:T(8,128)(2,1)S(1)}, u32[]{:S(2)}, u32[]{:S(2)}) async-start(bf16[8,280,128]{2,1,0:T(8,128)(2,1)} %add_convert_fusion), calls=%async_computation.3 | async-start | bytes 1146880 | tf_op jit(solution)/shard_map/rsd/all_to_all | solution.py:277
  152.2 1.6 constant_dynamic-slice_fusion.1.x_ref
  153.8 1.7 constant_dynamic-slice_fusion.dy_ref
  155.5 15.7 %all-to-all-done.3.got_ref = bf16[8,280,128]{2,1,0:T(8,128)(2,1)S(1)} async-done(((bf16[8,280,128]{2,1,0:T(8,128)(2,1)}), bf16[8,280,128]{2,1,0:T(8,128)(2,1)S(1)}, u32[]{:S(2)}, u32[]{:S(2)}) %all-to-all-start.3) | async-done | bytes 573472 | tf_op jit(solution)/shard_map/rsd/all_to_all | solution.py:277
  171.2 0.8 copy-done.2
  172.0 2.1 %final.1 = bf16[10,3584]{1,0:T(8,128)(2,1)} custom-call(bf16[8,280,128]{2,1,0:T(8,128)(2,1)} %copy-done.2, bf16[10,3584]{1,0:T(8,128)(2,1)} %constant_dynamic-slice_fusion.1.x_ref, f32[10,3584]{1,0:T(8,128)} %constant_dynamic-slice_fusion.dy_ref, f32[1,3584]{1,0:T(1,128)} %reshape.14.gain_ref), custom_call_target="tpu_custom_call" | custom-call | tf_op jit(solution)/shard_map/final/pallas_call | solution.py:390
  (18 shorter events, 2.6 us)
Async XLA Ops:
  9.7 14.2 %collective-permute-start = (bf16[8,40,896]{2,1,0:T(8,128)(2,1)}, bf16[8,40,896]{2,1,0:T(8,128)(2,1)S(1)}, u32[]{:S(2)}, u32[]{:S(2)}) collective-permute-start(bf16[8,40,896]{2,1,0:T(8,128)(2,1)} %get-tuple-element.14), channel_id=1, source_target_pairs={{0,1},{1,0},{2,3},{3,2},{4,5},{5,4},{6,7},{7,6},{8,9},{9,8},{10,11... | collective-permute-start | bytes 1720328 | tf_op jit(solution)/shard_map/rsb/ppermute | solution.py:271
  23.9 5.6 %copy-start.4 = (bf16[128,256]{1,0:T(8,128)(2,1)S(1)}, bf16[128,256]{1,0:T(8,128)(2,1)}, u32[]{:S(2)}) copy-start(bf16[128,256]{1,0:T(8,128)(2,1)} %param.10) | copy-start | bytes 196612
  26.0 22.5 %all-to-all-start = ((bf16[8,40,896]{2,1,0:T(8,128)(2,1)}), bf16[8,40,896]{2,1,0:T(8,128)(2,1)S(1)}, u32[]{:S(2)}, u32[]{:S(2)}) async-start(bf16[8,40,896]{2,1,0:T(8,128)(2,1)} %add_convert_fusion.2), calls=%async_computation | async-start | bytes 1146880 | tf_op jit(solution)/shard_map/rsb/all_to_all | solution.py:277
  29.5 25.3 %collective-permute-start.2 = (bf16[32,256]{1,0:T(8,128)(2,1)S(1)}, bf16[32,256]{1,0:T(8,128)(2,1)S(1)}, u32[]{:S(2)}, u32[]{:S(2)}) collective-permute-start(bf16[32,256]{1,0:T(8,128)(2,1)S(1)} %slice.9), channel_id=1, source_target_pairs={{0,16},{16,32},{32,48},{48,64},{64,80},{80,96},{96,112},{112,128},... | collective-permute-start | bytes 49160 | tf_op jit(solution)/shard_map/shift/ppermute | solution.py:267
  48.5 0.8 copy-start.1
  51.3 22.5 %all-to-all-start.1 = ((bf16[8,40,896]{2,1,0:T(8,128)(2,1)}), bf16[8,40,896]{2,1,0:T(8,128)(2,1)S(1)}, u32[]{:S(2)}, u32[]{:S(2)}) async-start(bf16[8,40,896]{2,1,0:T(8,128)(2,1)} %total.1), calls=%async_computation.1 | async-start | bytes 1146880 | tf_op jit(solution)/shard_map/agy/all_to_all | solution.py:352
  58.6 4.2 %collective-permute-start.3 = (bf16[8,40,896]{2,1,0:T(8,128)(2,1)}, bf16[8,40,896]{2,1,0:T(8,128)(2,1)S(1)}, u32[]{:S(2)}, u32[]{:S(2)}) collective-permute-start(bf16[8,40,896]{2,1,0:T(8,128)(2,1)} %get-tuple-element.16), channel_id=1, source_target_pairs={{0,1},{1,0},{2,3},{3,2},{4,5},{5,4},{6,7},{7,6},{8,9},{9,8},{10,11... | collective-permute-start | bytes 1720328 | tf_op jit(solution)/shard_map/rsa/ppermute | solution.py:271
  73.8 40.3 %copy-start = (bf16[8,40,896]{2,1,0:T(8,128)(2,1)}, bf16[8,40,896]{2,1,0:T(8,128)(2,1)S(1)}, u32[]{:S(2)}) copy-start(bf16[8,40,896]{2,1,0:T(8,128)(2,1)S(1)} %all-to-all-done.1.own_ref) | copy-start | bytes 1720324
  73.8 22.5 %all-to-all-start.2 = ((bf16[8,40,896]{2,1,0:T(8,128)(2,1)}), bf16[8,40,896]{2,1,0:T(8,128)(2,1)S(1)}, u32[]{:S(2)}, u32[]{:S(2)}) async-start(bf16[8,40,896]{2,1,0:T(8,128)(2,1)} %add_convert_fusion.1), calls=%async_computation.2 | async-start | bytes 1146880 | tf_op jit(solution)/shard_map/rsa/all_to_all | solution.py:277
  77.3 55.6 %collective-permute-start.1 = (bf16[8,40,896]{2,1,0:T(8,128)(2,1)S(1)}, bf16[8,40,896]{2,1,0:T(8,128)(2,1)S(1)}, u32[]{:S(2)}, u32[]{:S(2)}) collective-permute-start(bf16[8,40,896]{2,1,0:T(8,128)(2,1)S(1)} %all-to-all-done.1.own_ref), channel_id=1, source_target_pairs={{0,1},{1,0},{2,3},{3,2},{4,5},{5,4},{6,7},{7,6},{8,9},{9,8},{10,11... | collective-permute-start | bytes 1720328 | tf_op jit(solution)/shard_map/ppermute | solution.py:271
  132.9 0.8 copy-start.3
  142.5 4.1 %collective-permute-start.4 = (bf16[8,280,128]{2,1,0:T(8,128)(2,1)}, bf16[8,280,128]{2,1,0:T(8,128)(2,1)S(1)}, u32[]{:S(2)}, u32[]{:S(2)}) collective-permute-start(bf16[8,280,128]{2,1,0:T(8,128)(2,1)} %get-tuple-element.22), channel_id=1, source_target_pairs={{0,1},{1,0},{2,3},{3,2},{4,5},{5,4},{6,7},{7,6},{8,9},{9,8},{10,11... | collective-permute-start | bytes 1720328 | tf_op jit(solution)/shard_map/rsd/ppermute | solution.py:271
  148.6 22.5 %all-to-all-start.3 = ((bf16[8,280,128]{2,1,0:T(8,128)(2,1)}), bf16[8,280,128]{2,1,0:T(8,128)(2,1)S(1)}, u32[]{:S(2)}, u32[]{:S(2)}) async-start(bf16[8,280,128]{2,1,0:T(8,128)(2,1)} %add_convert_fusion), calls=%async_computation.3 | async-start | bytes 1146880 | tf_op jit(solution)/shard_map/rsd/all_to_all | solution.py:277
  171.2 0.8 copy-start.2

commit v3 on v2

v3 whole, which is shorter than its diff:
```python
import math

import jax
import jax.numpy as jnp
from jax import lax
from jax.experimental import pallas as pl
from jax.experimental.pallas import tpu as pltpu
from jax.sharding import Mesh
from jax.sharding import PartitionSpec as P

HD = 128
QPK = 2
PAIR = [(0, 1), (1, 0)]
COLS = 4
TP = ("y", "core")

epsilon = 1e-06

VMEM = pl.BlockSpec(memory_space=pltpu.VMEM)
SMEM = pl.BlockSpec(memory_space=pltpu.SMEM)
HBM = pl.BlockSpec(memory_space=pltpu.HBM)
F32 = jnp.float32
BF16 = jnp.bfloat16


def near(array):
    return pltpu.with_memory_space_constraint(array, pltpu.VMEM)


def shape(dims, dtype):
    return jax.ShapeDtypeStruct(dims, dtype)


def nt(a, b):
    return lax.dot_general(a, b, (((1,), (1,)), ((), ())), preferred_element_type=F32)


def tn(a, b):
    return lax.dot_general(a, b, (((0,), (0,)), ((), ())), preferred_element_type=F32)


def nn(a, b):
    return jnp.dot(a, b, preferred_element_type=F32)


def emit_blocks(core, lhs_ref, weight_ref, mine_ref, send_ref, loads=()):
    half = lhs_ref.shape[0] // 2
    high, wide = mine_ref.shape[1:]
    first = lhs_ref[pl.ds(pl.multiple_of(core * half, 16), half), :]
    second = lhs_ref[pl.ds(pl.multiple_of((1 - core) * half, 16), half), :]
    lhs = jnp.concatenate([first, second], axis=0)
    for j in range(COLS):
        if loads:
            loads[j].wait()
        out = nn(lhs, weight_ref[:, j * wide : (j + 1) * wide])
        for i in range(2):
            mine_ref[i * COLS + j] = out[i * high : (i + 1) * high].astype(BF16)
            send_ref[i * COLS + j] = out[half + i * high : half + (i + 1) * high].astype(BF16)


def goal_kernel(core_ref, rows_ref, weight_hbm, mine_ref, send_ref, weight_ref, sems):
    wide = mine_ref.shape[2]
    loads = []
    for j in range(COLS):
        span = slice(j * wide, (j + 1) * wide)
        load = pltpu.make_async_copy(weight_hbm.at[:, span], weight_ref.at[:, span], sems.at[j])
        load.start()
        loads.append(load)
    emit_blocks(core_ref[0], rows_ref, weight_ref, mine_ref, send_ref, loads)


def pair_kernel(mine_ref, other_ref, out_hbm, sum_ref, sems):
    stores = []
    for n in range(out_hbm.shape[0]):
        sum_ref[n] = (mine_ref[n].astype(F32) + other_ref[n].astype(F32)).astype(BF16)
        stores.append(pltpu.make_async_copy(sum_ref.at[n], out_hbm.at[n], sems.at[n]))
        stores[n].start()
    for store in stores:
        store.wait()


def align_kernel(start_ref, own_ref, earlier_ref, out_ref):
    slots = out_ref.shape[0]
    wide = own_ref.shape[2]
    row = lax.broadcasted_iota(jnp.int32, (slots, slots), 0)
    col = lax.broadcasted_iota(jnp.int32, (slots, slots), 1)
    pick = (col == row + start_ref[0]).astype(BF16)
    for j in range(COLS):
        bands = [earlier_ref[j]]
        for c in range(2):
            for i in range(2):
                bands.append(own_ref[2 * (i * COLS + j) + c])
        rows = jnp.concatenate(bands, axis=0)
        out_ref[:, j * wide : (j + 1) * wide] = nn(pick, rows).astype(BF16)


def direction(y, t, live, width):
    asum = sum(jnp.sum(a * a, axis=1, keepdims=True) for a in y) + epsilon
    bsum = sum(jnp.sum(a * a, axis=1, keepdims=True) for a in t) + epsilon
    dots = sum(jnp.sum(a * b, axis=1, keepdims=True) for a, b in zip(y, t))
    both = lax.rsqrt(asum * bsum)
    factor = -math.sqrt(width) * live
    return factor * both, factor * (dots * both) / asum


def finish_kernel(
    core_ref, first_ref, count_ref, own_ref, other_ref, goal_ref, x_ref, student_ref, dy_ref, x_own_ref
):
    core = core_ref[0]
    slots, width = student_ref.shape
    high, wide = own_ref.shape[1:]
    for c in range(2):
        for i in range(2):
            first = (2 * c + i) * high
            for j in range(COLS):
                n = i * COLS + j
                block = jnp.where(core == c, own_ref[n].astype(F32), other_ref[n].astype(F32))
                student_ref[first : first + high, j * wide : (j + 1) * wide] = block.astype(BF16)
    own_rows = dy_ref.shape[0]
    row = lax.broadcasted_iota(jnp.int32, (16, slots), 0) + first_ref[0]
    col = lax.broadcasted_iota(jnp.int32, (16, slots), 1)
    pick = (col == row).astype(BF16)
    y = nn(pick, student_ref[...])
    t = nn(pick, goal_ref[...])
    x_own_ref[...] = nn(pick, x_ref[...])[:own_rows]
    place = lax.broadcasted_iota(jnp.int32, (16, 1), 0) + first_ref[0]
    t_scale, y_scale = direction([y], [t], (place < count_ref[0]).astype(F32), width)
    dy_ref[...] = (t * t_scale - y * y_scale)[:own_rows]


def forward_kernel(
    core_ref,
    x_ref,
    gain_ref,
    starts_ref,
    w_query_hbm,
    w_keyval_hbm,
    w_out_hbm,
    query_ref,
    keyval_ref,
    probs_ref,
    mine_ref,
    send_ref,
    w_query,
    w_keyval,
    w_out,
    attn_ref,
    sems,
):
    loads = [
        pltpu.make_async_copy(source, target, sems.at[n])
        for n, (source, target) in enumerate(
            ((w_query_hbm, w_query), (w_keyval_hbm, w_keyval), (w_out_hbm, w_out))
        )
    ]
    for load in loads:
        load.start()
    slots = x_ref.shape[0]
    xf = x_ref[...].astype(F32)
    inv = lax.rsqrt(jnp.mean(xf * xf, axis=1, keepdims=True) + epsilon)
    normed = (xf * inv * gain_ref[...].reshape(1, xf.shape[1])).astype(BF16)
    loads[0].wait()
    query = nn(normed, w_query[...]).astype(BF16)
    query_ref[...] = query
    loads[1].wait()
    keyval = nn(normed, w_keyval[...]).astype(BF16)
    keyval_ref[...] = keyval
    keys = keyval[:, :HD]
    values = keyval[:, HD:]
    row = lax.broadcasted_iota(jnp.int32, (slots, slots), 0)
    col = lax.broadcasted_iota(jnp.int32, (slots, slots), 1)
    across = jnp.where(row == col, starts_ref[...].reshape(1, slots), 0).astype(F32)
    starts = jnp.sum(across, axis=1, keepdims=True).astype(jnp.int32)
    allowed = (col >= starts) & (col <= row)
    for e in range(QPK):
        scores = nt(query[:, e * HD : (e + 1) * HD], keys) * (1.0 / math.sqrt(HD))
        scores = jnp.where(allowed, scores, -jnp.inf)
        expo = jnp.exp(scores - jnp.max(scores, axis=1, keepdims=True))
        probs = expo / jnp.sum(expo, axis=1, keepdims=True)
        probs_ref[e] = probs
        attn_ref[:, e * HD : (e + 1) * HD] = nn(probs.astype(BF16), values).astype(BF16)
    loads[2].wait()
    emit_blocks(core_ref[0], attn_ref, w_out, mine_ref, send_ref)


def total_kernel(got_ref, x_ref, out_hbm, sum_ref, sems):
    branch = got_ref[0].astype(F32)
    for n in range(1, got_ref.shape[0]):
        branch = branch + got_ref[n].astype(F32)
    sum_ref[...] = (x_ref[...].astype(F32) + branch).astype(BF16)
    stores = []
    for n in range(out_hbm.shape[0]):
        stores.append(pltpu.make_async_copy(sum_ref, out_hbm.at[n], sems.at[n]))
        stores[n].start()
    for store in stores:
        store.wait()


def backward_kernel(
    core_ref,
    count_ref,
    own_ref,
    other_ref,
    goal_ref,
    w_out_hbm,
    probs_hbm,
    keyval_hbm,
    query_hbm,
    w_query_hbm,
    w_keyval_hbm,
    mine_ref,
    send_ref,
    w_out,
    probs_ref,
    keyval_ref,
    query_ref,
    w_query,
    w_keyval,
    dyb_ref,
    grads_ref,
    sems,
):
    loads = [
        pltpu.make_async_copy(source, target, sems.at[n])
        for n, (source, target) in enumerate(
            (
                (w_out_hbm, w_out),
                (probs_hbm, probs_ref),
                (keyval_hbm, keyval_ref),
                (query_hbm, query_ref),
                (w_query_hbm, w_query),
                (w_keyval_hbm, w_keyval),
            )
        )
    ]
    for load in loads:
        load.start()
    core = core_ref[0]
    count = count_ref[0]
    slots, width = goal_ref.shape
    high, wide = own_ref.shape[1:]
    for c in range(2):
        for i in range(2):
            first = (2 * c + i) * high
            y, t = [], []
            for j in range(COLS):
                n = i * COLS + j
                y.append(jnp.where(core == c, own_ref[n].astype(F32), other_ref[n].astype(F32)))
                t.append(goal_ref[first : first + high, j * wide : (j + 1) * wide].astype(F32))
            place = lax.broadcasted_iota(jnp.int32, (high, 1), 0) + first
            t_scale, y_scale = direction(y, t, (place < count).astype(F32), width)
            for j in range(COLS):
                dy = t[j] * t_scale - y[j] * y_scale
                dyb_ref[first : first + high, j * wide : (j + 1) * wide] = dy.astype(BF16)
    loads[0].wait()
    d_attn = nt(dyb_ref[...], w_out[...]).astype(BF16)
    for load in loads[1:4]:
        load.wait()
    keys = keyval_ref[:, :HD]
    values = keyval_ref[:, HD:]
    d_keys = d_values = None
    for e in range(QPK):
        head = slice(e * HD, (e + 1) * HD)
        d_out = d_attn[:, head]
        probs = probs_ref[e]
        d_value = tn(probs.astype(BF16), d_out)
        dprob = nt(d_out, values)
        dscore = probs * (dprob - jnp.sum(dprob * probs, axis=1, keepdims=True))
        dscore = (dscore * (1.0 / math.sqrt(HD))).astype(BF16)
        grads_ref[:, head] = nn(dscore, keys).astype(BF16)
        d_key = tn(dscore, query_ref[:, head])
        d_keys = d_key if d_keys is None else d_keys + d_key
        d_values = d_value if d_values is None else d_values + d_value
    grads_ref[:, QPK * HD : (QPK + 1) * HD] = d_keys.astype(BF16)
    grads_ref[:, (QPK + 1) * HD :] = d_values.astype(BF16)
    half = slots // 2
    row = lax.broadcasted_iota(jnp.int32, (slots, slots), 0)
    col = lax.broadcasted_iota(jnp.int32, (slots, slots), 1)
    sent = (row >= half).astype(jnp.int32)
    place = row - half * sent
    parity = core + sent - 2 * core * sent
    late = (place >= 64).astype(jnp.int32)
    early_row = 20 * (place >> 3) + (place & 7)
    late_row = 20 * ((place - 64) >> 1) + 8 + (place & 1)
    source = early_row + late * (late_row - early_row) + 10 * parity
    pick = (col == source).astype(BF16)
    rows = nn(pick, grads_ref[...]).astype(BF16)
    for load in loads[4:]:
        load.wait()
    sub = lax.broadcasted_iota(jnp.int32, (8, HD), 0) >> 1
    for j in range(width // (4 * HD)):
        span = slice(j * 4 * HD, (j + 1) * 4 * HD)
        part = nt(rows[:, : QPK * HD], w_query[span, :]) + nt(rows[:, QPK * HD :], w_keyval[span, :])
        for h, ref in ((0, mine_ref), (1, send_ref)):
            base = h * half
            for k in range(4):
                lane = slice(k * HD, (k + 1) * HD)
                at = 8 * (4 * j + k)
                for n in range(8):
                    ref[n, at : at + 8, :] = part[base + 8 * n : base + 8 * n + 8, lane].astype(BF16)
            for g in range(2):
                low = base + 64 + 8 * g
                tiles = [part[low : low + 8, k * HD : (k + 1) * HD] for k in range(4)]
                for i in range(4):
                    tile = None
                    for k in range(4):
                        turned = pltpu.roll(tiles[k], (2 * k - 2 * i) % 8, 0) if k != i else tiles[k]
                        tile = turned if tile is None else jnp.where(sub == k, turned, tile)
                    at = 224 + 8 * j
                    ref[4 * g + i, at : at + 8, :] = tile.astype(BF16)


def final_kernel(got_ref, x_ref, dy_ref, gain_ref, out_ref, rows_ref):
    total = got_ref[0].astype(F32)
    for n in range(1, got_ref.shape[0]):
        total = total + got_ref[n].astype(F32)
    for t in range(28):
        lane = slice(t * HD, (t + 1) * HD)
        rows_ref[0:8, lane] = total[8 * t : 8 * t + 8]
        at = 224 + 2 * t
        rows_ref[8:10, lane] = total[at : at + 2]
    x = x_ref[...]
    inv = lax.rsqrt(jnp.mean(x * x, axis=1, keepdims=True) + epsilon)
    upper = rows_ref[0:10, :] * gain_ref[...].reshape(1, x.shape[1])
    dx = inv * upper - x * (inv * inv * inv) * jnp.mean(upper * x, axis=1, keepdims=True)
    out_ref[...] = (dy_ref[...] + dx).astype(BF16)


def from_behind(block, axis, distance):
    devices = range(lax.axis_size(axis))
    route = [(i - distance, i) for i in devices if i - distance in devices]
    return lax.ppermute(block, axis, route)


def swap(block):
    return lax.ppermute(block, "core", PAIR)


def call(kernel, outs, scratch, *args, far=0, place=VMEM):
    specs = [SMEM if a.shape == (1,) else VMEM for a in args]
    specs[len(args) - far :] = [HBM] * far
    return pl.pallas_call(
        kernel,
        out_shape=outs,
        in_specs=specs,
        out_specs=jax.tree.map(lambda _: place, outs),
        scratch_shapes=scratch,
    )(*args)


def spread(mine, send):
    out = shape(mine.shape, BF16)
    scratch = [pltpu.VMEM(out.shape, BF16), pltpu.SemaphoreType.DMA((8,))]
    chip = call(pair_kernel, out, scratch, mine, near(swap(send)), place=HBM)
    return lax.all_to_all(chip, "y", 0, 0)


def body(
    teacher_hidden,
    proj_weight,
    student_in,
    norm_gain,
    w_query,
    w_keyval,
    w_out,
    row_offsets,
    row_counts,
    doc_start,
):
    tokens_here = teacher_hidden.shape[0]
    quarter = tokens_here // 4
    slots, width = student_in.shape
    high, wide = slots // 4, width // COLS
    core = lax.axis_index("core")
    ypos = lax.axis_index("y")
    core_s = core.astype(jnp.int32).reshape(1)
    start = row_offsets - lax.axis_index("seq") * tokens_here + quarter
    blocks = shape((8, high, wide), BF16)
    parts = shape((8, quarter, wide), BF16)
    goal_mine, goal_send = call(
        goal_kernel,
        (parts, parts),
        [pltpu.VMEM(proj_weight.shape, BF16), pltpu.SemaphoreType.DMA((COLS,))],
        core_s,
        teacher_hidden,
        proj_weight,
        far=1,
    )
    goal_got = spread(goal_mine, goal_send)
    query, keyval, probs, mine, send = pl.pallas_call(
        forward_kernel,
        out_shape=(
            shape((slots, QPK * HD), BF16),
            shape((slots, 2 * HD), BF16),
            shape((QPK, slots, slots), F32),
            blocks,
            blocks,
        ),
        in_specs=[SMEM, VMEM, VMEM, VMEM, HBM, HBM, HBM],
        out_specs=(VMEM,) * 5,
        scratch_shapes=[
            pltpu.VMEM(w_query.shape, BF16),
            pltpu.VMEM(w_keyval.shape, BF16),
            pltpu.VMEM(w_out.shape, BF16),
            pltpu.VMEM((slots, QPK * HD), BF16),
            pltpu.SemaphoreType.DMA((3,)),
        ],
        name="forward",
    )(core_s, student_in, norm_gain, doc_start, w_query, w_keyval, w_out)
    branch_got = spread(mine, send)
    goal_own = jnp.sum(goal_got.astype(F32), axis=0).astype(BF16)
    goal_rows = lax.all_gather(goal_own, TP)
    earlier = goal_rows.reshape(2, COLS, 2, quarter, wide)[1, :, 1]
    earlier = from_behind(earlier, "seq", 1)
    goal = call(align_kernel, shape((slots, width), BF16), (), start, goal_rows, earlier)
    x_block = lax.dynamic_slice(
        student_in,
        (core * (slots // 2) + (ypos // COLS) * high, (ypos % COLS) * wide),
        (high, wide),
    )
    y_own = call(
        total_kernel,
        blocks,
        [pltpu.VMEM((high, wide), BF16), pltpu.SemaphoreType.DMA((8,))],
        near(branch_got),
        x_block,
        place=HBM,
    )
    y_half = lax.all_to_all(y_own, "y", 0, 0)
    y_other = swap(y_half)
    pieces = shape((8, slots // 16 * (width // HD), HD), BF16)
    saved = (w_out, probs, keyval, query, w_query, w_keyval)
    mine, send = call(
        backward_kernel,
        (pieces, pieces),
        [pltpu.VMEM(a.shape, a.dtype) for a in saved]
        + [
            pltpu.VMEM((slots, width), BF16),
            pltpu.VMEM((slots, (QPK + 2) * HD), BF16),
            pltpu.SemaphoreType.DMA((len(saved),)),
        ],
        core_s,
        row_counts,
        near(y_half),
        near(y_other),
        goal,
        *saved,
        far=len(saved),
    )
    got = spread(mine, send)
    own_rows = slots // 16
    first_row = ((ypos * 2 + core) * own_rows).astype(jnp.int32).reshape(1)
    rows = shape((own_rows, width), F32)
    student_out, dy_own, x_own = call(
        finish_kernel,
        (shape((slots, width), BF16), rows, rows),
        (),
        core_s,
        first_row,
        row_counts,
        y_half,
        y_other,
        goal,
        student_in,
    )
    grad_in = call(
        final_kernel,
        shape((own_rows, width), BF16),
        [pltpu.VMEM((16, width), F32)],
        near(got),
        x_own,
        dy_own,
        norm_gain,
    )
    return (student_out, grad_in)


def solution(mesh):
    seqs, tps = mesh.devices.shape
    split = Mesh(mesh.devices.reshape(seqs, tps // 2, 2), ("seq",) + TP)
    in_specs = (
        P("seq", TP),
        P(TP, None),
        P("seq", None),
        P(),
        P(None, TP),
        P(None, TP),
        P(TP, None),
        P("seq"),
        P("seq"),
        P("seq"),
    )
    out_specs = (P("seq", None), P(("seq",) + TP, None))
    return jax.shard_map(body, mesh=split, in_specs=in_specs, out_specs=out_specs, check_vma=False)
```

time: 175 us -> 158 us (0.903)
  blocking collectives: 36.5 us -> 17.2 us
  Pallas kernels: 22.2 us -> 34.5 us
  local copies, waits for them, and re-layouts: 10.1 us -> 2.27 us
  other arithmetic: 6.88 us -> 0.07 us
  waiting for transfers between devices: 61.6 us -> 65.8 us
    all_gather x2 -> x1, blocking collectives: 36.5 us -> 17.2 us  [body(): goal_rows = lax.all_gather(goal_own, TP)]
    pallas_call x4 -> x9, Pallas kernels: 15.8 us -> 28.2 us  [call(): pl.pallas_call(kernel, out_shape=outs, in_specs=specs, out_specs=jax.tree...]
    all_to_all x1, waiting for transfers between devices: 9 us -> 18.9 us  [body(): y_half = lax.all_to_all(y_own, 'y', 0, 0)]
    all_to_all x3, waiting for transfers between devices: 47 us -> 37.9 us  [spread(): return lax.all_to_all(chip, 'y', 0, 0)]
    convert_element_type x3 -> x0, other arithmetic: 6.06 us -> none  [spread(): chip = (mine.astype(F32) + other.astype(F32)).astype(BF16)]
    ppermute x1, waiting for transfers between devices: 0.01 us -> 3.75 us  [from_behind(): return lax.ppermute(block, axis, route)]
    dynamic_slice x3 -> x0, local copies, waits for them, and re-layouts: 3.4 us -> none  [the longest x1 1.7 us: body(): dy_own = lax.dynamic_slice_in_dim(dy, first_row, own_rows, 0)]
    reshape x2 -> x0, local copies, waits for them, and re-layouts: 2.75 us -> none  [the longest x1 1.43 us: body(): doc_start.reshape(slots, 1)]
  transfers between devices with their start and end apart: 9 -> 9, of which waited for: 7 -> 8; matrix products, arithmetic and copies ran while one was open for 4% -> 1% of each run, Pallas kernels for 3% -> 9%
where the time goes in v3:
time: 158 us; the launch traced here: 157 us
  waiting for transfers between devices  65.8 us (42%)
  starting transfers between devices  35.1 us (22%)
  Pallas kernels  34.5 us (22%)
  blocking collectives  17.2 us (11%)
  local copies, waits for them, and re-layouts  2.27 us (1%)
  between operations  2.14 us (1%)
    all_to_all x3, waiting for transfers between devices, spread(): return lax.all_to_all(chip, 'y', 0, 0)  37.9 us
    pallas_call x9, Pallas kernels, call(): pl.pallas_call(kernel, out_shape=outs, in_specs=specs, out_specs=jax.tree...  28.2 us
    ppermute x4, starting transfers between devices, swap(): return lax.ppermute(block, 'core', PAIR)  19.7 us
    all_to_all x1, waiting for transfers between devices, body(): y_half = lax.all_to_all(y_own, 'y', 0, 0)  18.9 us
    all_gather x1, blocking collectives, body(): goal_rows = lax.all_gather(goal_own, TP)  17.2 us
    all_to_all x3, starting transfers between devices, spread(): return lax.all_to_all(chip, 'y', 0, 0)  10.6 us
    pallas_call x1, Pallas kernels, body(): pl.pallas_call(forward_kernel, out_shape=(shape((slots, QPK * HD), BF16),...  6.32 us
    ppermute x4, waiting for transfers between devices, swap(): return lax.ppermute(block, 'core', PAIR)  5.23 us
  transfers between devices with their start and end apart: 9, of which 8 were waited for; matrix products, arithmetic and copies ran while one was open for 1% of the time, Pallas kernels for 9%

profile of v3, /device:TPU:1, one launch (start us, length us, event | category | flops | bytes accessed | tf_op | source)
XLA Modules:
  0.0 157.1 jit_solution(9621242680369305102)
XLA Ops:
  0.6 6.3 %forward.1 = (bf16[160,256]{1,0:T(8,128)(2,1)}, bf16[160,256]{1,0:T(8,128)(2,1)}, f32[2,160,160]{2,1,0:T(8,128)}, bf16[8,40,896]{2,1,0:T(8,128)(2,1)}, bf16[8,40,896]{2,1,0:T(8,128)(2,1)}) custom-call(s32[1]{0:T(128)} %bitcast.core_ref, bf16[160,3584]{1,0:T(8,128)(2,1)} %x_ref.3, f32[3584]{0:T(1024)} %gain_ref.3, s32[160]{0:T(256)} %starts_ref.1, ...), custom_call_target="tpu_custom_call" | custom-call | tf_op jit(solution)/shard_map/forward/pallas_call | solution.py:390
  7.0 12.4 %collective-permute-start = (bf16[8,40,896]{2,1,0:T(8,128)(2,1)}, bf16[8,40,896]{2,1,0:T(8,128)(2,1)S(1)}, u32[]{:S(2)}, u32[]{:S(2)}) collective-permute-start(bf16[8,40,896]{2,1,0:T(8,128)(2,1)} %get-tuple-element.15), channel_id=1, source_target_pairs={{0,1},{1,0},{2,3},{3,2},{4,5},{5,4},{6,7},{7,6},{8,9},{9,8},{10,11... | collective-permute-start | bytes 1720328 | tf_op jit(solution)/shard_map/ppermute | solution.py:336
  19.4 1.8 %collective-permute-done.other_ref = bf16[8,40,896]{2,1,0:T(8,128)(2,1)S(1)} collective-permute-done((bf16[8,40,896]{2,1,0:T(8,128)(2,1)}, bf16[8,40,896]{2,1,0:T(8,128)(2,1)S(1)}, u32[]{:S(2)}, u32[]{:S(2)}) %collective-permute-start) | collective-permute-done | bytes 573472 | tf_op jit(solution)/shard_map/ppermute | solution.py:336
  21.2 2.0 %shard_map.113 = bf16[8,40,896]{2,1,0:T(8,128)(2,1)} custom-call(bf16[8,40,896]{2,1,0:T(8,128)(2,1)} %get-tuple-element.14.mine_ref, bf16[8,40,896]{2,1,0:T(8,128)(2,1)S(1)} %collective-permute-done.other_ref), custom_call_target="tpu_custom_call" | custom-call | tf_op jit(solution)/shard_map/pallas_call | solution.py:342
  23.1 3.5 %all-to-all-start = ((bf16[8,40,896]{2,1,0:T(8,128)(2,1)}), bf16[8,40,896]{2,1,0:T(8,128)(2,1)S(1)}, u32[]{:S(2)}, u32[]{:S(2)}) async-start(bf16[8,40,896]{2,1,0:T(8,128)(2,1)} %shard_map.113), calls=%async_computation | async-start | bytes 1146880 | tf_op jit(solution)/shard_map/all_to_all | solution.py:355
  26.7 3.8 %shard_map.115 = (bf16[8,32,896]{2,1,0:T(8,128)(2,1)}, bf16[8,32,896]{2,1,0:T(8,128)(2,1)}) custom-call(s32[1]{0:T(128)} %bitcast.core_ref, bf16[128,256]{1,0:T(8,128)(2,1)} %rows_ref.1, bf16[256,3584]{1,0:T(8,128)(2,1)} %weight_hbm.1), custom_call_target="tpu_custom_call" | custom-call | tf_op jit(solution)/shard_map/pallas_call | solution.py:342
  30.5 2.3 %collective-permute-start.2 = (bf16[8,32,896]{2,1,0:T(8,128)(2,1)}, bf16[8,32,896]{2,1,0:T(8,128)(2,1)S(1)}, u32[]{:S(2)}, u32[]{:S(2)}) collective-permute-start(bf16[8,32,896]{2,1,0:T(8,128)(2,1)} %get-tuple-element.17), channel_id=1, source_target_pairs={{0,1},{1,0},{2,3},{3,2},{4,5},{5,4},{6,7},{7,6},{8,9},{9,8},{10,11... | collective-permute-start | bytes 1376264 | tf_op jit(solution)/shard_map/ppermute | solution.py:336
  32.7 1.6 %collective-permute-done.2.other_ref = bf16[8,32,896]{2,1,0:T(8,128)(2,1)S(1)} collective-permute-done((bf16[8,32,896]{2,1,0:T(8,128)(2,1)}, bf16[8,32,896]{2,1,0:T(8,128)(2,1)S(1)}, u32[]{:S(2)}, u32[]{:S(2)}) %collective-permute-start.2) | collective-permute-done | bytes 458784 | tf_op jit(solution)/shard_map/ppermute | solution.py:336
  34.4 1.9 %shard_map.116 = bf16[8,32,896]{2,1,0:T(8,128)(2,1)} custom-call(bf16[8,32,896]{2,1,0:T(8,128)(2,1)} %get-tuple-element.16.mine_ref, bf16[8,32,896]{2,1,0:T(8,128)(2,1)S(1)} %collective-permute-done.2.other_ref), custom_call_target="tpu_custom_call" | custom-call | tf_op jit(solution)/shard_map/pallas_call | solution.py:342
  36.3 9.4 %all-to-all-done.got_ref = bf16[8,40,896]{2,1,0:T(8,128)(2,1)S(1)} async-done(((bf16[8,40,896]{2,1,0:T(8,128)(2,1)}), bf16[8,40,896]{2,1,0:T(8,128)(2,1)S(1)}, u32[]{:S(2)}, u32[]{:S(2)}) %all-to-all-start) | async-done | bytes 573472 | tf_op jit(solution)/shard_map/all_to_all | solution.py:355
  45.7 3.5 %all-to-all-start.2 = ((bf16[8,32,896]{2,1,0:T(8,128)(2,1)}), bf16[8,32,896]{2,1,0:T(8,128)(2,1)S(1)}, u32[]{:S(2)}, u32[]{:S(2)}) async-start(bf16[8,32,896]{2,1,0:T(8,128)(2,1)} %shard_map.116), calls=%async_computation.2 | async-start | bytes 917504 | tf_op jit(solution)/shard_map/all_to_all | solution.py:355
  49.2 1.5 dynamic_slice.3.x_ref
  50.7 1.8 %shard_map.114 = bf16[8,40,896]{2,1,0:T(8,128)(2,1)} custom-call(bf16[8,40,896]{2,1,0:T(8,128)(2,1)S(1)} %all-to-all-done.got_ref, bf16[40,896]{1,0:T(8,128)(2,1)} %dynamic_slice.3.x_ref), custom_call_target="tpu_custom_call" | custom-call | tf_op jit(solution)/shard_map/pallas_call | solution.py:342
  52.6 13.0 %all-to-all-done.2 = bf16[8,32,896]{2,1,0:T(8,128)(2,1)S(1)} async-done(((bf16[8,32,896]{2,1,0:T(8,128)(2,1)}), bf16[8,32,896]{2,1,0:T(8,128)(2,1)S(1)}, u32[]{:S(2)}, u32[]{:S(2)}) %all-to-all-start.2) | async-done | bytes 458784 | tf_op jit(solution)/shard_map/all_to_all | solution.py:355
  65.6 3.5 %all-to-all-start.1 = ((bf16[8,40,896]{2,1,0:T(8,128)(2,1)}), bf16[8,40,896]{2,1,0:T(8,128)(2,1)S(1)}, u32[]{:S(2)}, u32[]{:S(2)}) async-start(bf16[8,40,896]{2,1,0:T(8,128)(2,1)} %shard_map.114), calls=%async_computation.1 | async-start | bytes 1146880 | tf_op jit(solution)/shard_map/all_to_all | solution.py:429
  69.2 0.1 reduce_sum.12
  69.2 18.9 %all-to-all-done.1.own_ref = bf16[8,40,896]{2,1,0:T(8,128)(2,1)S(1)} async-done(((bf16[8,40,896]{2,1,0:T(8,128)(2,1)}), bf16[8,40,896]{2,1,0:T(8,128)(2,1)S(1)}, u32[]{:S(2)}, u32[]{:S(2)}) %all-to-all-start.1) | async-done | bytes 573472 | tf_op jit(solution)/shard_map/all_to_all | solution.py:429
  88.1 2.4 %collective-permute-start.1 = (bf16[8,40,896]{2,1,0:T(8,128)(2,1)S(1)}, bf16[8,40,896]{2,1,0:T(8,128)(2,1)S(1)}, u32[]{:S(2)}, u32[]{:S(2)}) collective-permute-start(bf16[8,40,896]{2,1,0:T(8,128)(2,1)S(1)} %all-to-all-done.1.own_ref), channel_id=1, source_target_pairs={{0,1},{1,0},{2,3},{3,2},{4,5},{5,4},{6,7},{7,6},{8,9},{9,8},{10,11... | collective-permute-start | bytes 1720328 | tf_op jit(solution)/shard_map/ppermute | solution.py:336
  90.5 17.2 %all-gather = bf16[512,896]{1,0:T(8,128)(2,1)S(1)} all-gather(bf16[32,896]{1,0:T(8,128)(2,1)S(1)} %reduce_sum.12), channel_id=2, replica_groups=mesh['seq'=48,'y'=8,'core'=2] {'y','core'}, dimensions={0}, use_global_device_ids=true | all-gather | bytes 974848 | tf_op jit(solution)/shard_map/all_gather | solution.py:412
  107.7 1.3 collective-permute-start.3
  110.3 3.7 %collective-permute-done.3.earlier_ref = bf16[4,32,896]{2,1,0:T(8,128)(2,1)S(1)} collective-permute-done((bf16[4,32,896]{2,1,0:T(8,128)(2,1)S(1)}, bf16[4,32,896]{2,1,0:T(8,128)(2,1)S(1)}, u32[]{:S(2)}, u32[]{:S(2)}) %collective-permute-start.3) | collective-permute-done | bytes 229408 | tf_op jit(solution)/shard_map/ppermute | solution.py:332
  114.1 0.7 copy-done.3
  114.8 2.7 %shard_map.117.goal_ref = bf16[160,3584]{1,0:T(8,128)(2,1)} custom-call(s32[1]{0:T(128)S(6)} %add.25.start_ref, bf16[16,32,896]{2,1,0:T(8,128)(2,1)} %bitcast.10, bf16[4,32,896]{2,1,0:T(8,128)(2,1)} %copy-done.3), custom_call_target="tpu_custom_call" | custom-call | tf_op jit(solution)/shard_map/pallas_call | solution.py:342
  117.5 0.0 collective-permute-done.1.other_ref
  117.5 8.6 %shard_map.119 = (bf16[8,280,128]{2,1,0:T(8,128)(2,1)}, bf16[8,280,128]{2,1,0:T(8,128)(2,1)}) custom-call(s32[1]{0:T(128)} %bitcast.core_ref, s32[1]{0:T(128)S(6)} %copy.15.count_ref, bf16[8,40,896]{2,1,0:T(8,128)(2,1)S(1)} %all-to-all-done.1.own_ref, bf16[8,40,896]{2,1,0:T(8,128)(2,1)S(1)} %collective-permute-done.1.other_ref, ...), custom_call_target="tpu_custom_call" | custom-call | tf_op jit(solution)/shard_map/pallas_call | solution.py:342
  126.2 2.6 %collective-permute-start.4 = (bf16[8,280,128]{2,1,0:T(8,128)(2,1)}, bf16[8,280,128]{2,1,0:T(8,128)(2,1)S(1)}, u32[]{:S(2)}, u32[]{:S(2)}) collective-permute-start(bf16[8,280,128]{2,1,0:T(8,128)(2,1)} %get-tuple-element.23), channel_id=1, source_target_pairs={{0,1},{1,0},{2,3},{3,2},{4,5},{5,4},{6,7},{7,6},{8,9},{9,8},{10,11... | collective-permute-start | bytes 1720328 | tf_op jit(solution)/shard_map/ppermute | solution.py:336
  128.8 1.8 %collective-permute-done.4.other_ref = bf16[8,280,128]{2,1,0:T(8,128)(2,1)S(1)} collective-permute-done((bf16[8,280,128]{2,1,0:T(8,128)(2,1)}, bf16[8,280,128]{2,1,0:T(8,128)(2,1)S(1)}, u32[]{:S(2)}, u32[]{:S(2)}) %collective-permute-start.4) | collective-permute-done | bytes 573472 | tf_op jit(solution)/shard_map/ppermute | solution.py:336
  130.6 2.0 %shard_map.120 = bf16[8,280,128]{2,1,0:T(8,128)(2,1)} custom-call(bf16[8,280,128]{2,1,0:T(8,128)(2,1)} %get-tuple-element.22.mine_ref, bf16[8,280,128]{2,1,0:T(8,128)(2,1)S(1)} %collective-permute-done.4.other_ref), custom_call_target="tpu_custom_call" | custom-call | tf_op jit(solution)/shard_map/pallas_call | solution.py:342
  132.6 3.5 %all-to-all-start.3 = ((bf16[8,280,128]{2,1,0:T(8,128)(2,1)}), bf16[8,280,128]{2,1,0:T(8,128)(2,1)S(1)}, u32[]{:S(2)}, u32[]{:S(2)}) async-start(bf16[8,280,128]{2,1,0:T(8,128)(2,1)} %shard_map.120), calls=%async_computation.3 | async-start | bytes 1146880 | tf_op jit(solution)/shard_map/all_to_all | solution.py:355
  136.2 3.5 %shard_map.118 = (bf16[160,3584]{1,0:T(8,128)(2,1)}, f32[10,3584]{1,0:T(8,128)}, f32[10,3584]{1,0:T(8,128)}) custom-call(s32[1]{0:T(128)} %bitcast.core_ref, s32[1]{0:T(128)} %bitcast.1.first_ref, s32[1]{0:T(128)S(6)} %copy.15.count_ref, bf16[8,40,896]{2,1,0:T(8,128)(2,1)} %copy-done, bf16[8,40,896]{2,1,0:T(8,128)(2,1)} %copy-done.1, ...), custom_call_target="tpu_custom_call" | custom-call | tf_op jit(solution)/shard_map/pallas_call | solution.py:342
  139.6 15.5 %all-to-all-done.3.got_ref = bf16[8,280,128]{2,1,0:T(8,128)(2,1)S(1)} async-done(((bf16[8,280,128]{2,1,0:T(8,128)(2,1)}), bf16[8,280,128]{2,1,0:T(8,128)(2,1)S(1)}, u32[]{:S(2)}, u32[]{:S(2)}) %all-to-all-start.3) | async-done | bytes 573472 | tf_op jit(solution)/shard_map/all_to_all | solution.py:355
  155.1 1.9 %shard_map.121 = bf16[10,3584]{1,0:T(8,128)(2,1)} custom-call(bf16[8,280,128]{2,1,0:T(8,128)(2,1)S(1)} %all-to-all-done.3.got_ref, f32[10,3584]{1,0:T(8,128)} %get-tuple-element.24.x_ref, f32[10,3584]{1,0:T(8,128)} %get-tuple-element.25.dy_ref, f32[3584]{0:T(1024)} %gain_ref.3), custom_call_target="tpu_custom_call" | custom-call | tf_op jit(solution)/shard_map/pallas_call | solution.py:342
  (8 shorter events, 0.0 us)
Async XLA Ops:
  7.0 14.2 %collective-permute-start = (bf16[8,40,896]{2,1,0:T(8,128)(2,1)}, bf16[8,40,896]{2,1,0:T(8,128)(2,1)S(1)}, u32[]{:S(2)}, u32[]{:S(2)}) collective-permute-start(bf16[8,40,896]{2,1,0:T(8,128)(2,1)} %get-tuple-element.15), channel_id=1, source_target_pairs={{0,1},{1,0},{2,3},{3,2},{4,5},{5,4},{6,7},{7,6},{8,9},{9,8},{10,11... | collective-permute-start | bytes 1720328 | tf_op jit(solution)/shard_map/ppermute | solution.py:336
  23.1 22.5 %all-to-all-start = ((bf16[8,40,896]{2,1,0:T(8,128)(2,1)}), bf16[8,40,896]{2,1,0:T(8,128)(2,1)S(1)}, u32[]{:S(2)}, u32[]{:S(2)}) async-start(bf16[8,40,896]{2,1,0:T(8,128)(2,1)} %shard_map.113), calls=%async_computation | async-start | bytes 1146880 | tf_op jit(solution)/shard_map/all_to_all | solution.py:355
  30.5 3.9 %collective-permute-start.2 = (bf16[8,32,896]{2,1,0:T(8,128)(2,1)}, bf16[8,32,896]{2,1,0:T(8,128)(2,1)S(1)}, u32[]{:S(2)}, u32[]{:S(2)}) collective-permute-start(bf16[8,32,896]{2,1,0:T(8,128)(2,1)} %get-tuple-element.17), channel_id=1, source_target_pairs={{0,1},{1,0},{2,3},{3,2},{4,5},{5,4},{6,7},{7,6},{8,9},{9,8},{10,11... | collective-permute-start | bytes 1376264 | tf_op jit(solution)/shard_map/ppermute | solution.py:336
  45.7 19.9 %all-to-all-start.2 = ((bf16[8,32,896]{2,1,0:T(8,128)(2,1)}), bf16[8,32,896]{2,1,0:T(8,128)(2,1)S(1)}, u32[]{:S(2)}, u32[]{:S(2)}) async-start(bf16[8,32,896]{2,1,0:T(8,128)(2,1)} %shard_map.116), calls=%async_computation.2 | async-start | bytes 917504 | tf_op jit(solution)/shard_map/all_to_all | solution.py:355
  65.6 22.5 %all-to-all-start.1 = ((bf16[8,40,896]{2,1,0:T(8,128)(2,1)}), bf16[8,40,896]{2,1,0:T(8,128)(2,1)S(1)}, u32[]{:S(2)}, u32[]{:S(2)}) async-start(bf16[8,40,896]{2,1,0:T(8,128)(2,1)} %shard_map.114), calls=%async_computation.1 | async-start | bytes 1146880 | tf_op jit(solution)/shard_map/all_to_all | solution.py:429
  88.1 29.4 %copy-start = (bf16[8,40,896]{2,1,0:T(8,128)(2,1)}, bf16[8,40,896]{2,1,0:T(8,128)(2,1)S(1)}, u32[]{:S(2)}) copy-start(bf16[8,40,896]{2,1,0:T(8,128)(2,1)S(1)} %all-to-all-done.1.own_ref) | copy-start | bytes 1720324
  88.1 29.4 %collective-permute-start.1 = (bf16[8,40,896]{2,1,0:T(8,128)(2,1)S(1)}, bf16[8,40,896]{2,1,0:T(8,128)(2,1)S(1)}, u32[]{:S(2)}, u32[]{:S(2)}) collective-permute-start(bf16[8,40,896]{2,1,0:T(8,128)(2,1)S(1)} %all-to-all-done.1.own_ref), channel_id=1, source_target_pairs={{0,1},{1,0},{2,3},{3,2},{4,5},{5,4},{6,7},{7,6},{8,9},{9,8},{10,11... | collective-permute-start | bytes 1720328 | tf_op jit(solution)/shard_map/ppermute | solution.py:336
  107.7 6.4 %copy-start.2 = (bf16[512,896]{1,0:T(8,128)(2,1)}, bf16[512,896]{1,0:T(8,128)(2,1)S(1)}, u32[]{:S(2)}) copy-start(bf16[512,896]{1,0:T(8,128)(2,1)S(1)} %all-gather) | copy-start | bytes 2752516
  107.7 6.4 %collective-permute-start.3 = (bf16[4,32,896]{2,1,0:T(8,128)(2,1)S(1)}, bf16[4,32,896]{2,1,0:T(8,128)(2,1)S(1)}, u32[]{:S(2)}, u32[]{:S(2)}) collective-permute-start(bf16[4,32,896]{2,1,0:T(8,128)(2,1)S(1)} %slice_bitcast_fusion), channel_id=1, source_target_pairs={{0,16},{16,32},{32,48},{48,64},{64,80},{80,96},{96,112},{112,128},... | collective-permute-start | bytes 688136 | tf_op jit(solution)/shard_map/ppermute | solution.py:332
  114.1 0.7 copy-start.3
  117.5 8.7 %copy-start.1 = (bf16[8,40,896]{2,1,0:T(8,128)(2,1)}, bf16[8,40,896]{2,1,0:T(8,128)(2,1)S(1)}, u32[]{:S(2)}) copy-start(bf16[8,40,896]{2,1,0:T(8,128)(2,1)S(1)} %collective-permute-done.1.other_ref) | copy-start | bytes 1720324
  126.2 4.4 %collective-permute-start.4 = (bf16[8,280,128]{2,1,0:T(8,128)(2,1)}, bf16[8,280,128]{2,1,0:T(8,128)(2,1)S(1)}, u32[]{:S(2)}, u32[]{:S(2)}) collective-permute-start(bf16[8,280,128]{2,1,0:T(8,128)(2,1)} %get-tuple-element.23), channel_id=1, source_target_pairs={{0,1},{1,0},{2,3},{3,2},{4,5},{5,4},{6,7},{7,6},{8,9},{9,8},{10,11... | collective-permute-start | bytes 1720328 | tf_op jit(solution)/shard_map/ppermute | solution.py:336
  132.6 22.5 %all-to-all-start.3 = ((bf16[8,280,128]{2,1,0:T(8,128)(2,1)}), bf16[8,280,128]{2,1,0:T(8,128)(2,1)S(1)}, u32[]{:S(2)}, u32[]{:S(2)}) async-start(bf16[8,280,128]{2,1,0:T(8,128)(2,1)} %shard_map.120), calls=%async_computation.3 | async-start | bytes 1146880 | tf_op jit(solution)/shard_map/all_to_all | solution.py:355

commit v4 on v3

--- a/solution.py
+++ b/solution.py
@@ -77,6 +77,23 @@
         stores[n].start()
     for store in stores:
         store.wait()
+
+
+def first_kernel(y_ref, mine_ref, other_ref, up_ref, down_ref, keep_ref):
+    for ref, away in ((up_ref, (1, 4, -2)), (down_ref, (-1, 2)), (keep_ref, (0, 3, -3))):
+        for k, r in enumerate(away):
+            n = (y_ref[0] + (r + 8)) & 7
+            ref[k] = (mine_ref[n].astype(F32) + other_ref[n].astype(F32)).astype(BF16)
+
+
+def second_kernel(keep_ref, below_ref, above_ref, own_ref, plus_ref, minus_ref):
+    def at(ref, k):
+        return ref[k].astype(F32)
+
+    own_ref[...] = at(keep_ref, 0) + at(below_ref, 0) + at(above_ref, 0)
+    plus = at(keep_ref, 1) + at(below_ref, 1) + at(above_ref, 1)
+    plus_ref[...] = plus.astype(BF16)
+    minus_ref[...] = (at(keep_ref, 2) + at(below_ref, 2)).astype(BF16)
 
 
 def align_kernel(start_ref, own_ref, earlier_ref, out_ref):
@@ -336,6 +353,11 @@
     return lax.ppermute(block, "core", PAIR)
 
 
+def turn(block, distance):
+    size = lax.axis_size("y")
+    return lax.ppermute(block, "y", [(i, (i + distance) % size) for i in range(size)])
+
+
 def call(kernel, outs, scratch, *args, far=0, place=VMEM):
     specs = [SMEM if a.shape == (1,) else VMEM for a in args]
     specs[len(args) - far :] = [HBM] * far
@@ -386,7 +408,21 @@
         proj_weight,
         far=1,
     )
-    goal_got = spread(goal_mine, goal_send)
+    some = [shape((n, quarter, wide), BF16) for n in (3, 2, 3)]
+    ypos_s = ypos.astype(jnp.int32).reshape(1)
+    up, down, keep = call(first_kernel, tuple(some), (), ypos_s, goal_mine, near(swap(goal_send)))
+    one = (quarter, wide)
+    own, plus, minus = call(
+        second_kernel,
+        (shape(one, F32), shape(one, BF16), shape(one, BF16)),
+        (),
+        keep,
+        near(turn(up, 1)),
+        near(turn(down, -1)),
+    )
+    plus = turn(plus, 3)
+    minus = turn(minus, -3)
+    goal_own = (own + plus.astype(F32) + minus.astype(F32)).astype(BF16)
     query, keyval, probs, mine, send = pl.pallas_call(
         forward_kernel,
         out_shape=(
@@ -408,7 +444,6 @@
         name="forward",
     )(core_s, student_in, norm_gain, doc_start, w_query, w_keyval, w_out)
     branch_got = spread(mine, send)
-    goal_own = jnp.sum(goal_got.astype(F32), axis=0).astype(BF16)
     goal_rows = lax.all_gather(goal_own, TP)
     earlier = goal_rows.reshape(2, COLS, 2, quarter, wide)[1, :, 1]
     earlier = from_behind(earlier, "seq", 1)

time: 158 us -> 162 us (1.025)
  starting transfers between devices: 35.1 us -> 50.4 us
  waiting for transfers between devices: 65.8 us -> 51.8 us
    all_to_all x1, waiting for transfers between devices: 18.9 us -> 0.01 us  [body(): y_half = lax.all_to_all(y_own, 'y', 0, 0)]
    ppermute x0 -> x4, starting transfers between devices: none -> 15 us  [turn(): lax.ppermute(block, 'y', [(i, (i + distance) % size) for i in range(size)])]
    ppermute x0 -> x4, waiting for transfers between devices: none -> 9.87 us  [turn(): lax.ppermute(block, 'y', [(i, (i + distance) % size) for i in range(size)])]
    all_to_all x3 -> x2, waiting for transfers between devices: 37.9 us -> 33 us  [spread(): return lax.all_to_all(chip, 'y', 0, 0)]
    ppermute x4, starting transfers between devices: 19.7 us -> 22.6 us  [swap(): return lax.ppermute(block, 'core', PAIR)]
    all_to_all x3 -> x2, starting transfers between devices: 10.6 us -> 7.95 us  [spread(): return lax.all_to_all(chip, 'y', 0, 0)]
    pallas_call x9 -> x10, Pallas kernels: 28.2 us -> 29.7 us  [call(): pl.pallas_call(kernel, out_shape=outs, in_specs=specs, out_specs=jax.tree...]
  transfers between devices with their start and end apart: 9 -> 12, of which waited for: 8 -> 10; matrix products, arithmetic and copies ran while one was open for 1% -> 2% of each run, Pallas kernels for 9% -> 8%
where the time goes in v4:
time: 162 us; the launch traced here: 161 us
  waiting for transfers between devices  51.8 us (32%)
  starting transfers between devices  50.4 us (31%)
  Pallas kernels  36.1 us (22%)
  blocking collectives  17 us (10%)
  local copies, waits for them, and re-layouts  2.27 us (1%)
  between operations  2.15 us (1%)
    all_to_all x2, waiting for transfers between devices, spread(): return lax.all_to_all(chip, 'y', 0, 0)  33 us
    pallas_call x10, Pallas kernels, call(): pl.pallas_call(kernel, out_shape=outs, in_specs=specs, out_specs=jax.tree...  29.7 us
    ppermute x4, starting transfers between devices, swap(): return lax.ppermute(block, 'core', PAIR)  22.6 us
    all_gather x1, blocking collectives, body(): goal_rows = lax.all_gather(goal_own, TP)  17 us
    ppermute x4, starting transfers between devices, turn(): lax.ppermute(block, 'y', [(i, (i + distance) % size) for i in range(size)])  15 us
    ppermute x4, waiting for transfers between devices, turn(): lax.ppermute(block, 'y', [(i, (i + distance) % size) for i in range(size)])  9.87 us
    all_to_all x2, starting transfers between devices, spread(): return lax.all_to_all(chip, 'y', 0, 0)  7.95 us
    pallas_call x1, Pallas kernels, body(): pl.pallas_call(forward_kernel, out_shape=(shape((slots, QPK * HD), BF16),...  6.33 us
  transfers between devices with their start and end apart: 12, of which 10 were waited for; matrix products, arithmetic and copies ran while one was open for 2% of the time, Pallas kernels for 8%

profile of v4, /device:TPU:1, one launch (start us, length us, event | category | flops | bytes accessed | tf_op | source)
XLA Modules:
  0.0 160.6 jit_solution(754333692512505070)
XLA Ops:
  0.6 6.3 %forward.1 = (bf16[160,256]{1,0:T(8,128)(2,1)}, bf16[160,256]{1,0:T(8,128)(2,1)}, f32[2,160,160]{2,1,0:T(8,128)}, bf16[8,40,896]{2,1,0:T(8,128)(2,1)}, bf16[8,40,896]{2,1,0:T(8,128)(2,1)}) custom-call(s32[1]{0:T(128)} %bitcast.core_ref, bf16[160,3584]{1,0:T(8,128)(2,1)} %x_ref.3, f32[3584]{0:T(1024)} %gain_ref.3, s32[160]{0:T(256)} %starts_ref.1, ...), custom_call_target="tpu_custom_call" | custom-call | tf_op jit(solution)/shard_map/forward/pallas_call | solution.py:426
  7.0 12.4 %collective-permute-start = (bf16[8,40,896]{2,1,0:T(8,128)(2,1)}, bf16[8,40,896]{2,1,0:T(8,128)(2,1)S(1)}, u32[]{:S(2)}, u32[]{:S(2)}) collective-permute-start(bf16[8,40,896]{2,1,0:T(8,128)(2,1)} %get-tuple-element.21), channel_id=1, source_target_pairs={{0,1},{1,0},{2,3},{3,2},{4,5},{5,4},{6,7},{7,6},{8,9},{9,8},{10,11... | collective-permute-start | bytes 1720328 | tf_op jit(solution)/shard_map/ppermute | solution.py:353
  19.4 1.8 %collective-permute-done.other_ref = bf16[8,40,896]{2,1,0:T(8,128)(2,1)S(1)} collective-permute-done((bf16[8,40,896]{2,1,0:T(8,128)(2,1)}, bf16[8,40,896]{2,1,0:T(8,128)(2,1)S(1)}, u32[]{:S(2)}, u32[]{:S(2)}) %collective-permute-start) | collective-permute-done | bytes 573472 | tf_op jit(solution)/shard_map/ppermute | solution.py:353
  21.2 2.0 %shard_map.113 = bf16[8,40,896]{2,1,0:T(8,128)(2,1)} custom-call(bf16[8,40,896]{2,1,0:T(8,128)(2,1)} %get-tuple-element.20.mine_ref, bf16[8,40,896]{2,1,0:T(8,128)(2,1)S(1)} %collective-permute-done.other_ref), custom_call_target="tpu_custom_call" | custom-call | tf_op jit(solution)/shard_map/pallas_call | solution.py:364
  23.1 3.5 %all-to-all-start = ((bf16[8,40,896]{2,1,0:T(8,128)(2,1)}), bf16[8,40,896]{2,1,0:T(8,128)(2,1)S(1)}, u32[]{:S(2)}, u32[]{:S(2)}) async-start(bf16[8,40,896]{2,1,0:T(8,128)(2,1)} %shard_map.113), calls=%async_computation | async-start | bytes 1146880 | tf_op jit(solution)/shard_map/all_to_all | solution.py:377
  28.3 17.4 %all-to-all-done.got_ref = bf16[8,40,896]{2,1,0:T(8,128)(2,1)S(1)} async-done(((bf16[8,40,896]{2,1,0:T(8,128)(2,1)}), bf16[8,40,896]{2,1,0:T(8,128)(2,1)S(1)}, u32[]{:S(2)}, u32[]{:S(2)}) %all-to-all-start) | async-done | bytes 573472 | tf_op jit(solution)/shard_map/all_to_all | solution.py:377
  45.7 1.8 %shard_map.114 = bf16[8,40,896]{2,1,0:T(8,128)(2,1)} custom-call(bf16[8,40,896]{2,1,0:T(8,128)(2,1)S(1)} %all-to-all-done.got_ref, bf16[40,896]{1,0:T(8,128)(2,1)} %dynamic_slice.3.x_ref), custom_call_target="tpu_custom_call" | custom-call | tf_op jit(solution)/shard_map/pallas_call | solution.py:364
  47.5 3.6 %all-to-all-start.1 = ((bf16[8,40,896]{2,1,0:T(8,128)(2,1)}), bf16[8,40,896]{2,1,0:T(8,128)(2,1)S(1)}, u32[]{:S(2)}, u32[]{:S(2)}) async-start(bf16[8,40,896]{2,1,0:T(8,128)(2,1)} %shard_map.114), calls=%async_computation.1 | async-start | bytes 1146880 | tf_op jit(solution)/shard_map/all_to_all | solution.py:464
  51.1 3.8 %shard_map.115 = (bf16[8,32,896]{2,1,0:T(8,128)(2,1)}, bf16[8,32,896]{2,1,0:T(8,128)(2,1)}) custom-call(s32[1]{0:T(128)} %bitcast.core_ref, bf16[128,256]{1,0:T(8,128)(2,1)} %rows_ref.1, bf16[256,3584]{1,0:T(8,128)(2,1)} %weight_hbm.1), custom_call_target="tpu_custom_call" | custom-call | tf_op jit(solution)/shard_map/pallas_call | solution.py:364
  54.8 2.4 %collective-permute-start.2 = (bf16[8,32,896]{2,1,0:T(8,128)(2,1)}, bf16[8,32,896]{2,1,0:T(8,128)(2,1)S(1)}, u32[]{:S(2)}, u32[]{:S(2)}) collective-permute-start(bf16[8,32,896]{2,1,0:T(8,128)(2,1)} %get-tuple-element.23), channel_id=1, source_target_pairs={{0,1},{1,0},{2,3},{3,2},{4,5},{5,4},{6,7},{7,6},{8,9},{9,8},{10,11... | collective-permute-start | bytes 1376264 | tf_op jit(solution)/shard_map/ppermute | solution.py:353
  57.2 1.6 %collective-permute-done.2.other_ref = bf16[8,32,896]{2,1,0:T(8,128)(2,1)S(1)} collective-permute-done((bf16[8,32,896]{2,1,0:T(8,128)(2,1)}, bf16[8,32,896]{2,1,0:T(8,128)(2,1)S(1)}, u32[]{:S(2)}, u32[]{:S(2)}) %collective-permute-start.2) | collective-permute-done | bytes 458784 | tf_op jit(solution)/shard_map/ppermute | solution.py:353
  58.9 1.8 %shard_map.116 = (bf16[3,32,896]{2,1,0:T(8,128)(2,1)}, bf16[2,32,896]{2,1,0:T(8,128)(2,1)}, bf16[3,32,896]{2,1,0:T(8,128)(2,1)}) custom-call(s32[1]{0:T(128)} %bitcast.3.y_ref, bf16[8,32,896]{2,1,0:T(8,128)(2,1)} %get-tuple-element.22.mine_ref, bf16[8,32,896]{2,1,0:T(8,128)(2,1)S(1)} %collective-permute-done.2.other_ref), custom_call_target="tpu_custom_call" | custom-call | tf_op jit(solution)/shard_map/pallas_call | solution.py:364
  60.7 3.5 %collective-permute-start.3 = (bf16[3,32,896]{2,1,0:T(8,128)(2,1)}, bf16[3,32,896]{2,1,0:T(8,128)(2,1)S(1)}, u32[]{:S(2)}, u32[]{:S(2)}) collective-permute-start(bf16[3,32,896]{2,1,0:T(8,128)(2,1)} %get-tuple-element.25), channel_id=1, source_target_pairs={{0,2},{2,4},{4,6},{6,8},{8,10},{10,12},{12,14},{14,0},{1,3},{3,5},... | collective-permute-start | bytes 516104 | tf_op jit(solution)/shard_map/ppermute | solution.py:358
  64.2 3.2 %collective-permute-start.4 = (bf16[2,32,896]{2,1,0:T(8,128)(2,1)}, bf16[2,32,896]{2,1,0:T(8,128)(2,1)S(1)}, u32[]{:S(2)}, u32[]{:S(2)}) collective-permute-start(bf16[2,32,896]{2,1,0:T(8,128)(2,1)} %get-tuple-element.26), channel_id=1, source_target_pairs={{0,14},{2,0},{4,2},{6,4},{8,6},{10,8},{12,10},{14,12},{1,15},{3,1}... | collective-permute-start | bytes 344072 | tf_op jit(solution)/shard_map/ppermute | solution.py:358
  67.4 3.0 %collective-permute-done.4.above_ref = bf16[2,32,896]{2,1,0:T(8,128)(2,1)S(1)} collective-permute-done((bf16[2,32,896]{2,1,0:T(8,128)(2,1)}, bf16[2,32,896]{2,1,0:T(8,128)(2,1)S(1)}, u32[]{:S(2)}, u32[]{:S(2)}) %collective-permute-start.4) | collective-permute-done | bytes 114720 | tf_op jit(solution)/shard_map/ppermute | solution.py:358
  70.4 1.6 %collective-permute-done.3.below_ref = bf16[3,32,896]{2,1,0:T(8,128)(2,1)S(1)} collective-permute-done((bf16[3,32,896]{2,1,0:T(8,128)(2,1)}, bf16[3,32,896]{2,1,0:T(8,128)(2,1)S(1)}, u32[]{:S(2)}, u32[]{:S(2)}) %collective-permute-start.3) | collective-permute-done | bytes 172064 | tf_op jit(solution)/shard_map/ppermute | solution.py:358
  72.0 1.6 %shard_map.117 = (f32[32,896]{1,0:T(8,128)}, bf16[32,896]{1,0:T(8,128)(2,1)}, bf16[32,896]{1,0:T(8,128)(2,1)}) custom-call(bf16[3,32,896]{2,1,0:T(8,128)(2,1)} %get-tuple-element.24.keep_ref, bf16[3,32,896]{2,1,0:T(8,128)(2,1)S(1)} %collective-permute-done.3.below_ref, bf16[2,32,896]{2,1,0:T(8,128)(2,1)S(1)} %collective-permute-done.4.above_ref), custom_call_target="tpu_custom_call" | custom-call | tf_op jit(solution)/shard_map/pallas_call | solution.py:364
  73.6 5.7 %collective-permute-start.5 = (bf16[32,896]{1,0:T(8,128)(2,1)}, bf16[32,896]{1,0:T(8,128)(2,1)S(1)}, u32[]{:S(2)}, u32[]{:S(2)}) collective-permute-start(bf16[32,896]{1,0:T(8,128)(2,1)} %get-tuple-element.28), channel_id=1, source_target_pairs={{0,6},{2,8},{4,10},{6,12},{8,14},{10,0},{12,2},{14,4},{1,7},{3,9},... | collective-permute-start | bytes 172040 | tf_op jit(solution)/shard_map/ppermute | solution.py:358
  79.3 2.6 %collective-permute-start.6 = (bf16[32,896]{1,0:T(8,128)(2,1)}, bf16[32,896]{1,0:T(8,128)(2,1)S(1)}, u32[]{:S(2)}, u32[]{:S(2)}) collective-permute-start(bf16[32,896]{1,0:T(8,128)(2,1)} %get-tuple-element.29), channel_id=1, source_target_pairs={{0,10},{2,12},{4,14},{6,0},{8,2},{10,4},{12,6},{14,8},{1,11},{3,13... | collective-permute-start | bytes 172040 | tf_op jit(solution)/shard_map/ppermute | solution.py:358
  82.0 5.2 %collective-permute-done.6 = bf16[32,896]{1,0:T(8,128)(2,1)S(1)} collective-permute-done((bf16[32,896]{1,0:T(8,128)(2,1)}, bf16[32,896]{1,0:T(8,128)(2,1)S(1)}, u32[]{:S(2)}, u32[]{:S(2)}) %collective-permute-start.6) | collective-permute-done | bytes 57376 | tf_op jit(solution)/shard_map/ppermute | solution.py:358
  88.1 5.2 %collective-permute-start.1 = (bf16[8,40,896]{2,1,0:T(8,128)(2,1)S(1)}, bf16[8,40,896]{2,1,0:T(8,128)(2,1)S(1)}, u32[]{:S(2)}, u32[]{:S(2)}) collective-permute-start(bf16[8,40,896]{2,1,0:T(8,128)(2,1)S(1)} %all-to-all-done.1.own_ref), channel_id=1, source_target_pairs={{0,1},{1,0},{2,3},{3,2},{4,5},{5,4},{6,7},{7,6},{8,9},{9,8},{10,11... | collective-permute-start | bytes 1720328 | tf_op jit(solution)/shard_map/ppermute | solution.py:353
  93.4 17.0 %all-gather = bf16[512,896]{1,0:T(8,128)(2,1)S(1)} all-gather(bf16[32,896]{1,0:T(8,128)(2,1)S(1)} %add_convert_fusion), channel_id=2, replica_groups=mesh['seq'=48,'y'=8,'core'=2] {'y','core'}, dimensions={0}, use_global_device_ids=true | all-gather | bytes 974848 | tf_op jit(solution)/shard_map/all_gather | solution.py:447
  113.0 3.7 %collective-permute-done.7.earlier_ref = bf16[4,32,896]{2,1,0:T(8,128)(2,1)S(1)} collective-permute-done((bf16[4,32,896]{2,1,0:T(8,128)(2,1)S(1)}, bf16[4,32,896]{2,1,0:T(8,128)(2,1)S(1)}, u32[]{:S(2)}, u32[]{:S(2)}) %collective-permute-start.7) | collective-permute-done | bytes 229408 | tf_op jit(solution)/shard_map/ppermute | solution.py:349
  117.5 2.7 %shard_map.118.goal_ref = bf16[160,3584]{1,0:T(8,128)(2,1)} custom-call(s32[1]{0:T(128)S(6)} %add.31.start_ref, bf16[16,32,896]{2,1,0:T(8,128)(2,1)} %bitcast.11, bf16[4,32,896]{2,1,0:T(8,128)(2,1)} %copy-done.3), custom_call_target="tpu_custom_call" | custom-call | tf_op jit(solution)/shard_map/pallas_call | solution.py:364
  120.2 8.6 %shard_map.120 = (bf16[8,280,128]{2,1,0:T(8,128)(2,1)}, bf16[8,280,128]{2,1,0:T(8,128)(2,1)}) custom-call(s32[1]{0:T(128)} %bitcast.core_ref, s32[1]{0:T(128)S(6)} %copy.15.count_ref, bf16[8,40,896]{2,1,0:T(8,128)(2,1)S(1)} %all-to-all-done.1.own_ref, bf16[8,40,896]{2,1,0:T(8,128)(2,1)S(1)} %collective-permute-done.1.other_ref, ...), custom_call_target="tpu_custom_call" | custom-call | tf_op jit(solution)/shard_map/pallas_call | solution.py:364
  128.9 2.6 %collective-permute-start.8 = (bf16[8,280,128]{2,1,0:T(8,128)(2,1)}, bf16[8,280,128]{2,1,0:T(8,128)(2,1)S(1)}, u32[]{:S(2)}, u32[]{:S(2)}) collective-permute-start(bf16[8,280,128]{2,1,0:T(8,128)(2,1)} %get-tuple-element.35), channel_id=1, source_target_pairs={{0,1},{1,0},{2,3},{3,2},{4,5},{5,4},{6,7},{7,6},{8,9},{9,8},{10,11... | collective-permute-start | bytes 1720328 | tf_op jit(solution)/shard_map/ppermute | solution.py:353
  131.5 1.8 %collective-permute-done.8.other_ref = bf16[8,280,128]{2,1,0:T(8,128)(2,1)S(1)} collective-permute-done((bf16[8,280,128]{2,1,0:T(8,128)(2,1)}, bf16[8,280,128]{2,1,0:T(8,128)(2,1)S(1)}, u32[]{:S(2)}, u32[]{:S(2)}) %collective-permute-start.8) | collective-permute-done | bytes 573472 | tf_op jit(solution)/shard_map/ppermute | solution.py:353
  133.3 2.0 %shard_map.121 = bf16[8,280,128]{2,1,0:T(8,128)(2,1)} custom-call(bf16[8,280,128]{2,1,0:T(8,128)(2,1)} %get-tuple-element.34.mine_ref, bf16[8,280,128]{2,1,0:T(8,128)(2,1)S(1)} %collective-permute-done.8.other_ref), custom_call_target="tpu_custom_call" | custom-call | tf_op jit(solution)/shard_map/pallas_call | solution.py:364
  135.3 4.4 %all-to-all-start.2 = ((bf16[8,280,128]{2,1,0:T(8,128)(2,1)}), bf16[8,280,128]{2,1,0:T(8,128)(2,1)S(1)}, u32[]{:S(2)}, u32[]{:S(2)}) async-start(bf16[8,280,128]{2,1,0:T(8,128)(2,1)} %shard_map.121), calls=%async_computation.2 | async-start | bytes 1146880 | tf_op jit(solution)/shard_map/all_to_all | solution.py:377
  139.7 3.5 %shard_map.119 = (bf16[160,3584]{1,0:T(8,128)(2,1)}, f32[10,3584]{1,0:T(8,128)}, f32[10,3584]{1,0:T(8,128)}) custom-call(s32[1]{0:T(128)} %bitcast.core_ref, s32[1]{0:T(128)} %bitcast.1.first_ref, s32[1]{0:T(128)S(6)} %copy.15.count_ref, bf16[8,40,896]{2,1,0:T(8,128)(2,1)} %copy-done, bf16[8,40,896]{2,1,0:T(8,128)(2,1)} %copy-done.1, ...), custom_call_target="tpu_custom_call" | custom-call | tf_op jit(solution)/shard_map/pallas_call | solution.py:364
  143.1 15.6 %all-to-all-done.2.got_ref = bf16[8,280,128]{2,1,0:T(8,128)(2,1)S(1)} async-done(((bf16[8,280,128]{2,1,0:T(8,128)(2,1)}), bf16[8,280,128]{2,1,0:T(8,128)(2,1)S(1)}, u32[]{:S(2)}, u32[]{:S(2)}) %all-to-all-start.2) | async-done | bytes 573472 | tf_op jit(solution)/shard_map/all_to_all | solution.py:377
  158.7 1.9 %shard_map.122 = bf16[10,3584]{1,0:T(8,128)(2,1)} custom-call(bf16[8,280,128]{2,1,0:T(8,128)(2,1)S(1)} %all-to-all-done.2.got_ref, f32[10,3584]{1,0:T(8,128)} %get-tuple-element.36.x_ref, f32[10,3584]{1,0:T(8,128)} %get-tuple-element.37.dy_ref, f32[3584]{0:T(1024)} %gain_ref.3), custom_call_target="tpu_custom_call" | custom-call | tf_op jit(solution)/shard_map/pallas_call | solution.py:364
  (15 shorter events, 4.6 us)
Async XLA Ops:
  7.0 14.2 %collective-permute-start = (bf16[8,40,896]{2,1,0:T(8,128)(2,1)}, bf16[8,40,896]{2,1,0:T(8,128)(2,1)S(1)}, u32[]{:S(2)}, u32[]{:S(2)}) collective-permute-start(bf16[8,40,896]{2,1,0:T(8,128)(2,1)} %get-tuple-element.21), channel_id=1, source_target_pairs={{0,1},{1,0},{2,3},{3,2},{4,5},{5,4},{6,7},{7,6},{8,9},{9,8},{10,11... | collective-permute-start | bytes 1720328 | tf_op jit(solution)/shard_map/ppermute | solution.py:353
  23.1 22.5 %all-to-all-start = ((bf16[8,40,896]{2,1,0:T(8,128)(2,1)}), bf16[8,40,896]{2,1,0:T(8,128)(2,1)S(1)}, u32[]{:S(2)}, u32[]{:S(2)}) async-start(bf16[8,40,896]{2,1,0:T(8,128)(2,1)} %shard_map.113), calls=%async_computation | async-start | bytes 1146880 | tf_op jit(solution)/shard_map/all_to_all | solution.py:377
  47.5 40.6 %all-to-all-start.1 = ((bf16[8,40,896]{2,1,0:T(8,128)(2,1)}), bf16[8,40,896]{2,1,0:T(8,128)(2,1)S(1)}, u32[]{:S(2)}, u32[]{:S(2)}) async-start(bf16[8,40,896]{2,1,0:T(8,128)(2,1)} %shard_map.114), calls=%async_computation.1 | async-start | bytes 1146880 | tf_op jit(solution)/shard_map/all_to_all | solution.py:464
  54.8 4.0 %collective-permute-start.2 = (bf16[8,32,896]{2,1,0:T(8,128)(2,1)}, bf16[8,32,896]{2,1,0:T(8,128)(2,1)S(1)}, u32[]{:S(2)}, u32[]{:S(2)}) collective-permute-start(bf16[8,32,896]{2,1,0:T(8,128)(2,1)} %get-tuple-element.23), channel_id=1, source_target_pairs={{0,1},{1,0},{2,3},{3,2},{4,5},{5,4},{6,7},{7,6},{8,9},{9,8},{10,11... | collective-permute-start | bytes 1376264 | tf_op jit(solution)/shard_map/ppermute | solution.py:353
  60.7 11.3 %collective-permute-start.3 = (bf16[3,32,896]{2,1,0:T(8,128)(2,1)}, bf16[3,32,896]{2,1,0:T(8,128)(2,1)S(1)}, u32[]{:S(2)}, u32[]{:S(2)}) collective-permute-start(bf16[3,32,896]{2,1,0:T(8,128)(2,1)} %get-tuple-element.25), channel_id=1, source_target_pairs={{0,2},{2,4},{4,6},{6,8},{8,10},{10,12},{12,14},{14,0},{1,3},{3,5},... | collective-permute-start | bytes 516104 | tf_op jit(solution)/shard_map/ppermute | solution.py:358
  64.2 6.2 %collective-permute-start.4 = (bf16[2,32,896]{2,1,0:T(8,128)(2,1)}, bf16[2,32,896]{2,1,0:T(8,128)(2,1)S(1)}, u32[]{:S(2)}, u32[]{:S(2)}) collective-permute-start(bf16[2,32,896]{2,1,0:T(8,128)(2,1)} %get-tuple-element.26), channel_id=1, source_target_pairs={{0,14},{2,0},{4,2},{6,4},{8,6},{10,8},{12,10},{14,12},{1,15},{3,1}... | collective-permute-start | bytes 344072 | tf_op jit(solution)/shard_map/ppermute | solution.py:358
  73.6 8.4 %collective-permute-start.5 = (bf16[32,896]{1,0:T(8,128)(2,1)}, bf16[32,896]{1,0:T(8,128)(2,1)S(1)}, u32[]{:S(2)}, u32[]{:S(2)}) collective-permute-start(bf16[32,896]{1,0:T(8,128)(2,1)} %get-tuple-element.28), channel_id=1, source_target_pairs={{0,6},{2,8},{4,10},{6,12},{8,14},{10,0},{12,2},{14,4},{1,7},{3,9},... | collective-permute-start | bytes 172040 | tf_op jit(solution)/shard_map/ppermute | solution.py:358
  79.3 7.9 %collective-permute-start.6 = (bf16[32,896]{1,0:T(8,128)(2,1)}, bf16[32,896]{1,0:T(8,128)(2,1)S(1)}, u32[]{:S(2)}, u32[]{:S(2)}) collective-permute-start(bf16[32,896]{1,0:T(8,128)(2,1)} %get-tuple-element.29), channel_id=1, source_target_pairs={{0,10},{2,12},{4,14},{6,0},{8,2},{10,4},{12,6},{14,8},{1,11},{3,13... | collective-permute-start | bytes 172040 | tf_op jit(solution)/shard_map/ppermute | solution.py:358
  88.1 32.1 %copy-start = (bf16[8,40,896]{2,1,0:T(8,128)(2,1)}, bf16[8,40,896]{2,1,0:T(8,128)(2,1)S(1)}, u32[]{:S(2)}) copy-start(bf16[8,40,896]{2,1,0:T(8,128)(2,1)S(1)} %all-to-all-done.1.own_ref) | copy-start | bytes 1720324
  88.1 32.0 %collective-permute-start.1 = (bf16[8,40,896]{2,1,0:T(8,128)(2,1)S(1)}, bf16[8,40,896]{2,1,0:T(8,128)(2,1)S(1)}, u32[]{:S(2)}, u32[]{:S(2)}) collective-permute-start(bf16[8,40,896]{2,1,0:T(8,128)(2,1)S(1)} %all-to-all-done.1.own_ref), channel_id=1, source_target_pairs={{0,1},{1,0},{2,3},{3,2},{4,5},{5,4},{6,7},{7,6},{8,9},{9,8},{10,11... | collective-permute-start | bytes 1720328 | tf_op jit(solution)/shard_map/ppermute | solution.py:353
  110.3 6.4 %copy-start.2 = (bf16[512,896]{1,0:T(8,128)(2,1)}, bf16[512,896]{1,0:T(8,128)(2,1)S(1)}, u32[]{:S(2)}) copy-start(bf16[512,896]{1,0:T(8,128)(2,1)S(1)} %all-gather) | copy-start | bytes 2752516
  110.4 6.4 %collective-permute-start.7 = (bf16[4,32,896]{2,1,0:T(8,128)(2,1)S(1)}, bf16[4,32,896]{2,1,0:T(8,128)(2,1)S(1)}, u32[]{:S(2)}, u32[]{:S(2)}) collective-permute-start(bf16[4,32,896]{2,1,0:T(8,128)(2,1)S(1)} %slice_bitcast_fusion), channel_id=1, source_target_pairs={{0,16},{16,32},{32,48},{48,64},{64,80},{80,96},{96,112},{112,128},... | collective-permute-start | bytes 688136 | tf_op jit(solution)/shard_map/ppermute | solution.py:349
  116.7 0.7 copy-start.3
  120.2 8.7 %copy-start.1 = (bf16[8,40,896]{2,1,0:T(8,128)(2,1)}, bf16[8,40,896]{2,1,0:T(8,128)(2,1)S(1)}, u32[]{:S(2)}) copy-start(bf16[8,40,896]{2,1,0:T(8,128)(2,1)S(1)} %collective-permute-done.1.other_ref) | copy-start | bytes 1720324
  128.9 4.5 %collective-permute-start.8 = (bf16[8,280,128]{2,1,0:T(8,128)(2,1)}, bf16[8,280,128]{2,1,0:T(8,128)(2,1)S(1)}, u32[]{:S(2)}, u32[]{:S(2)}) collective-permute-start(bf16[8,280,128]{2,1,0:T(8,128)(2,1)} %get-tuple-element.35), channel_id=1, source_target_pairs={{0,1},{1,0},{2,3},{3,2},{4,5},{5,4},{6,7},{7,6},{8,9},{9,8},{10,11... | collective-permute-start | bytes 1720328 | tf_op jit(solution)/shard_map/ppermute | solution.py:353
  135.3 23.4 %all-to-all-start.2 = ((bf16[8,280,128]{2,1,0:T(8,128)(2,1)}), bf16[8,280,128]{2,1,0:T(8,128)(2,1)S(1)}, u32[]{:S(2)}, u32[]{:S(2)}) async-start(bf16[8,280,128]{2,1,0:T(8,128)(2,1)} %shard_map.121), calls=%async_computation.2 | async-start | bytes 1146880 | tf_op jit(solution)/shard_map/all_to_all | solution.py:377

commit v5 on v3

--- a/solution.py
+++ b/solution.py
@@ -79,18 +79,36 @@
         store.wait()
 
 
-def align_kernel(start_ref, own_ref, earlier_ref, out_ref):
+def collect_kernel(y_ref, own_ref, far_ref, below_ref, above_ref, out_ref):
+    own, low, high = 0, -3, 3
+
+    def put(r, block):
+        out_ref[(y_ref[0] + (r + 8)) & 7] = block
+
+    put(own, own_ref[0])
+    put(low, far_ref[0])
+    put(high, far_ref[1])
+    for k, r in enumerate((own, low, high)):
+        put(r - 1, below_ref[k])
+    for k, r in enumerate((own, low)):
+        put(r + 1, above_ref[k])
+
+
+def align_kernel(core_ref, start_ref, half_ref, other_ref, earlier_ref, out_ref):
     slots = out_ref.shape[0]
-    wide = own_ref.shape[2]
+    wide = half_ref.shape[2]
     row = lax.broadcasted_iota(jnp.int32, (slots, slots), 0)
     col = lax.broadcasted_iota(jnp.int32, (slots, slots), 1)
     pick = (col == row + start_ref[0]).astype(BF16)
     for j in range(COLS):
-        bands = [earlier_ref[j]]
+        bands = [earlier_ref[j].astype(F32)]
         for c in range(2):
             for i in range(2):
-                bands.append(own_ref[2 * (i * COLS + j) + c])
-        rows = jnp.concatenate(bands, axis=0)
+                n = i * COLS + j
+                bands.append(
+                    jnp.where(core_ref[0] == c, half_ref[n].astype(F32), other_ref[n].astype(F32))
+                )
+        rows = jnp.concatenate(bands, axis=0).astype(BF16)
         out_ref[:, j * wide : (j + 1) * wide] = nn(pick, rows).astype(BF16)
 
 
@@ -336,6 +354,11 @@
     return lax.ppermute(block, "core", PAIR)
 
 
+def turn(block, distance):
+    size = lax.axis_size("y")
+    return lax.ppermute(block, "y", [(i, (i + distance) % size) for i in range(size)])
+
+
 def call(kernel, outs, scratch, *args, far=0, place=VMEM):
     specs = [SMEM if a.shape == (1,) else VMEM for a in args]
     specs[len(args) - far :] = [HBM] * far
@@ -409,10 +432,18 @@
     )(core_s, student_in, norm_gain, doc_start, w_query, w_keyval, w_out)
     branch_got = spread(mine, send)
     goal_own = jnp.sum(goal_got.astype(F32), axis=0).astype(BF16)
-    goal_rows = lax.all_gather(goal_own, TP)
-    earlier = goal_rows.reshape(2, COLS, 2, quarter, wide)[1, :, 1]
-    earlier = from_behind(earlier, "seq", 1)
-    goal = call(align_kernel, shape((slots, width), BF16), (), start, goal_rows, earlier)
+    goal_own = goal_own[None]
+    far = jnp.concatenate([turn(goal_own, 3), turn(goal_own, -3)], axis=0)
+    below = turn(jnp.concatenate([goal_own, far], axis=0), 1)
+    above = turn(jnp.concatenate([goal_own, far[:1]], axis=0), -1)
+    ypos_s = ypos.astype(jnp.int32).reshape(1)
+    goal_half = call(collect_kernel, parts, (), ypos_s, goal_own, far, near(below), near(above))
+    goal_other = swap(goal_half)
+    last = jnp.where(core == 1, goal_half[COLS:], goal_other[COLS:])
+    earlier = from_behind(last, "seq", 1)
+    goal = call(
+        align_kernel, shape((slots, width), BF16), (), core_s, start, goal_half, goal_other, earlier
+    )
     x_block = lax.dynamic_slice(
         student_in,
         (core * (slots // 2) + (ypos // COLS) * high, (ypos % COLS) * wide),

time: 158 us -> 160 us (1.013)
  starting transfers between devices: 35.1 us -> 58.4 us
  blocking collectives: 17.2 us -> 0 us
  waiting for transfers between devices: 65.8 us -> 57.5 us
  other arithmetic: 0.07 us -> 1.9 us
  Pallas kernels: 34.5 us -> 36.3 us
    all_to_all x1, waiting for transfers between devices: 18.9 us -> 0.01 us  [body(): y_half = lax.all_to_all(y_own, 'y', 0, 0)]
    all_gather x1 -> x0, blocking collectives: 17.2 us -> none  [body(): goal_rows = lax.all_gather(goal_own, TP)]
    ppermute x0 -> x4, starting transfers between devices: none -> 17.1 us  [turn(): lax.ppermute(block, 'y', [(i, (i + distance) % size) for i in range(size)])]
    ppermute x0 -> x4, waiting for transfers between devices: none -> 10.8 us  [turn(): lax.ppermute(block, 'y', [(i, (i + distance) % size) for i in range(size)])]
    ppermute x4 -> x5, starting transfers between devices: 19.7 us -> 24.8 us  [swap(): return lax.ppermute(block, 'core', PAIR)]
    pallas_call x9 -> x10, Pallas kernels: 28.2 us -> 29.9 us  [call(): pl.pallas_call(kernel, out_shape=outs, in_specs=specs, out_specs=jax.tree...]
    ppermute x4 -> x5, waiting for transfers between devices: 5.23 us -> 5.23 us  [swap(): return lax.ppermute(block, 'core', PAIR)]
  transfers between devices with their start and end apart: 9 -> 14, of which waited for: 8 -> 10; matrix products, arithmetic and copies ran while one was open for 1% -> 2% of each run, Pallas kernels for 9% -> 10%
where the time goes in v5:
time: 160 us; the launch traced here: 158 us
  starting transfers between devices  58.4 us (36%)
  waiting for transfers between devices  57.5 us (36%)
  Pallas kernels  36.3 us (23%)
  local copies, waits for them, and re-layouts  2.23 us (1%)
  between operations  2.22 us (1%)
  other arithmetic  1.9 us (1%)
    all_to_all x3, waiting for transfers between devices, spread(): return lax.all_to_all(chip, 'y', 0, 0)  38 us
    pallas_call x10, Pallas kernels, call(): pl.pallas_call(kernel, out_shape=outs, in_specs=specs, out_specs=jax.tree...  29.9 us
    ppermute x5, starting transfers between devices, swap(): return lax.ppermute(block, 'core', PAIR)  24.8 us
    ppermute x4, starting transfers between devices, turn(): lax.ppermute(block, 'y', [(i, (i + distance) % size) for i in range(size)])  17.1 us
    all_to_all x3, starting transfers between devices, spread(): return lax.all_to_all(chip, 'y', 0, 0)  11.7 us
    ppermute x4, waiting for transfers between devices, turn(): lax.ppermute(block, 'y', [(i, (i + distance) % size) for i in range(size)])  10.8 us
    pallas_call x1, Pallas kernels, body(): pl.pallas_call(forward_kernel, out_shape=(shape((slots, QPK * HD), BF16),...  6.32 us
    ppermute x5, waiting for transfers between devices, swap(): return lax.ppermute(block, 'core', PAIR)  5.23 us
  transfers between devices with their start and end apart: 14, of which 10 were waited for; matrix products, arithmetic and copies ran while one was open for 2% of the time, Pallas kernels for 10%

profile of v5, /device:TPU:1, one launch (start us, length us, event | category | flops | bytes accessed | tf_op | source)
XLA Modules:
  0.0 158.5 jit_solution(3285079967417368937)
XLA Ops:
  0.6 6.3 %forward.1 = (bf16[160,256]{1,0:T(8,128)(2,1)}, bf16[160,256]{1,0:T(8,128)(2,1)}, f32[2,160,160]{2,1,0:T(8,128)}, bf16[8,40,896]{2,1,0:T(8,128)(2,1)}, bf16[8,40,896]{2,1,0:T(8,128)(2,1)}) custom-call(s32[1]{0:T(128)} %bitcast.core_ref, bf16[160,3584]{1,0:T(8,128)(2,1)} %x_ref.3, f32[3584]{0:T(1024)} %gain_ref.3, s32[160]{0:T(256)} %starts_ref.1, ...), custom_call_target="tpu_custom_call" | custom-call | tf_op jit(solution)/shard_map/forward/pallas_call | solution.py:413
  7.0 12.4 %collective-permute-start = (bf16[8,40,896]{2,1,0:T(8,128)(2,1)}, bf16[8,40,896]{2,1,0:T(8,128)(2,1)S(1)}, u32[]{:S(2)}, u32[]{:S(2)}) collective-permute-start(bf16[8,40,896]{2,1,0:T(8,128)(2,1)} %get-tuple-element.15), channel_id=1, source_target_pairs={{0,1},{1,0},{2,3},{3,2},{4,5},{5,4},{6,7},{7,6},{8,9},{9,8},{10,11... | collective-permute-start | bytes 1720328 | tf_op jit(solution)/shard_map/ppermute | solution.py:354
  19.4 1.8 %collective-permute-done.other_ref = bf16[8,40,896]{2,1,0:T(8,128)(2,1)S(1)} collective-permute-done((bf16[8,40,896]{2,1,0:T(8,128)(2,1)}, bf16[8,40,896]{2,1,0:T(8,128)(2,1)S(1)}, u32[]{:S(2)}, u32[]{:S(2)}) %collective-permute-start) | collective-permute-done | bytes 573472 | tf_op jit(solution)/shard_map/ppermute | solution.py:354
  21.2 2.0 %shard_map.113 = bf16[8,40,896]{2,1,0:T(8,128)(2,1)} custom-call(bf16[8,40,896]{2,1,0:T(8,128)(2,1)} %get-tuple-element.14.mine_ref, bf16[8,40,896]{2,1,0:T(8,128)(2,1)S(1)} %collective-permute-done.other_ref), custom_call_target="tpu_custom_call" | custom-call | tf_op jit(solution)/shard_map/pallas_call | solution.py:365
  23.1 3.5 %all-to-all-start = ((bf16[8,40,896]{2,1,0:T(8,128)(2,1)}), bf16[8,40,896]{2,1,0:T(8,128)(2,1)S(1)}, u32[]{:S(2)}, u32[]{:S(2)}) async-start(bf16[8,40,896]{2,1,0:T(8,128)(2,1)} %shard_map.113), calls=%async_computation | async-start | bytes 1146880 | tf_op jit(solution)/shard_map/all_to_all | solution.py:378
  26.7 3.8 %shard_map.115 = (bf16[8,32,896]{2,1,0:T(8,128)(2,1)}, bf16[8,32,896]{2,1,0:T(8,128)(2,1)}) custom-call(s32[1]{0:T(128)} %bitcast.core_ref, bf16[128,256]{1,0:T(8,128)(2,1)} %rows_ref.1, bf16[256,3584]{1,0:T(8,128)(2,1)} %weight_hbm.1), custom_call_target="tpu_custom_call" | custom-call | tf_op jit(solution)/shard_map/pallas_call | solution.py:365
  30.4 2.3 %collective-permute-start.2 = (bf16[8,32,896]{2,1,0:T(8,128)(2,1)}, bf16[8,32,896]{2,1,0:T(8,128)(2,1)S(1)}, u32[]{:S(2)}, u32[]{:S(2)}) collective-permute-start(bf16[8,32,896]{2,1,0:T(8,128)(2,1)} %get-tuple-element.17), channel_id=1, source_target_pairs={{0,1},{1,0},{2,3},{3,2},{4,5},{5,4},{6,7},{7,6},{8,9},{9,8},{10,11... | collective-permute-start | bytes 1376264 | tf_op jit(solution)/shard_map/ppermute | solution.py:354
  34.4 1.9 %shard_map.116 = bf16[8,32,896]{2,1,0:T(8,128)(2,1)} custom-call(bf16[8,32,896]{2,1,0:T(8,128)(2,1)} %get-tuple-element.16.mine_ref, bf16[8,32,896]{2,1,0:T(8,128)(2,1)S(1)} %collective-permute-done.2.other_ref), custom_call_target="tpu_custom_call" | custom-call | tf_op jit(solution)/shard_map/pallas_call | solution.py:365
  36.3 9.4 %all-to-all-done.got_ref = bf16[8,40,896]{2,1,0:T(8,128)(2,1)S(1)} async-done(((bf16[8,40,896]{2,1,0:T(8,128)(2,1)}), bf16[8,40,896]{2,1,0:T(8,128)(2,1)S(1)}, u32[]{:S(2)}, u32[]{:S(2)}) %all-to-all-start) | async-done | bytes 573472 | tf_op jit(solution)/shard_map/all_to_all | solution.py:378
  45.7 3.5 %all-to-all-start.2 = ((bf16[8,32,896]{2,1,0:T(8,128)(2,1)}), bf16[8,32,896]{2,1,0:T(8,128)(2,1)S(1)}, u32[]{:S(2)}, u32[]{:S(2)}) async-start(bf16[8,32,896]{2,1,0:T(8,128)(2,1)} %shard_map.116), calls=%async_computation.2 | async-start | bytes 917504 | tf_op jit(solution)/shard_map/all_to_all | solution.py:378
  50.7 1.8 %shard_map.114 = bf16[8,40,896]{2,1,0:T(8,128)(2,1)} custom-call(bf16[8,40,896]{2,1,0:T(8,128)(2,1)S(1)} %all-to-all-done.got_ref, bf16[40,896]{1,0:T(8,128)(2,1)} %dynamic_slice.3.x_ref), custom_call_target="tpu_custom_call" | custom-call | tf_op jit(solution)/shard_map/pallas_call | solution.py:365
  52.6 13.1 %all-to-all-done.2 = bf16[8,32,896]{2,1,0:T(8,128)(2,1)S(1)} async-done(((bf16[8,32,896]{2,1,0:T(8,128)(2,1)}), bf16[8,32,896]{2,1,0:T(8,128)(2,1)S(1)}, u32[]{:S(2)}, u32[]{:S(2)}) %all-to-all-start.2) | async-done | bytes 458784 | tf_op jit(solution)/shard_map/all_to_all | solution.py:378
  65.6 3.5 %all-to-all-start.1 = ((bf16[8,40,896]{2,1,0:T(8,128)(2,1)}), bf16[8,40,896]{2,1,0:T(8,128)(2,1)S(1)}, u32[]{:S(2)}, u32[]{:S(2)}) async-start(bf16[8,40,896]{2,1,0:T(8,128)(2,1)} %shard_map.114), calls=%async_computation.1 | async-start | bytes 1146880 | tf_op jit(solution)/shard_map/all_to_all | solution.py:460
  69.2 5.1 %collective-permute-start.3 = (bf16[1,32,896]{2,1,0:T(8,128)(2,1)S(1)}, bf16[1,32,896]{2,1,0:T(8,128)(2,1)S(1)}, u32[]{:S(2)}, u32[]{:S(2)}) collective-permute-start(bf16[1,32,896]{2,1,0:T(8,128)(2,1)S(1)} %bitcast.5), channel_id=1, source_target_pairs={{0,6},{2,8},{4,10},{6,12},{8,14},{10,0},{12,2},{14,4},{1,7},{3,9},... | collective-permute-start | bytes 172040 | tf_op jit(solution)/shard_map/ppermute | solution.py:359
  74.3 3.2 %collective-permute-start.4 = (bf16[1,32,896]{2,1,0:T(8,128)(2,1)S(1)}, bf16[1,32,896]{2,1,0:T(8,128)(2,1)S(1)}, u32[]{:S(2)}, u32[]{:S(2)}) collective-permute-start(bf16[1,32,896]{2,1,0:T(8,128)(2,1)S(1)} %bitcast.6), channel_id=1, source_target_pairs={{0,10},{2,12},{4,14},{6,0},{8,2},{10,4},{12,6},{14,8},{1,11},{3,13... | collective-permute-start | bytes 172040 | tf_op jit(solution)/shard_map/ppermute | solution.py:359
  77.6 6.7 %collective-permute-done.3 = bf16[1,32,896]{2,1,0:T(8,128)(2,1)S(1)} collective-permute-done((bf16[1,32,896]{2,1,0:T(8,128)(2,1)S(1)}, bf16[1,32,896]{2,1,0:T(8,128)(2,1)S(1)}, u32[]{:S(2)}, u32[]{:S(2)}) %collective-permute-start.3) | collective-permute-done | bytes 57376 | tf_op jit(solution)/shard_map/ppermute | solution.py:359
  86.0 5.4 %collective-permute-start.5 = (bf16[3,32,896]{2,1,0:T(8,128)(2,1)S(1)}, bf16[3,32,896]{2,1,0:T(8,128)(2,1)S(1)}, u32[]{:S(2)}, u32[]{:S(2)}) collective-permute-start(bf16[3,32,896]{2,1,0:T(8,128)(2,1)S(1)} %pad_maximum_fusion), channel_id=1, source_target_pairs={{0,2},{2,4},{4,6},{6,8},{8,10},{10,12},{12,14},{14,0},{1,3},{3,5},... | collective-permute-start | bytes 516104 | tf_op jit(solution)/shard_map/ppermute | solution.py:359
  92.1 3.4 %collective-permute-start.6 = (bf16[2,32,896]{2,1,0:T(8,128)(2,1)S(1)}, bf16[2,32,896]{2,1,0:T(8,128)(2,1)S(1)}, u32[]{:S(2)}, u32[]{:S(2)}) collective-permute-start(bf16[2,32,896]{2,1,0:T(8,128)(2,1)S(1)} %get-tuple-element.26), channel_id=1, source_target_pairs={{0,14},{2,0},{4,2},{6,4},{8,6},{10,8},{12,10},{14,12},{1,15},{3,1}... | collective-permute-start | bytes 344072 | tf_op jit(solution)/shard_map/ppermute | solution.py:359
  95.4 2.4 %collective-permute-done.6.above_ref = bf16[2,32,896]{2,1,0:T(8,128)(2,1)S(1)} collective-permute-done((bf16[2,32,896]{2,1,0:T(8,128)(2,1)S(1)}, bf16[2,32,896]{2,1,0:T(8,128)(2,1)S(1)}, u32[]{:S(2)}, u32[]{:S(2)}) %collective-permute-start.6) | collective-permute-done | bytes 114720 | tf_op jit(solution)/shard_map/ppermute | solution.py:359
  97.9 1.7 %shard_map.117.half_ref = bf16[8,32,896]{2,1,0:T(8,128)(2,1)} custom-call(s32[1]{0:T(128)} %bitcast.3.y_ref, bf16[1,32,896]{2,1,0:T(8,128)(2,1)} %bitcast.9, bf16[2,32,896]{2,1,0:T(8,128)(2,1)} %get-tuple-element.27.far_ref, bf16[3,32,896]{2,1,0:T(8,128)(2,1)S(1)} %collective-permute-done.5.below_ref, bf16[2,32,896]{2,1,0:T(8,128)(2,1)S(1)} %collective-permute-done.6.above_ref), custom_call_target="tpu_custom_call" | custom-call | tf_op jit(solution)/shard_map/pallas_call | solution.py:365
  99.6 5.2 %collective-permute-start.7 = (bf16[8,32,896]{2,1,0:T(8,128)(2,1)}, bf16[8,32,896]{2,1,0:T(8,128)(2,1)S(1)}, u32[]{:S(2)}, u32[]{:S(2)}) collective-permute-start(bf16[8,32,896]{2,1,0:T(8,128)(2,1)} %shard_map.117.half_ref), channel_id=1, source_target_pairs={{0,1},{1,0},{2,3},{3,2},{4,5},{5,4},{6,7},{7,6},{8,9},{9,8},{10,11... | collective-permute-start | bytes 1376264 | tf_op jit(solution)/shard_map/ppermute | solution.py:354
  104.9 1.9 %collective-permute-start.1 = (bf16[8,40,896]{2,1,0:T(8,128)(2,1)S(1)}, bf16[8,40,896]{2,1,0:T(8,128)(2,1)S(1)}, u32[]{:S(2)}, u32[]{:S(2)}) collective-permute-start(bf16[8,40,896]{2,1,0:T(8,128)(2,1)S(1)} %all-to-all-done.1.own_ref), channel_id=1, source_target_pairs={{0,1},{1,0},{2,3},{3,2},{4,5},{5,4},{6,7},{7,6},{8,9},{9,8},{10,11... | collective-permute-start | bytes 1720328 | tf_op jit(solution)/shard_map/ppermute | solution.py:354
  110.6 3.4 %collective-permute-done.8.earlier_ref = bf16[4,32,896]{2,1,0:T(8,128)(2,1)S(1)} collective-permute-done((bf16[4,32,896]{2,1,0:T(8,128)(2,1)S(1)}, bf16[4,32,896]{2,1,0:T(8,128)(2,1)S(1)}, u32[]{:S(2)}, u32[]{:S(2)}) %collective-permute-start.8) | collective-permute-done | bytes 229408 | tf_op jit(solution)/shard_map/ppermute | solution.py:350
  114.7 2.8 %shard_map.118.goal_ref = bf16[160,3584]{1,0:T(8,128)(2,1)} custom-call(s32[1]{0:T(128)} %bitcast.core_ref, s32[1]{0:T(128)S(6)} %add.25.start_ref, bf16[8,32,896]{2,1,0:T(8,128)(2,1)} %shard_map.117.half_ref, bf16[8,32,896]{2,1,0:T(8,128)(2,1)} %copy-done.2, bf16[4,32,896]{2,1,0:T(8,128)(2,1)} %copy-done.4), custom_call_target="tpu_custom_call" | custom-call | tf_op jit(solution)/shard_map/pallas_call | solution.py:365
  117.5 8.6 %shard_map.120 = (bf16[8,280,128]{2,1,0:T(8,128)(2,1)}, bf16[8,280,128]{2,1,0:T(8,128)(2,1)}) custom-call(s32[1]{0:T(128)} %bitcast.core_ref, s32[1]{0:T(128)S(6)} %copy.13.count_ref, bf16[8,40,896]{2,1,0:T(8,128)(2,1)S(1)} %all-to-all-done.1.own_ref, bf16[8,40,896]{2,1,0:T(8,128)(2,1)S(1)} %collective-permute-done.1.other_ref, ...), custom_call_target="tpu_custom_call" | custom-call | tf_op jit(solution)/shard_map/pallas_call | solution.py:365
  126.1 3.0 %collective-permute-start.9 = (bf16[8,280,128]{2,1,0:T(8,128)(2,1)}, bf16[8,280,128]{2,1,0:T(8,128)(2,1)S(1)}, u32[]{:S(2)}, u32[]{:S(2)}) collective-permute-start(bf16[8,280,128]{2,1,0:T(8,128)(2,1)} %get-tuple-element.23), channel_id=1, source_target_pairs={{0,1},{1,0},{2,3},{3,2},{4,5},{5,4},{6,7},{7,6},{8,9},{9,8},{10,11... | collective-permute-start | bytes 1720328 | tf_op jit(solution)/shard_map/ppermute | solution.py:354
  129.1 1.8 %collective-permute-done.9.other_ref = bf16[8,280,128]{2,1,0:T(8,128)(2,1)S(1)} collective-permute-done((bf16[8,280,128]{2,1,0:T(8,128)(2,1)}, bf16[8,280,128]{2,1,0:T(8,128)(2,1)S(1)}, u32[]{:S(2)}, u32[]{:S(2)}) %collective-permute-start.9) | collective-permute-done | bytes 573472 | tf_op jit(solution)/shard_map/ppermute | solution.py:354
  130.9 2.0 %shard_map.121 = bf16[8,280,128]{2,1,0:T(8,128)(2,1)} custom-call(bf16[8,280,128]{2,1,0:T(8,128)(2,1)} %get-tuple-element.22.mine_ref, bf16[8,280,128]{2,1,0:T(8,128)(2,1)S(1)} %collective-permute-done.9.other_ref), custom_call_target="tpu_custom_call" | custom-call | tf_op jit(solution)/shard_map/pallas_call | solution.py:365
  132.9 4.6 %all-to-all-start.3 = ((bf16[8,280,128]{2,1,0:T(8,128)(2,1)}), bf16[8,280,128]{2,1,0:T(8,128)(2,1)S(1)}, u32[]{:S(2)}, u32[]{:S(2)}) async-start(bf16[8,280,128]{2,1,0:T(8,128)(2,1)} %shard_map.121), calls=%async_computation.3 | async-start | bytes 1146880 | tf_op jit(solution)/shard_map/all_to_all | solution.py:378
  137.5 3.5 %shard_map.119 = (bf16[160,3584]{1,0:T(8,128)(2,1)}, f32[10,3584]{1,0:T(8,128)}, f32[10,3584]{1,0:T(8,128)}) custom-call(s32[1]{0:T(128)} %bitcast.core_ref, s32[1]{0:T(128)} %bitcast.1.first_ref, s32[1]{0:T(128)S(6)} %copy.13.count_ref, bf16[8,40,896]{2,1,0:T(8,128)(2,1)} %copy-done, bf16[8,40,896]{2,1,0:T(8,128)(2,1)} %copy-done.1, ...), custom_call_target="tpu_custom_call" | custom-call | tf_op jit(solution)/shard_map/pallas_call | solution.py:365
  141.0 15.6 %all-to-all-done.3.got_ref = bf16[8,280,128]{2,1,0:T(8,128)(2,1)S(1)} async-done(((bf16[8,280,128]{2,1,0:T(8,128)(2,1)}), bf16[8,280,128]{2,1,0:T(8,128)(2,1)S(1)}, u32[]{:S(2)}, u32[]{:S(2)}) %all-to-all-start.3) | async-done | bytes 573472 | tf_op jit(solution)/shard_map/all_to_all | solution.py:378
  156.5 1.9 %shard_map.122 = bf16[10,3584]{1,0:T(8,128)(2,1)} custom-call(bf16[8,280,128]{2,1,0:T(8,128)(2,1)S(1)} %all-to-all-done.3.got_ref, f32[10,3584]{1,0:T(8,128)} %get-tuple-element.24.x_ref, f32[10,3584]{1,0:T(8,128)} %get-tuple-element.25.dy_ref, f32[3584]{0:T(1024)} %gain_ref.3), custom_call_target="tpu_custom_call" | custom-call | tf_op jit(solution)/shard_map/pallas_call | solution.py:365
  (22 shorter events, 8.8 us)
Async XLA Ops:
  7.0 14.2 %collective-permute-start = (bf16[8,40,896]{2,1,0:T(8,128)(2,1)}, bf16[8,40,896]{2,1,0:T(8,128)(2,1)S(1)}, u32[]{:S(2)}, u32[]{:S(2)}) collective-permute-start(bf16[8,40,896]{2,1,0:T(8,128)(2,1)} %get-tuple-element.15), channel_id=1, source_target_pairs={{0,1},{1,0},{2,3},{3,2},{4,5},{5,4},{6,7},{7,6},{8,9},{9,8},{10,11... | collective-permute-start | bytes 1720328 | tf_op jit(solution)/shard_map/ppermute | solution.py:354
  23.1 22.5 %all-to-all-start = ((bf16[8,40,896]{2,1,0:T(8,128)(2,1)}), bf16[8,40,896]{2,1,0:T(8,128)(2,1)S(1)}, u32[]{:S(2)}, u32[]{:S(2)}) async-start(bf16[8,40,896]{2,1,0:T(8,128)(2,1)} %shard_map.113), calls=%async_computation | async-start | bytes 1146880 | tf_op jit(solution)/shard_map/all_to_all | solution.py:378
  30.4 3.9 %collective-permute-start.2 = (bf16[8,32,896]{2,1,0:T(8,128)(2,1)}, bf16[8,32,896]{2,1,0:T(8,128)(2,1)S(1)}, u32[]{:S(2)}, u32[]{:S(2)}) collective-permute-start(bf16[8,32,896]{2,1,0:T(8,128)(2,1)} %get-tuple-element.17), channel_id=1, source_target_pairs={{0,1},{1,0},{2,3},{3,2},{4,5},{5,4},{6,7},{7,6},{8,9},{9,8},{10,11... | collective-permute-start | bytes 1376264 | tf_op jit(solution)/shard_map/ppermute | solution.py:354
  45.7 19.9 %all-to-all-start.2 = ((bf16[8,32,896]{2,1,0:T(8,128)(2,1)}), bf16[8,32,896]{2,1,0:T(8,128)(2,1)S(1)}, u32[]{:S(2)}, u32[]{:S(2)}) async-start(bf16[8,32,896]{2,1,0:T(8,128)(2,1)} %shard_map.116), calls=%async_computation.2 | async-start | bytes 917504 | tf_op jit(solution)/shard_map/all_to_all | solution.py:378
  65.6 39.2 %all-to-all-start.1 = ((bf16[8,40,896]{2,1,0:T(8,128)(2,1)}), bf16[8,40,896]{2,1,0:T(8,128)(2,1)S(1)}, u32[]{:S(2)}, u32[]{:S(2)}) async-start(bf16[8,40,896]{2,1,0:T(8,128)(2,1)} %shard_map.114), calls=%async_computation.1 | async-start | bytes 1146880 | tf_op jit(solution)/shard_map/all_to_all | solution.py:460
  69.2 28.7 %copy-start.3 = (bf16[32,896]{1,0:T(8,128)(2,1)}, bf16[32,896]{1,0:T(8,128)(2,1)S(1)}, u32[]{:S(2)}) copy-start(bf16[32,896]{1,0:T(8,128)(2,1)S(1)} %reduce_sum.12) | copy-start | bytes 172036
  69.2 15.0 %collective-permute-start.3 = (bf16[1,32,896]{2,1,0:T(8,128)(2,1)S(1)}, bf16[1,32,896]{2,1,0:T(8,128)(2,1)S(1)}, u32[]{:S(2)}, u32[]{:S(2)}) collective-permute-start(bf16[1,32,896]{2,1,0:T(8,128)(2,1)S(1)} %bitcast.5), channel_id=1, source_target_pairs={{0,6},{2,8},{4,10},{6,12},{8,14},{10,0},{12,2},{14,4},{1,7},{3,9},... | collective-permute-start | bytes 172040 | tf_op jit(solution)/shard_map/ppermute | solution.py:359
  74.3 11.6 %collective-permute-start.4 = (bf16[1,32,896]{2,1,0:T(8,128)(2,1)S(1)}, bf16[1,32,896]{2,1,0:T(8,128)(2,1)S(1)}, u32[]{:S(2)}, u32[]{:S(2)}) collective-permute-start(bf16[1,32,896]{2,1,0:T(8,128)(2,1)S(1)} %bitcast.6), channel_id=1, source_target_pairs={{0,10},{2,12},{4,14},{6,0},{8,2},{10,4},{12,6},{14,8},{1,11},{3,13... | collective-permute-start | bytes 172040 | tf_op jit(solution)/shard_map/ppermute | solution.py:359
  86.0 11.9 %collective-permute-start.5 = (bf16[3,32,896]{2,1,0:T(8,128)(2,1)S(1)}, bf16[3,32,896]{2,1,0:T(8,128)(2,1)S(1)}, u32[]{:S(2)}, u32[]{:S(2)}) collective-permute-start(bf16[3,32,896]{2,1,0:T(8,128)(2,1)S(1)} %pad_maximum_fusion), channel_id=1, source_target_pairs={{0,2},{2,4},{4,6},{6,8},{8,10},{10,12},{12,14},{14,0},{1,3},{3,5},... | collective-permute-start | bytes 516104 | tf_op jit(solution)/shard_map/ppermute | solution.py:359
  92.1 5.8 %collective-permute-start.6 = (bf16[2,32,896]{2,1,0:T(8,128)(2,1)S(1)}, bf16[2,32,896]{2,1,0:T(8,128)(2,1)S(1)}, u32[]{:S(2)}, u32[]{:S(2)}) collective-permute-start(bf16[2,32,896]{2,1,0:T(8,128)(2,1)S(1)} %get-tuple-element.26), channel_id=1, source_target_pairs={{0,14},{2,0},{4,2},{6,4},{8,6},{10,8},{12,10},{14,12},{1,15},{3,1}... | collective-permute-start | bytes 344072 | tf_op jit(solution)/shard_map/ppermute | solution.py:359
  99.6 7.2 %collective-permute-start.7 = (bf16[8,32,896]{2,1,0:T(8,128)(2,1)}, bf16[8,32,896]{2,1,0:T(8,128)(2,1)S(1)}, u32[]{:S(2)}, u32[]{:S(2)}) collective-permute-start(bf16[8,32,896]{2,1,0:T(8,128)(2,1)} %shard_map.117.half_ref), channel_id=1, source_target_pairs={{0,1},{1,0},{2,3},{3,2},{4,5},{5,4},{6,7},{7,6},{8,9},{9,8},{10,11... | collective-permute-start | bytes 1376264 | tf_op jit(solution)/shard_map/ppermute | solution.py:354
  104.9 21.2 %copy-start = (bf16[8,40,896]{2,1,0:T(8,128)(2,1)}, bf16[8,40,896]{2,1,0:T(8,128)(2,1)S(1)}, u32[]{:S(2)}) copy-start(bf16[8,40,896]{2,1,0:T(8,128)(2,1)S(1)} %all-to-all-done.1.own_ref) | copy-start | bytes 1720324
  104.9 12.6 %collective-permute-start.1 = (bf16[8,40,896]{2,1,0:T(8,128)(2,1)S(1)}, bf16[8,40,896]{2,1,0:T(8,128)(2,1)S(1)}, u32[]{:S(2)}, u32[]{:S(2)}) collective-permute-start(bf16[8,40,896]{2,1,0:T(8,128)(2,1)S(1)} %all-to-all-done.1.own_ref), channel_id=1, source_target_pairs={{0,1},{1,0},{2,3},{3,2},{4,5},{5,4},{6,7},{7,6},{8,9},{9,8},{10,11... | collective-permute-start | bytes 1720328 | tf_op jit(solution)/shard_map/ppermute | solution.py:354
  106.8 7.2 %copy-start.2 = (bf16[8,32,896]{2,1,0:T(8,128)(2,1)}, bf16[8,32,896]{2,1,0:T(8,128)(2,1)S(1)}, u32[]{:S(2)}) copy-start(bf16[8,32,896]{2,1,0:T(8,128)(2,1)S(1)} %collective-permute-done.7.other_ref) | copy-start | bytes 1376260
  108.0 6.0 %collective-permute-start.8 = (bf16[4,32,896]{2,1,0:T(8,128)(2,1)S(1)}, bf16[4,32,896]{2,1,0:T(8,128)(2,1)S(1)}, u32[]{:S(2)}, u32[]{:S(2)}) collective-permute-start(bf16[4,32,896]{2,1,0:T(8,128)(2,1)S(1)} %slice_select_fusion), channel_id=1, source_target_pairs={{0,16},{16,32},{32,48},{48,64},{64,80},{80,96},{96,112},{112,128},... | collective-permute-start | bytes 688136 | tf_op jit(solution)/shard_map/ppermute | solution.py:350
  114.0 0.7 copy-start.4
  117.5 8.7 %copy-start.1 = (bf16[8,40,896]{2,1,0:T(8,128)(2,1)}, bf16[8,40,896]{2,1,0:T(8,128)(2,1)S(1)}, u32[]{:S(2)}) copy-start(bf16[8,40,896]{2,1,0:T(8,128)(2,1)S(1)} %collective-permute-done.1.other_ref) | copy-start | bytes 1720324
  126.1 4.8 %collective-permute-start.9 = (bf16[8,280,128]{2,1,0:T(8,128)(2,1)}, bf16[8,280,128]{2,1,0:T(8,128)(2,1)S(1)}, u32[]{:S(2)}, u32[]{:S(2)}) collective-permute-start(bf16[8,280,128]{2,1,0:T(8,128)(2,1)} %get-tuple-element.23), channel_id=1, source_target_pairs={{0,1},{1,0},{2,3},{3,2},{4,5},{5,4},{6,7},{7,6},{8,9},{9,8},{10,11... | collective-permute-start | bytes 1720328 | tf_op jit(solution)/shard_map/ppermute | solution.py:354
  132.9 23.6 %all-to-all-start.3 = ((bf16[8,280,128]{2,1,0:T(8,128)(2,1)}), bf16[8,280,128]{2,1,0:T(8,128)(2,1)S(1)}, u32[]{:S(2)}, u32[]{:S(2)}) async-start(bf16[8,280,128]{2,1,0:T(8,128)(2,1)} %shard_map.121), calls=%async_computation.3 | async-start | bytes 1146880 | tf_op jit(solution)/shard_map/all_to_all | solution.py:378

commit v6 on v3

--- a/solution.py
+++ b/solution.py
@@ -25,6 +25,10 @@
 
 def near(array):
     return pltpu.with_memory_space_constraint(array, pltpu.VMEM)
+
+
+def far_off(array):
+    return pltpu.with_memory_space_constraint(array, pltpu.HBM)
 
 
 def shape(dims, dtype):
@@ -58,14 +62,19 @@
             send_ref[i * COLS + j] = out[half + i * high : half + (i + 1) * high].astype(BF16)
 
 
-def goal_kernel(core_ref, rows_ref, weight_hbm, mine_ref, send_ref, weight_ref, sems):
+def goal_kernel(
+    core_ref, rows_hbm, weight_hbm, mine_ref, send_ref, rows_ref, weight_ref, sems
+):
     wide = mine_ref.shape[2]
+    load_rows = pltpu.make_async_copy(rows_hbm, rows_ref, sems.at[COLS])
+    load_rows.start()
     loads = []
     for j in range(COLS):
         span = slice(j * wide, (j + 1) * wide)
         load = pltpu.make_async_copy(weight_hbm.at[:, span], weight_ref.at[:, span], sems.at[j])
         load.start()
         loads.append(load)
+    load_rows.wait()
     emit_blocks(core_ref[0], rows_ref, weight_ref, mine_ref, send_ref, loads)
 
 
@@ -336,7 +345,7 @@
     return lax.ppermute(block, "core", PAIR)
 
 
-def call(kernel, outs, scratch, *args, far=0, place=VMEM):
+def call(kernel, outs, scratch, *args, far=0, place=VMEM, limit=None):
     specs = [SMEM if a.shape == (1,) else VMEM for a in args]
     specs[len(args) - far :] = [HBM] * far
     return pl.pallas_call(
@@ -345,13 +354,15 @@
         in_specs=specs,
         out_specs=jax.tree.map(lambda _: place, outs),
         scratch_shapes=scratch,
-    )(*args)
-
-
-def spread(mine, send):
+        compiler_params=pltpu.CompilerParams(vmem_limit_bytes=limit),
+    )(*args[: len(args) - far], *map(far_off, args[len(args) - far :]))
+
+
+def spread(mine, send, kept=True):
     out = shape(mine.shape, BF16)
+    first = (near(mine) if kept else mine,)
     scratch = [pltpu.VMEM(out.shape, BF16), pltpu.SemaphoreType.DMA((8,))]
-    chip = call(pair_kernel, out, scratch, mine, near(swap(send)), place=HBM)
+    chip = call(pair_kernel, out, scratch, *first, near(swap(send)), place=HBM)
     return lax.all_to_all(chip, "y", 0, 0)
 
 
@@ -380,11 +391,16 @@
     goal_mine, goal_send = call(
         goal_kernel,
         (parts, parts),
-        [pltpu.VMEM(proj_weight.shape, BF16), pltpu.SemaphoreType.DMA((COLS,))],
+        [
+            pltpu.VMEM(teacher_hidden.shape, BF16),
+            pltpu.VMEM(proj_weight.shape, BF16),
+            pltpu.SemaphoreType.DMA((COLS + 1,)),
+        ],
         core_s,
         teacher_hidden,
         proj_weight,
-        far=1,
+        far=2,
+        limit=24 << 20,
     )
     goal_got = spread(goal_mine, goal_send)
     query, keyval, probs, mine, send = pl.pallas_call(
@@ -407,12 +423,14 @@
         ],
         name="forward",
     )(core_s, student_in, norm_gain, doc_start, w_query, w_keyval, w_out)
-    branch_got = spread(mine, send)
+    branch_got = spread(mine, send, kept=False)
     goal_own = jnp.sum(goal_got.astype(F32), axis=0).astype(BF16)
     goal_rows = lax.all_gather(goal_own, TP)
     earlier = goal_rows.reshape(2, COLS, 2, quarter, wide)[1, :, 1]
     earlier = from_behind(earlier, "seq", 1)
-    goal = call(align_kernel, shape((slots, width), BF16), (), start, goal_rows, earlier)
+    goal = call(
+        align_kernel, shape((slots, width), BF16), (), start, goal_rows, earlier, limit=24 << 20
+    )
     x_block = lax.dynamic_slice(
         student_in,
         (core * (slots // 2) + (ypos // COLS) * high, (ypos % COLS) * wide),
@@ -443,9 +461,10 @@
         row_counts,
         near(y_half),
         near(y_other),
-        goal,
+        near(goal),
         *saved,
         far=len(saved),
+        limit=32 << 20,
     )
     got = spread(mine, send)
     own_rows = slots // 16
@@ -468,8 +487,8 @@
         shape((own_rows, width), BF16),
         [pltpu.VMEM((16, width), F32)],
         near(got),
-        x_own,
-        dy_own,
+        near(x_own),
+        near(dy_own),
         norm_gain,
     )
     return (student_out, grad_in)

time: 158 us -> 153 us (0.968)
  Pallas kernels: 34.5 us -> 25.7 us
  waiting for transfers between devices: 65.8 us -> 68.3 us
    pallas_call x9, Pallas kernels: 28.2 us -> 19.4 us  [call(): pl.pallas_call(kernel, out_shape=outs, in_specs=specs, out_specs=jax.tree...]
    all_to_all x3, waiting for transfers between devices: 37.9 us -> 40.9 us  [spread(): return lax.all_to_all(chip, 'y', 0, 0)]
  transfers between devices with their start and end apart: 9 -> 9, of which waited for: 8 -> 8; matrix products, arithmetic and copies ran while one was open for 1% -> 1% of each run, Pallas kernels for 9% -> 6%
where the time goes in v6:
time: 153 us; the launch traced here: 152 us
  waiting for transfers between devices  68.3 us (45%)
  starting transfers between devices  35.1 us (23%)
  Pallas kernels  25.7 us (17%)
  blocking collectives  17.2 us (11%)
  local copies, waits for them, and re-layouts  3.43 us (2%)
  between operations  2.19 us (1%)
    all_to_all x3, waiting for transfers between devices, spread(): return lax.all_to_all(chip, 'y', 0, 0)  40.9 us
    ppermute x4, starting transfers between devices, swap(): return lax.ppermute(block, 'core', PAIR)  19.7 us
    pallas_call x9, Pallas kernels, call(): pl.pallas_call(kernel, out_shape=outs, in_specs=specs, out_specs=jax.tree...  19.4 us
    all_to_all x1, waiting for transfers between devices, body(): y_half = lax.all_to_all(y_own, 'y', 0, 0)  18.9 us
    all_gather x1, blocking collectives, body(): goal_rows = lax.all_gather(goal_own, TP)  17.2 us
    all_to_all x3, starting transfers between devices, spread(): return lax.all_to_all(chip, 'y', 0, 0)  10.6 us
    pallas_call x1, Pallas kernels, body(): pl.pallas_call(forward_kernel, out_shape=(shape((slots, QPK * HD), BF16),...  6.32 us
    ppermute x4, waiting for transfers between devices, swap(): return lax.ppermute(block, 'core', PAIR)  4.8 us
  transfers between devices with their start and end apart: 9, of which 8 were waited for; matrix products, arithmetic and copies ran while one was open for 1% of the time, Pallas kernels for 6%

profile of v6, /device:TPU:1, one launch (start us, length us, event | category | flops | bytes accessed | tf_op | source)
XLA Modules:
  0.0 152.0 jit_solution(6090876689259575918)
XLA Ops:
  0.6 6.3 %forward.1 = (bf16[160,256]{1,0:T(8,128)(2,1)}, bf16[160,256]{1,0:T(8,128)(2,1)}, f32[2,160,160]{2,1,0:T(8,128)}, bf16[8,40,896]{2,1,0:T(8,128)(2,1)}, bf16[8,40,896]{2,1,0:T(8,128)(2,1)}) custom-call(s32[1]{0:T(128)} %bitcast.core_ref, bf16[160,3584]{1,0:T(8,128)(2,1)} %x_ref.3, f32[3584]{0:T(1024)} %gain_ref.3, s32[160]{0:T(256)} %starts_ref.1, ...), custom_call_target="tpu_custom_call" | custom-call | tf_op jit(solution)/shard_map/forward/pallas_call | solution.py:406
  7.0 12.4 %collective-permute-start = (bf16[8,40,896]{2,1,0:T(8,128)(2,1)}, bf16[8,40,896]{2,1,0:T(8,128)(2,1)S(1)}, u32[]{:S(2)}, u32[]{:S(2)}) collective-permute-start(bf16[8,40,896]{2,1,0:T(8,128)(2,1)} %get-tuple-element.15), channel_id=1, source_target_pairs={{0,1},{1,0},{2,3},{3,2},{4,5},{5,4},{6,7},{7,6},{8,9},{9,8},{10,11... | collective-permute-start | bytes 1720328 | tf_op jit(solution)/shard_map/ppermute | solution.py:345
  19.4 1.8 %collective-permute-done.other_ref = bf16[8,40,896]{2,1,0:T(8,128)(2,1)S(1)} collective-permute-done((bf16[8,40,896]{2,1,0:T(8,128)(2,1)}, bf16[8,40,896]{2,1,0:T(8,128)(2,1)S(1)}, u32[]{:S(2)}, u32[]{:S(2)}) %collective-permute-start) | collective-permute-done | bytes 573472 | tf_op jit(solution)/shard_map/ppermute | solution.py:345
  21.2 2.0 %shard_map.113 = bf16[8,40,896]{2,1,0:T(8,128)(2,1)} custom-call(bf16[8,40,896]{2,1,0:T(8,128)(2,1)} %get-tuple-element.14.mine_ref, bf16[8,40,896]{2,1,0:T(8,128)(2,1)S(1)} %collective-permute-done.other_ref), custom_call_target="tpu_custom_call" | custom-call | tf_op jit(solution)/shard_map/pallas_call | solution.py:351
  23.1 3.5 %all-to-all-start = ((bf16[8,40,896]{2,1,0:T(8,128)(2,1)}), bf16[8,40,896]{2,1,0:T(8,128)(2,1)S(1)}, u32[]{:S(2)}, u32[]{:S(2)}) async-start(bf16[8,40,896]{2,1,0:T(8,128)(2,1)} %shard_map.113), calls=%async_computation | async-start | bytes 1146880 | tf_op jit(solution)/shard_map/all_to_all | solution.py:366
  26.7 2.0 %shard_map.115 = (bf16[8,32,896]{2,1,0:T(8,128)(2,1)S(1)}, bf16[8,32,896]{2,1,0:T(8,128)(2,1)S(1)}) custom-call(s32[1]{0:T(128)} %bitcast.core_ref, bf16[128,256]{1,0:T(8,128)(2,1)} %rows_hbm.1, bf16[256,3584]{1,0:T(8,128)(2,1)} %weight_hbm.1), custom_call_target="tpu_custom_call" | custom-call | tf_op jit(solution)/shard_map/pallas_call | solution.py:351
  28.7 2.3 %collective-permute-start.2 = (bf16[8,32,896]{2,1,0:T(8,128)(2,1)S(1)}, bf16[8,32,896]{2,1,0:T(8,128)(2,1)S(1)}, u32[]{:S(2)}, u32[]{:S(2)}) collective-permute-start(bf16[8,32,896]{2,1,0:T(8,128)(2,1)S(1)} %get-tuple-element.17), channel_id=1, source_target_pairs={{0,1},{1,0},{2,3},{3,2},{4,5},{5,4},{6,7},{7,6},{8,9},{9,8},{10,11... | collective-permute-start | bytes 1376264 | tf_op jit(solution)/shard_map/ppermute | solution.py:345
  31.0 1.4 collective-permute-done.2.other_ref
  32.5 0.9 shard_map.116
  33.3 12.3 %all-to-all-done.got_ref = bf16[8,40,896]{2,1,0:T(8,128)(2,1)S(1)} async-done(((bf16[8,40,896]{2,1,0:T(8,128)(2,1)}), bf16[8,40,896]{2,1,0:T(8,128)(2,1)S(1)}, u32[]{:S(2)}, u32[]{:S(2)}) %all-to-all-start) | async-done | bytes 573472 | tf_op jit(solution)/shard_map/all_to_all | solution.py:366
  45.7 3.5 %all-to-all-start.2 = ((bf16[8,32,896]{2,1,0:T(8,128)(2,1)}), bf16[8,32,896]{2,1,0:T(8,128)(2,1)S(1)}, u32[]{:S(2)}, u32[]{:S(2)}) async-start(bf16[8,32,896]{2,1,0:T(8,128)(2,1)} %shard_map.116), calls=%async_computation.2 | async-start | bytes 917504 | tf_op jit(solution)/shard_map/all_to_all | solution.py:366
  49.2 1.5 %dynamic_slice.3.x_ref = bf16[40,896]{1,0:T(8,128)(2,1)} dynamic-slice(bf16[160,3584]{1,0:T(8,128)(2,1)} %x_ref.3, s32[]{:T(128)S(6)} %select_n.18, s32[]{:T(128)S(6)} %select_n.20), dynamic_slice_sizes={40,896} | dynamic-slice | bytes 143364 | tf_op jit(solution)/shard_map/dynamic_slice | solution.py:434
  50.7 1.8 %shard_map.114 = bf16[8,40,896]{2,1,0:T(8,128)(2,1)} custom-call(bf16[8,40,896]{2,1,0:T(8,128)(2,1)S(1)} %all-to-all-done.got_ref, bf16[40,896]{1,0:T(8,128)(2,1)} %dynamic_slice.3.x_ref), custom_call_target="tpu_custom_call" | custom-call | tf_op jit(solution)/shard_map/pallas_call | solution.py:351
  52.6 13.1 %all-to-all-done.2 = bf16[8,32,896]{2,1,0:T(8,128)(2,1)S(1)} async-done(((bf16[8,32,896]{2,1,0:T(8,128)(2,1)}), bf16[8,32,896]{2,1,0:T(8,128)(2,1)S(1)}, u32[]{:S(2)}, u32[]{:S(2)}) %all-to-all-start.2) | async-done | bytes 458784 | tf_op jit(solution)/shard_map/all_to_all | solution.py:366
  65.6 3.5 %all-to-all-start.1 = ((bf16[8,40,896]{2,1,0:T(8,128)(2,1)}), bf16[8,40,896]{2,1,0:T(8,128)(2,1)S(1)}, u32[]{:S(2)}, u32[]{:S(2)}) async-start(bf16[8,40,896]{2,1,0:T(8,128)(2,1)} %shard_map.114), calls=%async_computation.1 | async-start | bytes 1146880 | tf_op jit(solution)/shard_map/all_to_all | solution.py:447
  69.2 0.1 reduce_sum.12
  69.2 18.9 %all-to-all-done.1.own_ref = bf16[8,40,896]{2,1,0:T(8,128)(2,1)S(1)} async-done(((bf16[8,40,896]{2,1,0:T(8,128)(2,1)}), bf16[8,40,896]{2,1,0:T(8,128)(2,1)S(1)}, u32[]{:S(2)}, u32[]{:S(2)}) %all-to-all-start.1) | async-done | bytes 573472 | tf_op jit(solution)/shard_map/all_to_all | solution.py:447
  88.1 2.4 %collective-permute-start.1 = (bf16[8,40,896]{2,1,0:T(8,128)(2,1)S(1)}, bf16[8,40,896]{2,1,0:T(8,128)(2,1)S(1)}, u32[]{:S(2)}, u32[]{:S(2)}) collective-permute-start(bf16[8,40,896]{2,1,0:T(8,128)(2,1)S(1)} %all-to-all-done.1.own_ref), channel_id=1, source_target_pairs={{0,1},{1,0},{2,3},{3,2},{4,5},{5,4},{6,7},{7,6},{8,9},{9,8},{10,11... | collective-permute-start | bytes 1720328 | tf_op jit(solution)/shard_map/ppermute | solution.py:345
  90.5 17.2 %all-gather = bf16[512,896]{1,0:T(8,128)(2,1)S(1)} all-gather(bf16[32,896]{1,0:T(8,128)(2,1)S(1)} %reduce_sum.12), channel_id=2, replica_groups=mesh['seq'=48,'y'=8,'core'=2] {'y','core'}, dimensions={0}, use_global_device_ids=true | all-gather | bytes 974848 | tf_op jit(solution)/shard_map/all_gather | solution.py:428
  107.7 1.3 collective-permute-start.3
  110.3 3.7 %collective-permute-done.3.earlier_ref = bf16[4,32,896]{2,1,0:T(8,128)(2,1)S(1)} collective-permute-done((bf16[4,32,896]{2,1,0:T(8,128)(2,1)S(1)}, bf16[4,32,896]{2,1,0:T(8,128)(2,1)S(1)}, u32[]{:S(2)}, u32[]{:S(2)}) %collective-permute-start.3) | collective-permute-done | bytes 229408 | tf_op jit(solution)/shard_map/ppermute | solution.py:341
  114.1 0.5 shard_map.117.goal_ref
  114.6 6.2 %shard_map.119 = (bf16[8,280,128]{2,1,0:T(8,128)(2,1)S(1)}, bf16[8,280,128]{2,1,0:T(8,128)(2,1)S(1)}) custom-call(s32[1]{0:T(128)} %bitcast.core_ref, s32[1]{0:T(128)S(6)} %copy.15.count_ref, bf16[8,40,896]{2,1,0:T(8,128)(2,1)S(1)} %all-to-all-done.1.own_ref, bf16[8,40,896]{2,1,0:T(8,128)(2,1)S(1)} %collective-permute-done.1.other_ref, ...), custom_call_target="tpu_custom_call" | custom-call | tf_op jit(solution)/shard_map/pallas_call | solution.py:351
  120.9 2.6 %collective-permute-start.4 = (bf16[8,280,128]{2,1,0:T(8,128)(2,1)S(1)}, bf16[8,280,128]{2,1,0:T(8,128)(2,1)S(1)}, u32[]{:S(2)}, u32[]{:S(2)}) collective-permute-start(bf16[8,280,128]{2,1,0:T(8,128)(2,1)S(1)} %get-tuple-element.23), channel_id=1, source_target_pairs={{0,1},{1,0},{2,3},{3,2},{4,5},{5,4},{6,7},{7,6},{8,9},{9,8},{10,11... | collective-permute-start | bytes 1720328 | tf_op jit(solution)/shard_map/ppermute | solution.py:345
  123.5 1.6 %collective-permute-done.4.other_ref = bf16[8,280,128]{2,1,0:T(8,128)(2,1)S(1)} collective-permute-done((bf16[8,280,128]{2,1,0:T(8,128)(2,1)S(1)}, bf16[8,280,128]{2,1,0:T(8,128)(2,1)S(1)}, u32[]{:S(2)}, u32[]{:S(2)}) %collective-permute-start.4) | collective-permute-done | bytes 573472 | tf_op jit(solution)/shard_map/ppermute | solution.py:345
  125.1 0.9 shard_map.120
  126.0 3.5 %all-to-all-start.3 = ((bf16[8,280,128]{2,1,0:T(8,128)(2,1)}), bf16[8,280,128]{2,1,0:T(8,128)(2,1)S(1)}, u32[]{:S(2)}, u32[]{:S(2)}) async-start(bf16[8,280,128]{2,1,0:T(8,128)(2,1)} %shard_map.120), calls=%async_computation.3 | async-start | bytes 1146880 | tf_op jit(solution)/shard_map/all_to_all | solution.py:366
  129.6 3.5 %shard_map.118 = (bf16[160,3584]{1,0:T(8,128)(2,1)}, f32[10,3584]{1,0:T(8,128)}, f32[10,3584]{1,0:T(8,128)}) custom-call(s32[1]{0:T(128)} %bitcast.core_ref, s32[1]{0:T(128)} %bitcast.1.first_ref, s32[1]{0:T(128)S(6)} %copy.15.count_ref, bf16[8,40,896]{2,1,0:T(8,128)(2,1)} %copy-done.1, bf16[8,40,896]{2,1,0:T(8,128)(2,1)} %copy-done.2, ...), custom_call_target="tpu_custom_call" | custom-call | tf_op jit(solution)/shard_map/pallas_call | solution.py:351
  133.0 15.5 %all-to-all-done.3.got_ref = bf16[8,280,128]{2,1,0:T(8,128)(2,1)S(1)} async-done(((bf16[8,280,128]{2,1,0:T(8,128)(2,1)}), bf16[8,280,128]{2,1,0:T(8,128)(2,1)S(1)}, u32[]{:S(2)}, u32[]{:S(2)}) %all-to-all-start.3) | async-done | bytes 573472 | tf_op jit(solution)/shard_map/all_to_all | solution.py:366
  148.5 0.9 copy-done.3
  149.4 0.9 copy-done.4
  150.4 1.6 %shard_map.121 = bf16[10,3584]{1,0:T(8,128)(2,1)} custom-call(bf16[8,280,128]{2,1,0:T(8,128)(2,1)S(1)} %all-to-all-done.3.got_ref, f32[10,3584]{1,0:T(8,128)S(1)} %copy-done.4, f32[10,3584]{1,0:T(8,128)S(1)} %copy-done.3, f32[3584]{0:T(1024)} %gain_ref.3), custom_call_target="tpu_custom_call" | custom-call | tf_op jit(solution)/shard_map/pallas_call | solution.py:351
  (10 shorter events, 0.0 us)
Async XLA Ops:
  7.0 14.2 %collective-permute-start = (bf16[8,40,896]{2,1,0:T(8,128)(2,1)}, bf16[8,40,896]{2,1,0:T(8,128)(2,1)S(1)}, u32[]{:S(2)}, u32[]{:S(2)}) collective-permute-start(bf16[8,40,896]{2,1,0:T(8,128)(2,1)} %get-tuple-element.15), channel_id=1, source_target_pairs={{0,1},{1,0},{2,3},{3,2},{4,5},{5,4},{6,7},{7,6},{8,9},{9,8},{10,11... | collective-permute-start | bytes 1720328 | tf_op jit(solution)/shard_map/ppermute | solution.py:345
  23.1 22.5 %all-to-all-start = ((bf16[8,40,896]{2,1,0:T(8,128)(2,1)}), bf16[8,40,896]{2,1,0:T(8,128)(2,1)S(1)}, u32[]{:S(2)}, u32[]{:S(2)}) async-start(bf16[8,40,896]{2,1,0:T(8,128)(2,1)} %shard_map.113), calls=%async_computation | async-start | bytes 1146880 | tf_op jit(solution)/shard_map/all_to_all | solution.py:366
  28.7 3.7 %collective-permute-start.2 = (bf16[8,32,896]{2,1,0:T(8,128)(2,1)S(1)}, bf16[8,32,896]{2,1,0:T(8,128)(2,1)S(1)}, u32[]{:S(2)}, u32[]{:S(2)}) collective-permute-start(bf16[8,32,896]{2,1,0:T(8,128)(2,1)S(1)} %get-tuple-element.17), channel_id=1, source_target_pairs={{0,1},{1,0},{2,3},{3,2},{4,5},{5,4},{6,7},{7,6},{8,9},{9,8},{10,11... | collective-permute-start | bytes 1376264 | tf_op jit(solution)/shard_map/ppermute | solution.py:345
  45.7 19.9 %all-to-all-start.2 = ((bf16[8,32,896]{2,1,0:T(8,128)(2,1)}), bf16[8,32,896]{2,1,0:T(8,128)(2,1)S(1)}, u32[]{:S(2)}, u32[]{:S(2)}) async-start(bf16[8,32,896]{2,1,0:T(8,128)(2,1)} %shard_map.116), calls=%async_computation.2 | async-start | bytes 917504 | tf_op jit(solution)/shard_map/all_to_all | solution.py:366
  65.6 22.5 %all-to-all-start.1 = ((bf16[8,40,896]{2,1,0:T(8,128)(2,1)}), bf16[8,40,896]{2,1,0:T(8,128)(2,1)S(1)}, u32[]{:S(2)}, u32[]{:S(2)}) async-start(bf16[8,40,896]{2,1,0:T(8,128)(2,1)} %shard_map.114), calls=%async_computation.1 | async-start | bytes 1146880 | tf_op jit(solution)/shard_map/all_to_all | solution.py:447
  88.1 26.5 %copy-start.1 = (bf16[8,40,896]{2,1,0:T(8,128)(2,1)}, bf16[8,40,896]{2,1,0:T(8,128)(2,1)S(1)}, u32[]{:S(2)}) copy-start(bf16[8,40,896]{2,1,0:T(8,128)(2,1)S(1)} %all-to-all-done.1.own_ref) | copy-start | bytes 1720324
  88.1 26.5 %collective-permute-start.1 = (bf16[8,40,896]{2,1,0:T(8,128)(2,1)S(1)}, bf16[8,40,896]{2,1,0:T(8,128)(2,1)S(1)}, u32[]{:S(2)}, u32[]{:S(2)}) collective-permute-start(bf16[8,40,896]{2,1,0:T(8,128)(2,1)S(1)} %all-to-all-done.1.own_ref), channel_id=1, source_target_pairs={{0,1},{1,0},{2,3},{3,2},{4,5},{5,4},{6,7},{7,6},{8,9},{9,8},{10,11... | collective-permute-start | bytes 1720328 | tf_op jit(solution)/shard_map/ppermute | solution.py:345
  107.7 6.4 %collective-permute-start.3 = (bf16[4,32,896]{2,1,0:T(8,128)(2,1)S(1)}, bf16[4,32,896]{2,1,0:T(8,128)(2,1)S(1)}, u32[]{:S(2)}, u32[]{:S(2)}) collective-permute-start(bf16[4,32,896]{2,1,0:T(8,128)(2,1)S(1)} %slice_bitcast_fusion), channel_id=1, source_target_pairs={{0,16},{16,32},{32,48},{48,64},{64,80},{80,96},{96,112},{112,128},... | collective-permute-start | bytes 688136 | tf_op jit(solution)/shard_map/ppermute | solution.py:341
  114.6 6.3 %copy-start = (bf16[160,3584]{1,0:T(8,128)(2,1)}, bf16[160,3584]{1,0:T(8,128)(2,1)S(1)}, u32[]{:S(2)}) copy-start(bf16[160,3584]{1,0:T(8,128)(2,1)S(1)} %shard_map.117.goal_ref) | copy-start | bytes 3440644
  114.6 6.3 %copy-start.2 = (bf16[8,40,896]{2,1,0:T(8,128)(2,1)}, bf16[8,40,896]{2,1,0:T(8,128)(2,1)S(1)}, u32[]{:S(2)}) copy-start(bf16[8,40,896]{2,1,0:T(8,128)(2,1)S(1)} %collective-permute-done.1.other_ref) | copy-start | bytes 1720324
  120.9 4.2 %collective-permute-start.4 = (bf16[8,280,128]{2,1,0:T(8,128)(2,1)S(1)}, bf16[8,280,128]{2,1,0:T(8,128)(2,1)S(1)}, u32[]{:S(2)}, u32[]{:S(2)}) collective-permute-start(bf16[8,280,128]{2,1,0:T(8,128)(2,1)S(1)} %get-tuple-element.23), channel_id=1, source_target_pairs={{0,1},{1,0},{2,3},{3,2},{4,5},{5,4},{6,7},{7,6},{8,9},{9,8},{10,11... | collective-permute-start | bytes 1720328 | tf_op jit(solution)/shard_map/ppermute | solution.py:345
  126.0 22.5 %all-to-all-start.3 = ((bf16[8,280,128]{2,1,0:T(8,128)(2,1)}), bf16[8,280,128]{2,1,0:T(8,128)(2,1)S(1)}, u32[]{:S(2)}, u32[]{:S(2)}) async-start(bf16[8,280,128]{2,1,0:T(8,128)(2,1)} %shard_map.120), calls=%async_computation.3 | async-start | bytes 1146880 | tf_op jit(solution)/shard_map/all_to_all | solution.py:366
  148.5 0.9 copy-start.3
  149.4 0.9 copy-start.4

commit v7 on v6

--- a/solution.py
+++ b/solution.py
@@ -88,7 +88,7 @@
         store.wait()
 
 
-def align_kernel(start_ref, own_ref, earlier_ref, out_ref):
+def align_kernel(start_ref, own_ref, earlier_ref, out_ref, norm_ref):
     slots = out_ref.shape[0]
     wide = own_ref.shape[2]
     row = lax.broadcasted_iota(jnp.int32, (slots, slots), 0)
@@ -100,16 +100,18 @@
             for i in range(2):
                 bands.append(own_ref[2 * (i * COLS + j) + c])
         rows = jnp.concatenate(bands, axis=0)
-        out_ref[:, j * wide : (j + 1) * wide] = nn(pick, rows).astype(BF16)
-
-
-def direction(y, t, live, width):
+        goal = nn(pick, rows)
+        out_ref[:, j * wide : (j + 1) * wide] = goal.astype(BF16)
+        part = jnp.sum(goal * goal, axis=1, keepdims=True)
+        bsum = part if j == 0 else bsum + part
+    norm_ref[...] = lax.rsqrt(bsum + epsilon)
+
+
+def direction(y, t, norm, live, width):
     asum = sum(jnp.sum(a * a, axis=1, keepdims=True) for a in y) + epsilon
-    bsum = sum(jnp.sum(a * a, axis=1, keepdims=True) for a in t) + epsilon
     dots = sum(jnp.sum(a * b, axis=1, keepdims=True) for a, b in zip(y, t))
-    both = lax.rsqrt(asum * bsum)
-    factor = -math.sqrt(width) * live
-    return factor * both, factor * (dots * both) / asum
+    factor = -math.sqrt(width) * live * (lax.rsqrt(asum) * norm)
+    return factor, factor * dots / asum
 
 
 def finish_kernel(
@@ -131,9 +133,10 @@
     pick = (col == row).astype(BF16)
     y = nn(pick, student_ref[...])
     t = nn(pick, goal_ref[...])
+    norm = lax.rsqrt(jnp.sum(t * t, axis=1, keepdims=True) + epsilon)
     x_own_ref[...] = nn(pick, x_ref[...])[:own_rows]
     place = lax.broadcasted_iota(jnp.int32, (16, 1), 0) + first_ref[0]
-    t_scale, y_scale = direction([y], [t], (place < count_ref[0]).astype(F32), width)
+    t_scale, y_scale = direction([y], [t], norm, (place < count_ref[0]).astype(F32), width)
     dy_ref[...] = (t * t_scale - y * y_scale)[:own_rows]
 
 
@@ -211,6 +214,7 @@
     own_ref,
     other_ref,
     goal_ref,
+    norm_ref,
     w_out_hbm,
     probs_hbm,
     keyval_hbm,
@@ -227,6 +231,7 @@
     w_keyval,
     dyb_ref,
     grads_ref,
+    d_attn_ref,
     sems,
 ):
     loads = [
@@ -248,21 +253,25 @@
     count = count_ref[0]
     slots, width = goal_ref.shape
     high, wide = own_ref.shape[1:]
-    for c in range(2):
+    half = slots // 2
+    for c, ref in ((0, own_ref), (1, other_ref)):
+        base = pl.multiple_of((core if c == 0 else 1 - core) * half, 16)
         for i in range(2):
-            first = (2 * c + i) * high
-            y, t = [], []
+            rows = pl.ds(pl.multiple_of(base + i * high, 8), high)
+            y = [ref[i * COLS + j].astype(F32) for j in range(COLS)]
+            t = [goal_ref[rows, j * wide : (j + 1) * wide].astype(F32) for j in range(COLS)]
+            place = lax.broadcasted_iota(jnp.int32, (high, 1), 0) + base + i * high
+            live = (place < count).astype(F32)
+            to_t, to_y = direction(y, t, norm_ref[rows, :], live, width)
+            first = c * half + i * high
             for j in range(COLS):
-                n = i * COLS + j
-                y.append(jnp.where(core == c, own_ref[n].astype(F32), other_ref[n].astype(F32)))
-                t.append(goal_ref[first : first + high, j * wide : (j + 1) * wide].astype(F32))
-            place = lax.broadcasted_iota(jnp.int32, (high, 1), 0) + first
-            t_scale, y_scale = direction(y, t, (place < count).astype(F32), width)
-            for j in range(COLS):
-                dy = t[j] * t_scale - y[j] * y_scale
+                dy = t[j] * to_t - y[j] * to_y
                 dyb_ref[first : first + high, j * wide : (j + 1) * wide] = dy.astype(BF16)
     loads[0].wait()
-    d_attn = nt(dyb_ref[...], w_out[...]).astype(BF16)
+    d_rows = nt(dyb_ref[...], w_out[...]).astype(BF16)
+    d_attn_ref[pl.ds(pl.multiple_of(core * half, 16), half), :] = d_rows[:half]
+    d_attn_ref[pl.ds(pl.multiple_of((1 - core) * half, 16), half), :] = d_rows[half:]
+    d_attn = d_attn_ref[...]
     for load in loads[1:4]:
         load.wait()
     keys = keyval_ref[:, :HD]
@@ -282,7 +291,6 @@
         d_values = d_value if d_values is None else d_values + d_value
     grads_ref[:, QPK * HD : (QPK + 1) * HD] = d_keys.astype(BF16)
     grads_ref[:, (QPK + 1) * HD :] = d_values.astype(BF16)
-    half = slots // 2
     row = lax.broadcasted_iota(jnp.int32, (slots, slots), 0)
     col = lax.broadcasted_iota(jnp.int32, (slots, slots), 1)
     sent = (row >= half).astype(jnp.int32)
@@ -428,8 +436,14 @@
     goal_rows = lax.all_gather(goal_own, TP)
     earlier = goal_rows.reshape(2, COLS, 2, quarter, wide)[1, :, 1]
     earlier = from_behind(earlier, "seq", 1)
-    goal = call(
-        align_kernel, shape((slots, width), BF16), (), start, goal_rows, earlier, limit=24 << 20
+    goal, norm = call(
+        align_kernel,
+        (shape((slots, width), BF16), shape((slots, 1), F32)),
+        (),
+        start,
+        goal_rows,
+        earlier,
+        limit=24 << 20,
     )
     x_block = lax.dynamic_slice(
         student_in,
@@ -455,6 +469,7 @@
         + [
             pltpu.VMEM((slots, width), BF16),
             pltpu.VMEM((slots, (QPK + 2) * HD), BF16),
+            pltpu.VMEM((slots, QPK * HD), BF16),
             pltpu.SemaphoreType.DMA((len(saved),)),
         ],
         core_s,
@@ -462,6 +477,7 @@
         near(y_half),
         near(y_other),
         near(goal),
+        norm,
         *saved,
         far=len(saved),
         limit=32 << 20,
@@ -487,8 +503,8 @@
         shape((own_rows, width), BF16),
         [pltpu.VMEM((16, width), F32)],
         near(got),
-        near(x_own),
-        near(dy_own),
+        x_own,
+        dy_own,
         norm_gain,
     )
     return (student_out, grad_in)

time: 153 us -> 151 us (0.987)
  local copies, waits for them, and re-layouts: 3.43 us -> 1.57 us
    unnamed x10 -> x6, local copies, waits for them, and re-layouts: 1.89 us -> 0.01 us
where the time goes in v7:
time: 151 us; the launch traced here: 150 us
  waiting for transfers between devices  68.3 us (45%)
  starting transfers between devices  35.1 us (23%)
  Pallas kernels  25.8 us (17%)
  blocking collectives  17.2 us (11%)
  between operations  2.18 us (1%)
  local copies, waits for them, and re-layouts  1.57 us (1%)
    all_to_all x3, waiting for transfers between devices, spread(): return lax.all_to_all(chip, 'y', 0, 0)  40.9 us
    ppermute x4, starting transfers between devices, swap(): return lax.ppermute(block, 'core', PAIR)  19.7 us
    pallas_call x9, Pallas kernels, call(): pl.pallas_call(kernel, out_shape=outs, in_specs=specs, out_specs=jax.tree...  19.5 us
    all_to_all x1, waiting for transfers between devices, body(): y_half = lax.all_to_all(y_own, 'y', 0, 0)  18.9 us
    all_gather x1, blocking collectives, body(): goal_rows = lax.all_gather(goal_own, TP)  17.2 us
    all_to_all x3, starting transfers between devices, spread(): return lax.all_to_all(chip, 'y', 0, 0)  10.6 us
    pallas_call x1, Pallas kernels, body(): pl.pallas_call(forward_kernel, out_shape=(shape((slots, QPK * HD), BF16),...  6.32 us
    ppermute x4, waiting for transfers between devices, swap(): return lax.ppermute(block, 'core', PAIR)  4.81 us
  transfers between devices with their start and end apart: 9, of which 8 were waited for; matrix products, arithmetic and copies ran while one was open for 1% of the time, Pallas kernels for 6%

profile of v7, /device:TPU:1, one launch (start us, length us, event | category | flops | bytes accessed | tf_op | source)
XLA Modules:
  0.0 150.2 jit_solution(17012888149189195584)
XLA Ops:
  0.6 6.3 %forward.1 = (bf16[160,256]{1,0:T(8,128)(2,1)}, bf16[160,256]{1,0:T(8,128)(2,1)}, f32[2,160,160]{2,1,0:T(8,128)}, bf16[8,40,896]{2,1,0:T(8,128)(2,1)}, bf16[8,40,896]{2,1,0:T(8,128)(2,1)}) custom-call(s32[1]{0:T(128)} %bitcast.core_ref, bf16[160,3584]{1,0:T(8,128)(2,1)} %x_ref.3, f32[3584]{0:T(1024)} %gain_ref.3, s32[160]{0:T(256)} %starts_ref.1, ...), custom_call_target="tpu_custom_call" | custom-call | tf_op jit(solution)/shard_map/forward/pallas_call | solution.py:414
  7.0 12.4 %collective-permute-start = (bf16[8,40,896]{2,1,0:T(8,128)(2,1)}, bf16[8,40,896]{2,1,0:T(8,128)(2,1)S(1)}, u32[]{:S(2)}, u32[]{:S(2)}) collective-permute-start(bf16[8,40,896]{2,1,0:T(8,128)(2,1)} %get-tuple-element.17), channel_id=1, source_target_pairs={{0,1},{1,0},{2,3},{3,2},{4,5},{5,4},{6,7},{7,6},{8,9},{9,8},{10,11... | collective-permute-start | bytes 1720328 | tf_op jit(solution)/shard_map/ppermute | solution.py:353
  19.4 1.8 %collective-permute-done.other_ref = bf16[8,40,896]{2,1,0:T(8,128)(2,1)S(1)} collective-permute-done((bf16[8,40,896]{2,1,0:T(8,128)(2,1)}, bf16[8,40,896]{2,1,0:T(8,128)(2,1)S(1)}, u32[]{:S(2)}, u32[]{:S(2)}) %collective-permute-start) | collective-permute-done | bytes 573472 | tf_op jit(solution)/shard_map/ppermute | solution.py:353
  21.2 2.0 %shard_map.113 = bf16[8,40,896]{2,1,0:T(8,128)(2,1)} custom-call(bf16[8,40,896]{2,1,0:T(8,128)(2,1)} %get-tuple-element.16.mine_ref, bf16[8,40,896]{2,1,0:T(8,128)(2,1)S(1)} %collective-permute-done.other_ref), custom_call_target="tpu_custom_call" | custom-call | tf_op jit(solution)/shard_map/pallas_call | solution.py:359
  23.1 3.5 %all-to-all-start = ((bf16[8,40,896]{2,1,0:T(8,128)(2,1)}), bf16[8,40,896]{2,1,0:T(8,128)(2,1)S(1)}, u32[]{:S(2)}, u32[]{:S(2)}) async-start(bf16[8,40,896]{2,1,0:T(8,128)(2,1)} %shard_map.113), calls=%async_computation | async-start | bytes 1146880 | tf_op jit(solution)/shard_map/all_to_all | solution.py:374
  26.7 2.0 %shard_map.115 = (bf16[8,32,896]{2,1,0:T(8,128)(2,1)S(1)}, bf16[8,32,896]{2,1,0:T(8,128)(2,1)S(1)}) custom-call(s32[1]{0:T(128)} %bitcast.core_ref, bf16[128,256]{1,0:T(8,128)(2,1)} %rows_hbm.1, bf16[256,3584]{1,0:T(8,128)(2,1)} %weight_hbm.1), custom_call_target="tpu_custom_call" | custom-call | tf_op jit(solution)/shard_map/pallas_call | solution.py:359
  28.7 2.3 %collective-permute-start.2 = (bf16[8,32,896]{2,1,0:T(8,128)(2,1)S(1)}, bf16[8,32,896]{2,1,0:T(8,128)(2,1)S(1)}, u32[]{:S(2)}, u32[]{:S(2)}) collective-permute-start(bf16[8,32,896]{2,1,0:T(8,128)(2,1)S(1)} %get-tuple-element.19), channel_id=1, source_target_pairs={{0,1},{1,0},{2,3},{3,2},{4,5},{5,4},{6,7},{7,6},{8,9},{9,8},{10,11... | collective-permute-start | bytes 1376264 | tf_op jit(solution)/shard_map/ppermute | solution.py:353
  31.0 1.4 collective-permute-done.2.other_ref
  32.5 0.9 shard_map.116
  33.3 12.3 %all-to-all-done.got_ref = bf16[8,40,896]{2,1,0:T(8,128)(2,1)S(1)} async-done(((bf16[8,40,896]{2,1,0:T(8,128)(2,1)}), bf16[8,40,896]{2,1,0:T(8,128)(2,1)S(1)}, u32[]{:S(2)}, u32[]{:S(2)}) %all-to-all-start) | async-done | bytes 573472 | tf_op jit(solution)/shard_map/all_to_all | solution.py:374
  45.7 3.5 %all-to-all-start.2 = ((bf16[8,32,896]{2,1,0:T(8,128)(2,1)}), bf16[8,32,896]{2,1,0:T(8,128)(2,1)S(1)}, u32[]{:S(2)}, u32[]{:S(2)}) async-start(bf16[8,32,896]{2,1,0:T(8,128)(2,1)} %shard_map.116), calls=%async_computation.2 | async-start | bytes 917504 | tf_op jit(solution)/shard_map/all_to_all | solution.py:374
  49.2 1.5 %dynamic_slice.3.x_ref = bf16[40,896]{1,0:T(8,128)(2,1)} dynamic-slice(bf16[160,3584]{1,0:T(8,128)(2,1)} %x_ref.3, s32[]{:T(128)S(6)} %select_n.18, s32[]{:T(128)S(6)} %select_n.20), dynamic_slice_sizes={40,896} | dynamic-slice | bytes 143364 | tf_op jit(solution)/shard_map/dynamic_slice | solution.py:448
  50.7 1.8 %shard_map.114 = bf16[8,40,896]{2,1,0:T(8,128)(2,1)} custom-call(bf16[8,40,896]{2,1,0:T(8,128)(2,1)S(1)} %all-to-all-done.got_ref, bf16[40,896]{1,0:T(8,128)(2,1)} %dynamic_slice.3.x_ref), custom_call_target="tpu_custom_call" | custom-call | tf_op jit(solution)/shard_map/pallas_call | solution.py:359
  52.6 13.0 %all-to-all-done.2 = bf16[8,32,896]{2,1,0:T(8,128)(2,1)S(1)} async-done(((bf16[8,32,896]{2,1,0:T(8,128)(2,1)}), bf16[8,32,896]{2,1,0:T(8,128)(2,1)S(1)}, u32[]{:S(2)}, u32[]{:S(2)}) %all-to-all-start.2) | async-done | bytes 458784 | tf_op jit(solution)/shard_map/all_to_all | solution.py:374
  65.6 3.5 %all-to-all-start.1 = ((bf16[8,40,896]{2,1,0:T(8,128)(2,1)}), bf16[8,40,896]{2,1,0:T(8,128)(2,1)S(1)}, u32[]{:S(2)}, u32[]{:S(2)}) async-start(bf16[8,40,896]{2,1,0:T(8,128)(2,1)} %shard_map.114), calls=%async_computation.1 | async-start | bytes 1146880 | tf_op jit(solution)/shard_map/all_to_all | solution.py:461
  69.2 0.1 reduce_sum.12
  69.2 18.9 %all-to-all-done.1.own_ref = bf16[8,40,896]{2,1,0:T(8,128)(2,1)S(1)} async-done(((bf16[8,40,896]{2,1,0:T(8,128)(2,1)}), bf16[8,40,896]{2,1,0:T(8,128)(2,1)S(1)}, u32[]{:S(2)}, u32[]{:S(2)}) %all-to-all-start.1) | async-done | bytes 573472 | tf_op jit(solution)/shard_map/all_to_all | solution.py:461
  88.1 2.4 %collective-permute-start.1 = (bf16[8,40,896]{2,1,0:T(8,128)(2,1)S(1)}, bf16[8,40,896]{2,1,0:T(8,128)(2,1)S(1)}, u32[]{:S(2)}, u32[]{:S(2)}) collective-permute-start(bf16[8,40,896]{2,1,0:T(8,128)(2,1)S(1)} %all-to-all-done.1.own_ref), channel_id=1, source_target_pairs={{0,1},{1,0},{2,3},{3,2},{4,5},{5,4},{6,7},{7,6},{8,9},{9,8},{10,11... | collective-permute-start | bytes 1720328 | tf_op jit(solution)/shard_map/ppermute | solution.py:353
  90.5 17.2 %all-gather = bf16[512,896]{1,0:T(8,128)(2,1)S(1)} all-gather(bf16[32,896]{1,0:T(8,128)(2,1)S(1)} %reduce_sum.12), channel_id=2, replica_groups=mesh['seq'=48,'y'=8,'core'=2] {'y','core'}, dimensions={0}, use_global_device_ids=true | all-gather | bytes 974848 | tf_op jit(solution)/shard_map/all_gather | solution.py:436
  107.7 1.3 collective-permute-start.3
  110.3 3.7 %collective-permute-done.3.earlier_ref = bf16[4,32,896]{2,1,0:T(8,128)(2,1)S(1)} collective-permute-done((bf16[4,32,896]{2,1,0:T(8,128)(2,1)S(1)}, bf16[4,32,896]{2,1,0:T(8,128)(2,1)S(1)}, u32[]{:S(2)}, u32[]{:S(2)}) %collective-permute-start.3) | collective-permute-done | bytes 229408 | tf_op jit(solution)/shard_map/ppermute | solution.py:349
  114.1 0.6 shard_map.117
  114.7 0.0 copy-start.1
  114.7 0.0 collective-permute-done.1.other_ref
  114.7 5.9 %shard_map.119 = (bf16[8,280,128]{2,1,0:T(8,128)(2,1)S(1)}, bf16[8,280,128]{2,1,0:T(8,128)(2,1)S(1)}) custom-call(s32[1]{0:T(128)} %bitcast.core_ref, s32[1]{0:T(128)S(6)} %copy.15.count_ref, bf16[8,40,896]{2,1,0:T(8,128)(2,1)S(1)} %all-to-all-done.1.own_ref, bf16[8,40,896]{2,1,0:T(8,128)(2,1)S(1)} %collective-permute-done.1.other_ref, ...), custom_call_target="tpu_custom_call" | custom-call | tf_op jit(solution)/shard_map/pallas_call | solution.py:359
  120.6 2.6 %collective-permute-start.4 = (bf16[8,280,128]{2,1,0:T(8,128)(2,1)S(1)}, bf16[8,280,128]{2,1,0:T(8,128)(2,1)S(1)}, u32[]{:S(2)}, u32[]{:S(2)}) collective-permute-start(bf16[8,280,128]{2,1,0:T(8,128)(2,1)S(1)} %get-tuple-element.27), channel_id=1, source_target_pairs={{0,1},{1,0},{2,3},{3,2},{4,5},{5,4},{6,7},{7,6},{8,9},{9,8},{10,11... | collective-permute-start | bytes 1720328 | tf_op jit(solution)/shard_map/ppermute | solution.py:353
  123.3 1.6 %collective-permute-done.4.other_ref = bf16[8,280,128]{2,1,0:T(8,128)(2,1)S(1)} collective-permute-done((bf16[8,280,128]{2,1,0:T(8,128)(2,1)S(1)}, bf16[8,280,128]{2,1,0:T(8,128)(2,1)S(1)}, u32[]{:S(2)}, u32[]{:S(2)}) %collective-permute-start.4) | collective-permute-done | bytes 573472 | tf_op jit(solution)/shard_map/ppermute | solution.py:353
  124.9 0.9 shard_map.120
  125.8 3.5 %all-to-all-start.3 = ((bf16[8,280,128]{2,1,0:T(8,128)(2,1)}), bf16[8,280,128]{2,1,0:T(8,128)(2,1)S(1)}, u32[]{:S(2)}, u32[]{:S(2)}) async-start(bf16[8,280,128]{2,1,0:T(8,128)(2,1)} %shard_map.120), calls=%async_computation.3 | async-start | bytes 1146880 | tf_op jit(solution)/shard_map/all_to_all | solution.py:374
  129.4 3.5 %shard_map.118 = (bf16[160,3584]{1,0:T(8,128)(2,1)}, f32[10,3584]{1,0:T(8,128)}, f32[10,3584]{1,0:T(8,128)}) custom-call(s32[1]{0:T(128)} %bitcast.core_ref, s32[1]{0:T(128)} %bitcast.1.first_ref, s32[1]{0:T(128)S(6)} %copy.15.count_ref, bf16[8,40,896]{2,1,0:T(8,128)(2,1)} %copy-done, bf16[8,40,896]{2,1,0:T(8,128)(2,1)} %copy-done.2, ...), custom_call_target="tpu_custom_call" | custom-call | tf_op jit(solution)/shard_map/pallas_call | solution.py:359
  132.8 15.5 %all-to-all-done.3.got_ref = bf16[8,280,128]{2,1,0:T(8,128)(2,1)S(1)} async-done(((bf16[8,280,128]{2,1,0:T(8,128)(2,1)}), bf16[8,280,128]{2,1,0:T(8,128)(2,1)S(1)}, u32[]{:S(2)}, u32[]{:S(2)}) %all-to-all-start.3) | async-done | bytes 573472 | tf_op jit(solution)/shard_map/all_to_all | solution.py:374
  148.3 1.9 %shard_map.121 = bf16[10,3584]{1,0:T(8,128)(2,1)} custom-call(bf16[8,280,128]{2,1,0:T(8,128)(2,1)S(1)} %all-to-all-done.3.got_ref, f32[10,3584]{1,0:T(8,128)} %get-tuple-element.28.x_ref, f32[10,3584]{1,0:T(8,128)} %get-tuple-element.29.dy_ref, f32[3584]{0:T(1024)} %gain_ref.3), custom_call_target="tpu_custom_call" | custom-call | tf_op jit(solution)/shard_map/pallas_call | solution.py:359
  (6 shorter events, 0.0 us)
Async XLA Ops:
  7.0 14.2 %collective-permute-start = (bf16[8,40,896]{2,1,0:T(8,128)(2,1)}, bf16[8,40,896]{2,1,0:T(8,128)(2,1)S(1)}, u32[]{:S(2)}, u32[]{:S(2)}) collective-permute-start(bf16[8,40,896]{2,1,0:T(8,128)(2,1)} %get-tuple-element.17), channel_id=1, source_target_pairs={{0,1},{1,0},{2,3},{3,2},{4,5},{5,4},{6,7},{7,6},{8,9},{9,8},{10,11... | collective-permute-start | bytes 1720328 | tf_op jit(solution)/shard_map/ppermute | solution.py:353
  23.1 22.5 %all-to-all-start = ((bf16[8,40,896]{2,1,0:T(8,128)(2,1)}), bf16[8,40,896]{2,1,0:T(8,128)(2,1)S(1)}, u32[]{:S(2)}, u32[]{:S(2)}) async-start(bf16[8,40,896]{2,1,0:T(8,128)(2,1)} %shard_map.113), calls=%async_computation | async-start | bytes 1146880 | tf_op jit(solution)/shard_map/all_to_all | solution.py:374
  28.7 3.7 %collective-permute-start.2 = (bf16[8,32,896]{2,1,0:T(8,128)(2,1)S(1)}, bf16[8,32,896]{2,1,0:T(8,128)(2,1)S(1)}, u32[]{:S(2)}, u32[]{:S(2)}) collective-permute-start(bf16[8,32,896]{2,1,0:T(8,128)(2,1)S(1)} %get-tuple-element.19), channel_id=1, source_target_pairs={{0,1},{1,0},{2,3},{3,2},{4,5},{5,4},{6,7},{7,6},{8,9},{9,8},{10,11... | collective-permute-start | bytes 1376264 | tf_op jit(solution)/shard_map/ppermute | solution.py:353
  45.7 19.9 %all-to-all-start.2 = ((bf16[8,32,896]{2,1,0:T(8,128)(2,1)}), bf16[8,32,896]{2,1,0:T(8,128)(2,1)S(1)}, u32[]{:S(2)}, u32[]{:S(2)}) async-start(bf16[8,32,896]{2,1,0:T(8,128)(2,1)} %shard_map.116), calls=%async_computation.2 | async-start | bytes 917504 | tf_op jit(solution)/shard_map/all_to_all | solution.py:374
  65.6 22.5 %all-to-all-start.1 = ((bf16[8,40,896]{2,1,0:T(8,128)(2,1)}), bf16[8,40,896]{2,1,0:T(8,128)(2,1)S(1)}, u32[]{:S(2)}, u32[]{:S(2)}) async-start(bf16[8,40,896]{2,1,0:T(8,128)(2,1)} %shard_map.114), calls=%async_computation.1 | async-start | bytes 1146880 | tf_op jit(solution)/shard_map/all_to_all | solution.py:461
  88.1 32.5 %copy-start = (bf16[8,40,896]{2,1,0:T(8,128)(2,1)}, bf16[8,40,896]{2,1,0:T(8,128)(2,1)S(1)}, u32[]{:S(2)}) copy-start(bf16[8,40,896]{2,1,0:T(8,128)(2,1)S(1)} %all-to-all-done.1.own_ref) | copy-start | bytes 1720324
  88.1 26.5 %collective-permute-start.1 = (bf16[8,40,896]{2,1,0:T(8,128)(2,1)S(1)}, bf16[8,40,896]{2,1,0:T(8,128)(2,1)S(1)}, u32[]{:S(2)}, u32[]{:S(2)}) collective-permute-start(bf16[8,40,896]{2,1,0:T(8,128)(2,1)S(1)} %all-to-all-done.1.own_ref), channel_id=1, source_target_pairs={{0,1},{1,0},{2,3},{3,2},{4,5},{5,4},{6,7},{7,6},{8,9},{9,8},{10,11... | collective-permute-start | bytes 1720328 | tf_op jit(solution)/shard_map/ppermute | solution.py:353
  107.7 6.4 %collective-permute-start.3 = (bf16[4,32,896]{2,1,0:T(8,128)(2,1)S(1)}, bf16[4,32,896]{2,1,0:T(8,128)(2,1)S(1)}, u32[]{:S(2)}, u32[]{:S(2)}) collective-permute-start(bf16[4,32,896]{2,1,0:T(8,128)(2,1)S(1)} %slice_bitcast_fusion), channel_id=1, source_target_pairs={{0,16},{16,32},{32,48},{48,64},{64,80},{80,96},{96,112},{112,128},... | collective-permute-start | bytes 688136 | tf_op jit(solution)/shard_map/ppermute | solution.py:349
  114.7 6.0 %copy-start.1 = (bf16[160,3584]{1,0:T(8,128)(2,1)}, bf16[160,3584]{1,0:T(8,128)(2,1)S(1)}, u32[]{:S(2)}) copy-start(bf16[160,3584]{1,0:T(8,128)(2,1)S(1)} %get-tuple-element.20.goal_ref) | copy-start | bytes 3440644
  114.7 5.9 %copy-start.2 = (bf16[8,40,896]{2,1,0:T(8,128)(2,1)}, bf16[8,40,896]{2,1,0:T(8,128)(2,1)S(1)}, u32[]{:S(2)}) copy-start(bf16[8,40,896]{2,1,0:T(8,128)(2,1)S(1)} %collective-permute-done.1.other_ref) | copy-start | bytes 1720324
  120.6 4.2 %collective-permute-start.4 = (bf16[8,280,128]{2,1,0:T(8,128)(2,1)S(1)}, bf16[8,280,128]{2,1,0:T(8,128)(2,1)S(1)}, u32[]{:S(2)}, u32[]{:S(2)}) collective-permute-start(bf16[8,280,128]{2,1,0:T(8,128)(2,1)S(1)} %get-tuple-element.27), channel_id=1, source_target_pairs={{0,1},{1,0},{2,3},{3,2},{4,5},{5,4},{6,7},{7,6},{8,9},{9,8},{10,11... | collective-permute-start | bytes 1720328 | tf_op jit(solution)/shard_map/ppermute | solution.py:353
  125.8 22.5 %all-to-all-start.3 = ((bf16[8,280,128]{2,1,0:T(8,128)(2,1)}), bf16[8,280,128]{2,1,0:T(8,128)(2,1)S(1)}, u32[]{:S(2)}, u32[]{:S(2)}) async-start(bf16[8,280,128]{2,1,0:T(8,128)(2,1)} %shard_map.120), calls=%async_computation.3 | async-start | bytes 1146880 | tf_op jit(solution)/shard_map/all_to_all | solution.py:374
